TPU v7x, 512 devices: a whole 4x8x8 slice. The times are simulated.
512 devices in a mesh: grp: 8 (over y), inner: 64 (over z, x, core).
Axes of the slice: x: 4, y: 8, z: 8, core: 2. Of those that a mesh axis runs over, the one named last changes fastest.
Arguments:
- row_left: bfloat16 [256, 1024, 128], P('inner', 'grp'), may hold values from -6 to 6
- row_right: bfloat16 [256, 1024, 128], P('inner', 'grp'), may hold values from -0.1875 to 0.1875
- col_left: bfloat16 [256, 1024, 2048], P('inner', None, 'grp'), may hold values from -6 to 6
- col_right: bfloat16 [256, 1024, 2048], P('inner', None, 'grp'), may hold values from -0.1875 to 0.1875
- sketch_cols: bfloat16 [1024, 2048], P(None, 'grp'), may hold values from -6 to 6
- target_left: bfloat16 [1024, 2048], P('inner', 'grp'), may hold values from -6 to 6
- target_right: bfloat16 [1024, 2048], P('inner', 'grp'), may hold values from -24 to 24
- live_counts: int32 [64], P('inner'), may hold values from 1 to 4, 160 in all
Outputs:
- new_basis: float32 [1024, 2048], P('inner', 'grp')
- new_coeffs: float32 [1024, 2048], P('inner', 'grp')
Inputs may be any that keep to these rules, and one draw needn't show every extreme that they name: Member m uses its first live_counts[m] slots; data in other slots is read by no output. Some member uses all 4 slots, and the counts sum to (5) times the number of members, halved.
All inputs are finite; a program needn't handle non-finite values. No bound on the sum of `live_counts` on one device may be relied on, other than what follows from the above.
Results may differ from a plain program's by a relative error of at most 0.0042.
Values may be sent and summed in bfloat16 or wider, within the bound.
No kernel may reach another device: no remote copies, remote signals or barrier semaphores. Data moves between devices by JAX's collectives and lax.ppermute only.
A program may use at most 64 MiB of HBM per device.

v0:
```python
import jax
import jax.numpy as jnp
from jax import lax
from jax.sharding import Mesh
from jax.sharding import PartitionSpec as P

INNER = ("inner_0", "inner_1", "inner_2")


exact_accumulation = lax.Precision.HIGHEST


def side_by_side(arrays, axis, dim, along):
    both = jnp.concatenate(arrays, axis=along)
    out, at, outs = (lax.all_gather(both, axis, axis=dim, tiled=True), 0, [])
    for a in arrays:
        outs.append(lax.slice_in_dim(out, at, at + a.shape[along], axis=along))
        at += a.shape[along]
    return tuple(outs)


def cut_along(x, dim, length):
    lengths = x.shape
    pieces = x.reshape(*lengths[:dim], length, lengths[dim] // length, *lengths[dim + 1 :])
    return jnp.moveaxis(pieces, dim, 0)


def sum_at_owner(x, axis, dim):
    length = lax.axis_size(axis)
    pieces = lax.all_to_all(cut_along(x, dim, length), axis, 0, 0, tiled=True)
    return jnp.sum(pieces, axis=0)


def sum_in_two_steps(x, axes, dim):
    far, near = axes
    own = sum_at_owner(cut_along(x, dim, lax.axis_size(far)), near, dim + 1)
    return jnp.sum(lax.all_to_all(own, far, 0, 0, tiled=True), axis=0)


def filled_up(lines, length):
    spare = -lines.shape[0] % length
    if not spare:
        return lines
    return jnp.concatenate([lines, jnp.zeros((spare, *lines.shape[1:]), lines.dtype)])


def sent_to_all(x, axis):
    length = lax.axis_size(axis)
    return lax.all_to_all(jnp.broadcast_to(x[None], (length, *x.shape)), axis, 0, 0, tiled=True)


def joined_along(pieces, dim):
    lengths = list(pieces.shape[1:])
    lengths[dim] *= pieces.shape[0]
    return jnp.moveaxis(pieces, 0, dim).reshape(lengths)


def gathered_by_axis(x, axes, dim):
    far, near = axes
    pieces = sent_to_all(sent_to_all(x, far), near)
    return joined_along(pieces.swapaxes(0, 1).reshape(-1, *x.shape), dim)


def nested_sum(x, axes):
    lines = x.reshape(-1, x.shape[-1])
    own = sum_in_two_steps(
        filled_up(lines, lax.axis_size(axes[0]) * lax.axis_size(axes[1])), axes, 0
    )
    whole = gathered_by_axis(own, axes, 0)
    return whole[: len(lines)].reshape(x.shape)


def orthonormal(sketched, gram):
    factor_low = jnp.linalg.cholesky(gram)
    blocks = jnp.transpose(sketched, (1, 2, 0))
    solved = jax.vmap(lambda tri, block: jax.scipy.linalg.solve_triangular(tri, block, lower=True))(
        factor_low, blocks
    )
    return jnp.transpose(solved, (2, 0, 1))


def shards(
    row_left, row_right, col_left, col_right, sketch_cols, target_left, target_right, live_counts
):
    slot_count, tile_rows, both_width = col_left.shape
    low_rank = row_left.shape[2]
    targets = both_width // low_rank
    local_row_block = target_left.shape[0]
    row_start = lax.axis_index(INNER) * local_row_block
    pivot_left, pivot_right = side_by_side((row_left, row_right), "grp", 1, 0)
    live_mask = (jnp.arange(slot_count) < live_counts[0]).astype(jnp.float32)
    sketch_partition = sketch_cols.reshape(tile_rows, targets, low_rank)
    own_sketch = lax.dynamic_slice_in_dim(sketch_partition, row_start, local_row_block, 0)
    left_split = target_left.reshape(local_row_block, targets, low_rank)
    right_split = target_right.reshape(local_row_block, targets, low_rank)
    core_part = jnp.einsum(
        "ntr,nts->trs", right_split, own_sketch, preferred_element_type=jnp.float32
    )
    target_core = nested_sum(core_part, (("inner_0", "inner_1"), "inner_2")).astype(jnp.bfloat16)
    target_rows = jnp.einsum(
        "ntr,trs->nts", left_split, target_core, preferred_element_type=jnp.float32
    ).reshape(local_row_block, both_width)
    paired_core_factors = jnp.einsum(
        "knr,knc->krc", pivot_right, col_right, preferred_element_type=jnp.float32
    ).reshape(slot_count, low_rank, targets, low_rank)
    column_partition = col_left.reshape(slot_count, tile_rows, targets, low_rank)
    random_test_matrix = jnp.einsum(
        "kntr,nts->ktrs", column_partition, sketch_partition, preferred_element_type=jnp.float32
    )
    mixed = (
        jnp.einsum(
            "hfge,hgen->hfgn", paired_core_factors, random_test_matrix, precision=exact_accumulation
        )
        * live_mask[:, None, None, None]
    )
    mixed = mixed.astype(jnp.bfloat16).reshape(slot_count, low_rank, both_width)
    partial_value = -jnp.einsum(
        "knr,krc->nc", pivot_left, mixed, preferred_element_type=jnp.float32
    )
    own_part = lax.dynamic_slice_in_dim(partial_value, row_start, local_row_block, 0) + target_rows
    partial_value = lax.dynamic_update_slice_in_dim(partial_value, own_part, row_start, 0)
    summed = nested_sum(partial_value, (("inner_0", "inner_1"), "inner_2")).reshape(
        tile_rows, targets, low_rank
    )
    gram = jnp.einsum("ntr,nts->trs", summed, summed, precision=exact_accumulation) / tile_rows
    basis_all = orthonormal(summed, gram).reshape(tile_rows, both_width)
    new_basis = lax.dynamic_slice_in_dim(basis_all, row_start, local_row_block, 0)
    basis_low = basis_all.astype(jnp.bfloat16)
    own_basis = lax.dynamic_slice_in_dim(basis_low, row_start, local_row_block, 0).reshape(
        local_row_block, targets, low_rank
    )
    back_part = jnp.einsum(
        "ntr,nts->trs", left_split, own_basis, preferred_element_type=jnp.float32
    )
    target_back = nested_sum(back_part, (("inner_0", "inner_1"), "inner_2")).astype(jnp.bfloat16)
    back = jnp.einsum(
        "knr,nc->krc", pivot_left, basis_low, preferred_element_type=jnp.float32
    ).reshape(slot_count, low_rank, targets, low_rank)
    collapsed_terms = (
        jnp.einsum("krtq,krts->kqts", paired_core_factors, back, precision=exact_accumulation)
        * live_mask[:, None, None, None]
    )
    collapsed_terms = collapsed_terms.astype(jnp.bfloat16)
    term = jnp.einsum(
        "kntq,kqts->nts", column_partition, collapsed_terms, preferred_element_type=jnp.float32
    )
    coupled = sum_in_two_steps(
        -term.reshape(local_row_block * lax.axis_size(INNER), both_width),
        (("inner_0", "inner_1"), "inner_2"),
        0,
    )
    own_terms = jnp.einsum(
        "ntr,trs->nts", right_split, target_back, preferred_element_type=jnp.float32
    ).reshape(local_row_block, both_width)
    new_coeffs = (coupled + own_terms) / tile_rows
    return (new_basis, new_coeffs)


def solution(mesh):
    finer = Mesh(
        mesh.devices.reshape(mesh.shape["grp"], 8, 4, 2), ("grp", "inner_0", "inner_1", "inner_2")
    )
    return jax.shard_map(
        shards,
        mesh=finer,
        in_specs=(
            P(INNER, "grp", None),
            P(INNER, "grp", None),
            P(INNER, None, "grp"),
            P(INNER, None, "grp"),
            P(None, "grp"),
            P(INNER, "grp"),
            P(INNER, "grp"),
            P(INNER),
        ),
        out_specs=(P(INNER, "grp"), P(INNER, "grp")),
        check_vma=False,
    )
```

profile of v0, /device:TPU:56, one launch (start us, length us, event | category | flops | bytes accessed | tf_op | source)
XLA Modules:
  0.0 269.5 jit_solution(3108124596856079740)
XLA Ops:
  11.8 3.8 %all_to_all.70 = f32[2,32,4,128]{3,2,1,0:T(4,128)S(1)} all-to-all(f32[2,32,4,128]{3,2,1,0:T(4,128)S(1)} %bitcast.172), channel_id=1, replica_groups=mesh['grp'=8,'inner_0'=8,'inner_1'=4,'inner_2'=2] {'inner_2'}, dimensions={0} | all-to-all | bytes 262144 | tf_op jit(solution)/shard_map/all_to_all | solution.py:30
  16.3 13.2 %all-to-all-start.1 = ((f32[32,4,128]{2,1,0:T(4,128)}), f32[32,4,128]{2,1,0:T(4,128)S(1)}, u32[]{:S(2)}, u32[]{:S(2)}) async-start(f32[32,4,128]{2,1,0:T(4,128)} %reduce_sum.72), calls=%async_computation.1 | async-start | bytes 131072 | tf_op jit(solution)/shard_map/all_to_all | solution.py:37
  30.6 8.9 %all-to-all-done.1 = f32[32,4,128]{2,1,0:T(4,128)S(1)} async-done(((f32[32,4,128]{2,1,0:T(4,128)}), f32[32,4,128]{2,1,0:T(4,128)S(1)}, u32[]{:S(2)}, u32[]{:S(2)}) %all-to-all-start.1) | async-done | bytes 65568 | tf_op jit(solution)/shard_map/all_to_all | solution.py:37
  40.1 3.8 %all-to-all-start.2 = ((bf16[32,4,128]{2,1,0:T(4,128)(2,1)}), bf16[32,4,128]{2,1,0:T(4,128)(2,1)S(1)}, u32[]{:S(2)}, u32[]{:S(2)}) async-start(bf16[32,4,128]{2,1,0:T(4,128)(2,1)} %broadcast_in_dim.14), calls=%async_computation.2 | async-start | bytes 65536 | tf_op jit(solution)/shard_map/all_to_all | solution.py:49
  43.9 9.8 %all-to-all-done.2 = bf16[32,4,128]{2,1,0:T(4,128)(2,1)S(1)} async-done(((bf16[32,4,128]{2,1,0:T(4,128)(2,1)}), bf16[32,4,128]{2,1,0:T(4,128)(2,1)S(1)}, u32[]{:S(2)}, u32[]{:S(2)}) %all-to-all-start.2) | async-done | bytes 32800 | tf_op jit(solution)/shard_map/all_to_all | solution.py:49
  53.7 3.8 %all_to_all.71 = bf16[2,32,4,128]{3,2,1,0:T(4,128)(2,1)S(1)} all-to-all(bf16[2,32,4,128]{3,2,1,0:T(4,128)(2,1)S(1)} %broadcast_in_dim.15), channel_id=1, replica_groups=mesh['grp'=8,'inner_0'=8,'inner_1'=4,'inner_2'=2] {'inner_2'}, dimensions={0} | all-to-all | bytes 131072 | tf_op jit(solution)/shard_map/all_to_all | solution.py:49
  57.7 6.6 %all-gather.2.cloned.1.call-done = bf16[8,1024,128]{1,2,0:T(8,128)(2,1)} async-done(((bf16[8,128,128]{1,2,0:T(8,128)(2,1)}), bf16[8,1024,128]{1,2,0:T(8,128)(2,1)}) %all-gather.2.cloned.1.call-update) | async-done | bytes 2097168 | tf_op jit(solution)/shard_map/all_gather | solution.py:15
  64.2 2.5 convolution_bitcast_fusion.1
  68.6 4.6 %all_to_all.72 = f32[2,32,16,256]{3,2,1,0:T(8,128)S(1)} all-to-all(f32[2,32,16,256]{3,2,1,0:T(8,128)S(1)} %bitcast.164), channel_id=1, replica_groups=mesh['grp'=8,'inner_0'=8,'inner_1'=4,'inner_2'=2] {'inner_2'}, dimensions={0} | all-to-all | bytes 2097152 | tf_op jit(solution)/shard_map/all_to_all | solution.py:30
  74.1 28.1 %all_to_all.73 = f32[32,16,256]{2,1,0:T(8,128)S(1)} all-to-all(f32[32,16,256]{2,1,0:T(8,128)} %reduce_sum.74), channel_id=1, replica_groups=mesh['grp'=8,'inner_0'=8,'inner_1'=4,'inner_2'=2] {'inner_0','inner_1'}, dimensions={0} | all-to-all | bytes 1048576 | tf_op jit(solution)/shard_map/all_to_all | solution.py:37
  103.1 4.6 %all-to-all-start.6 = ((f32[32,16,256]{2,1,0:T(8,128)}), f32[32,16,256]{2,1,0:T(8,128)S(1)}, u32[]{:S(2)}, u32[]{:S(2)}) async-start(f32[32,16,256]{2,1,0:T(8,128)} %broadcast_in_dim.16), calls=%async_computation.6 | async-start | bytes 1048576 | tf_op jit(solution)/shard_map/all_to_all | solution.py:49
  108.4 16.4 %all-to-all-done.6 = f32[32,16,256]{2,1,0:T(8,128)S(1)} async-done(((f32[32,16,256]{2,1,0:T(8,128)}), f32[32,16,256]{2,1,0:T(8,128)S(1)}, u32[]{:S(2)}, u32[]{:S(2)}) %all-to-all-start.6) | async-done | bytes 524320 | tf_op jit(solution)/shard_map/all_to_all | solution.py:49
  124.8 4.6 %all_to_all.74 = f32[2,32,16,256]{3,2,1,0:T(8,128)S(1)} all-to-all(f32[2,32,16,256]{3,2,1,0:T(8,128)S(1)} %broadcast_in_dim.17), channel_id=1, replica_groups=mesh['grp'=8,'inner_0'=8,'inner_1'=4,'inner_2'=2] {'inner_2'}, dimensions={0} | all-to-all | bytes 2097152 | tf_op jit(solution)/shard_map/all_to_all | solution.py:49
  133.7 23.5 %custom-call.8 = f32[2,128,128]{2,1,0:T(8,128)S(1)} custom-call(f32[2,128,128]{2,1,0:T(8,128)S(1)} %fusion.30), custom_call_target="Cholesky" | custom-call | tf_op jit(solution)/shard_map/jit(cholesky)/cholesky | solution.py:74
  158.1 19.7 %custom-call.9 = f32[2,1,128,128]{2,3,1,0:T(8,128)S(1)} custom-call(f32[2,1,128,128]{3,2,1,0:T(8,128)S(1)} %select_bitcast_fusion), custom_call_target="InvertDiagBlocksLowerTriangular" | custom-call | tf_op jit(solution)/shard_map/vmap(jit(_solve_triangular))/triangular_solve | solution.py:76
  187.3 4.5 %all_to_all.75 = f32[2,32,4,128]{3,2,1,0:T(4,128)} all-to-all(f32[2,32,4,128]{3,2,1,0:T(4,128)S(1)} %bitcast.171), channel_id=1, replica_groups=mesh['grp'=8,'inner_0'=8,'inner_1'=4,'inner_2'=2] {'inner_2'}, dimensions={0} | all-to-all | bytes 262144 | tf_op jit(solution)/shard_map/all_to_all | solution.py:30
  193.4 4.8 %all-to-all-start.11 = ((f32[32,4,128]{2,1,0:T(4,128)}), f32[32,4,128]{2,1,0:T(4,128)S(1)}, u32[]{:S(2)}, u32[]{:S(2)}) async-start(f32[32,4,128]{2,1,0:T(4,128)} %reduce_sum.78), calls=%async_computation.11 | async-start | bytes 131072 | tf_op jit(solution)/shard_map/all_to_all | solution.py:37
  202.2 3.0 %neg.16 = f32[32,2,16,256]{3,2,1,0:T(8,128)} reshape(f32[1024,2,128]{2,1,0:T(2,128)} %copy.146) | data formatting | bytes 2097152 | tf_op jit(solution)/shard_map/neg | solution.py:148
  207.9 4.4 %all-to-all-start.8 = ((f32[2,32,16,256]{3,2,1,0:T(8,128)}), f32[2,32,16,256]{3,2,1,0:T(8,128)}, u32[]{:S(2)}, u32[]{:S(2)}) async-start(f32[2,32,16,256]{3,2,1,0:T(8,128)} %copy.147), calls=%async_computation.8 | async-start | bytes 2097152 | tf_op jit(solution)/shard_map/all_to_all | solution.py:30
  215.1 9.3 %all-to-all-start.12 = ((bf16[32,4,128]{2,1,0:T(4,128)(2,1)}), bf16[32,4,128]{2,1,0:T(4,128)(2,1)S(1)}, u32[]{:S(2)}, u32[]{:S(2)}) async-start(bf16[32,4,128]{2,1,0:T(4,128)(2,1)} %broadcast_in_dim.18), calls=%async_computation.12 | async-start | bytes 65536 | tf_op jit(solution)/shard_map/all_to_all | solution.py:49
  226.6 7.6 %all-to-all-done.12 = bf16[32,4,128]{2,1,0:T(4,128)(2,1)S(1)} async-done(((bf16[32,4,128]{2,1,0:T(4,128)(2,1)}), bf16[32,4,128]{2,1,0:T(4,128)(2,1)S(1)}, u32[]{:S(2)}, u32[]{:S(2)}) %all-to-all-start.12) | async-done | bytes 32800 | tf_op jit(solution)/shard_map/all_to_all | solution.py:49
  234.3 3.8 %all_to_all.76 = bf16[2,32,4,128]{3,2,1,0:T(4,128)(2,1)S(1)} all-to-all(bf16[2,32,4,128]{3,2,1,0:T(4,128)(2,1)S(1)} %broadcast_in_dim.21), channel_id=1, replica_groups=mesh['grp'=8,'inner_0'=8,'inner_1'=4,'inner_2'=2] {'inner_2'}, dimensions={0} | all-to-all | bytes 131072 | tf_op jit(solution)/shard_map/all_to_all | solution.py:49
  238.1 4.6 %all-to-all-start.9 = ((f32[32,16,256]{2,1,0:T(8,128)}), f32[32,16,256]{2,1,0:T(8,128)}, u32[]{:S(2)}, u32[]{:S(2)}) async-start(f32[32,16,256]{2,1,0:T(8,128)} %reduce_sum.76), calls=%async_computation.9 | async-start | bytes 1048576 | tf_op jit(solution)/shard_map/all_to_all | solution.py:37
  243.5 17.5 %all-to-all-done.9 = f32[32,16,256]{2,1,0:T(8,128)} async-done(((f32[32,16,256]{2,1,0:T(8,128)}), f32[32,16,256]{2,1,0:T(8,128)}, u32[]{:S(2)}, u32[]{:S(2)}) %all-to-all-start.9) | async-done | bytes 524320 | tf_op jit(solution)/shard_map/all_to_all | solution.py:37
  (79 shorter events, 41.2 us)
Async XLA Ops:
  7.2 22.3 %copy-start = (bf16[4,1024,256]{2,1,0:T(8,128)(2,1)S(1)}, bf16[4,1024,256]{2,1,0:T(8,128)(2,1)}, u32[]{:S(2)}) copy-start(bf16[4,1024,256]{2,1,0:T(8,128)(2,1)} %param.10) | copy-start | bytes 6291460
  7.2 4.3 %copy-start.6 = (bf16[16,256]{1,0:T(8,128)(2,1)S(1)}, bf16[16,256]{1,0:T(8,128)(2,1)}, u32[]{:S(2)}) copy-start(bf16[16,256]{1,0:T(8,128)(2,1)} %param.14) | copy-start | bytes 24580
  7.2 57.0 %all-gather.2.cloned.1.call-start = ((), (), s32[]{:S(2)}) async-start(), calls=%async_computation.14 | async-start | bytes 2359296 | tf_op jit(solution)/shard_map/all_gather | solution.py:15
  15.6 41.9 %copy-start.4 = (bf16[16,256]{1,0:T(8,128)(2,1)S(1)}, bf16[16,256]{1,0:T(8,128)(2,1)}, u32[]{:S(2)}) copy-start(bf16[16,256]{1,0:T(8,128)(2,1)} %param.13) | copy-start | bytes 24580
  16.3 23.1 %all-to-all-start.1 = ((f32[32,4,128]{2,1,0:T(4,128)}), f32[32,4,128]{2,1,0:T(4,128)S(1)}, u32[]{:S(2)}, u32[]{:S(2)}) async-start(f32[32,4,128]{2,1,0:T(4,128)} %reduce_sum.72), calls=%async_computation.1 | async-start | bytes 131072 | tf_op jit(solution)/shard_map/all_to_all | solution.py:37
  40.1 13.6 %all-to-all-start.2 = ((bf16[32,4,128]{2,1,0:T(4,128)(2,1)}), bf16[32,4,128]{2,1,0:T(4,128)(2,1)S(1)}, u32[]{:S(2)}, u32[]{:S(2)}) async-start(bf16[32,4,128]{2,1,0:T(4,128)(2,1)} %broadcast_in_dim.14), calls=%async_computation.2 | async-start | bytes 65536 | tf_op jit(solution)/shard_map/all_to_all | solution.py:49
  43.9 22.9 %copy-start.8 = (f32[4]{0:T(128)}, f32[4]{0:T(128)S(1)}, u32[]{:S(2)}) copy-start(f32[4]{0:T(128)S(1)} %compare_convert_fusion) | copy-start | bytes 52
  64.2 3.8 %copy-start.3 = (bf16[8,1024,128]{1,2,0:T(8,128)(2,1)S(1)}, bf16[8,1024,128]{1,2,0:T(8,128)(2,1)}, u32[]{:S(2)}) copy-start(bf16[8,1024,128]{1,2,0:T(8,128)(2,1)} %all-gather.2.cloned.1.call-done) | copy-start | bytes 6291460
  66.8 1.8 copy-start.1
  103.1 21.6 %all-to-all-start.6 = ((f32[32,16,256]{2,1,0:T(8,128)}), f32[32,16,256]{2,1,0:T(8,128)S(1)}, u32[]{:S(2)}, u32[]{:S(2)}) async-start(f32[32,16,256]{2,1,0:T(8,128)} %broadcast_in_dim.16), calls=%async_computation.6 | async-start | bytes 1048576 | tf_op jit(solution)/shard_map/all_to_all | solution.py:49
  181.4 0.9 copy-start.5
  182.4 4.2 %copy-start.9 = (f32[4]{0:T(128)S(1)}, f32[4]{0:T(128)}, u32[]{:S(2)}) copy-start(f32[4]{0:T(128)} %copy-done.8) | copy-start | bytes 52
  184.7 1.9 copy-start.2
  193.4 14.5 %all-to-all-start.11 = ((f32[32,4,128]{2,1,0:T(4,128)}), f32[32,4,128]{2,1,0:T(4,128)S(1)}, u32[]{:S(2)}, u32[]{:S(2)}) async-start(f32[32,4,128]{2,1,0:T(4,128)} %reduce_sum.78), calls=%async_computation.11 | async-start | bytes 131072 | tf_op jit(solution)/shard_map/all_to_all | solution.py:37
  207.9 6.6 %all-to-all-start.8 = ((f32[2,32,16,256]{3,2,1,0:T(8,128)}), f32[2,32,16,256]{3,2,1,0:T(8,128)}, u32[]{:S(2)}, u32[]{:S(2)}) async-start(f32[2,32,16,256]{3,2,1,0:T(8,128)} %copy.147), calls=%async_computation.8 | async-start | bytes 2097152 | tf_op jit(solution)/shard_map/all_to_all | solution.py:30
  212.3 31.0 %copy-start.7 = (bf16[16,256]{1,0:T(8,128)(2,1)S(1)}, bf16[16,256]{1,0:T(8,128)(2,1)}, u32[]{:S(2)}) copy-start(bf16[16,256]{1,0:T(8,128)(2,1)} %param.14) | copy-start | bytes 24580
  215.1 19.1 %all-to-all-start.12 = ((bf16[32,4,128]{2,1,0:T(4,128)(2,1)}), bf16[32,4,128]{2,1,0:T(4,128)(2,1)S(1)}, u32[]{:S(2)}, u32[]{:S(2)}) async-start(bf16[32,4,128]{2,1,0:T(4,128)(2,1)} %broadcast_in_dim.18), calls=%async_computation.12 | async-start | bytes 65536 | tf_op jit(solution)/shard_map/all_to_all | solution.py:49
  238.1 22.9 %all-to-all-start.9 = ((f32[32,16,256]{2,1,0:T(8,128)}), f32[32,16,256]{2,1,0:T(8,128)}, u32[]{:S(2)}, u32[]{:S(2)}) async-start(f32[32,16,256]{2,1,0:T(8,128)} %reduce_sum.76), calls=%async_computation.9 | async-start | bytes 1048576 | tf_op jit(solution)/shard_map/all_to_all | solution.py:37
Sparse Core Ops, SparseCore 0:
  10.3 53.8 all-gather.1
where the time goes:
time: 272 us; the launch traced here: 270 us
  waiting for transfers between devices  69.2 us (25%)
  other arithmetic  53.6 us (20%)
  blocking collectives  53.2 us (20%)
  starting transfers between devices  44.7 us (16%)
  local copies, waits for them, and re-layouts  20.9 us (8%)
  between operations  15.1 us (6%)
  matrix products  12.9 us (5%)
    all_to_all x3, waiting for transfers between devices, sent_to_all(): lax.all_to_all(jnp.broadcast_to(x[None], (length, *x.shape)), axis, 0, 0,...  33.8 us
    all_to_all x1, blocking collectives, sum_in_two_steps(): return jnp.sum(lax.all_to_all(own, far, 0, 0, tiled=True), axis=0)  28.1 us
    all_to_all x3, waiting for transfers between devices, sum_in_two_steps(): return jnp.sum(lax.all_to_all(own, far, 0, 0, tiled=True), axis=0)  26.6 us
    another operation x4, other arithmetic, orthonormal(): factor_low = jnp.linalg.cholesky(gram)  25 us
    all_to_all x3, starting transfers between devices, sum_in_two_steps(): return jnp.sum(lax.all_to_all(own, far, 0, 0, tiled=True), axis=0)  22.6 us
    another operation x3, other arithmetic, orthonormal(): jax.scipy.linalg.solve_triangular(tri, block, lower=True)  19.8 us
    all_to_all x3, starting transfers between devices, sent_to_all(): lax.all_to_all(jnp.broadcast_to(x[None], (length, *x.shape)), axis, 0, 0,...  17.7 us
    all_to_all x3, blocking collectives, sum_at_owner(): pieces = lax.all_to_all(cut_along(x, dim, length), axis, 0, 0, tiled=True)  12.9 us
  transfers between devices with their start and end apart: 8, of which 8 were waited for; matrix products, arithmetic and copies ran while one was open for 6% of the time, Pallas kernels for 0%

commit v1 on v0

v1 whole, which is shorter than its diff:
```python
import jax
import jax.numpy as jnp
from jax import lax
from jax.experimental import pallas as pl
from jax.experimental.pallas import tpu as pltpu
from jax.sharding import Mesh
from jax.sharding import PartitionSpec as P

INNER = ("inner_0", "inner_1", "inner_2")
LOW = jnp.bfloat16
FULL = jnp.float32


def dot(a, b, ca, cb):
    return lax.dot_general(a, b, (((ca,), (cb,)), ((), ())), preferred_element_type=FULL)


def halves(x):
    high = x.astype(LOW)
    return high, (x - high.astype(FULL)).astype(LOW)


def fine_dot(a, b, ca, cb):
    ah, al = halves(a)
    bh, bl = halves(b)
    return dot(ah, bh, ca, cb) + (dot(ah, bl, ca, cb) + dot(al, bh, ca, cb))


def inverse_factors(grams):
    n, count, block = grams[0].shape[0], len(grams), 64
    groups = block // 8
    eye = (
        lax.broadcasted_iota(jnp.int32, (n, n), 0) == lax.broadcasted_iota(jnp.int32, (n, n), 1)
    ).astype(FULL)
    sub = lax.broadcasted_iota(jnp.int32, (8, n), 0)
    left, right, done = list(grams), [eye] * count, [[] for _ in range(count)]
    for start in range(0, n, block):
        a = [[left[t][8 * g : 8 * g + 8] for g in range(groups)] for t in range(count)]
        b = [[right[t][8 * g : 8 * g + 8] for g in range(groups)] for t in range(count)]
        scale = [[jnp.ones((8, n), FULL) for g in range(groups)] for t in range(count)]
        for i in range(block):
            j, first, at = start + i, i // 8, i % 8
            for t in range(count):
                row_a = jnp.broadcast_to(a[t][first][at : at + 1, :], (8, n))
                row_b = jnp.broadcast_to(b[t][first][at : at + 1, :], (8, n))
                cols = [
                    jnp.broadcast_to(a[t][g][:, j : j + 1], (8, n)) for g in range(first, groups)
                ]
                root = lax.rsqrt(jnp.broadcast_to(cols[0][at : at + 1, :], (8, n)))
                row_a, row_b = row_a * (root * root), row_b * (root * root)
                scale[t][first] = jnp.where(sub == at, root, scale[t][first])
                for g in range(first, groups):
                    c = cols[g - first]
                    if g == first:
                        c = jnp.where(sub > at, c, 0.0)
                    a[t][g] = a[t][g] - c * row_a
                    b[t][g] = b[t][g] - c * row_b
        for t in range(count):
            rows_b = jnp.concatenate([b[t][g] * scale[t][g] for g in range(groups)], 0)
            done[t].append(rows_b)
            if start + block < n:
                rows_a = jnp.concatenate([a[t][g] * scale[t][g] for g in range(groups)], 0)
                ah, al = halves(rows_a)
                bh, bl = halves(rows_b)
                factor = jnp.concatenate([ah, ah, al], 0)
                cut_a = dot(factor, jnp.concatenate([ah, al, ah], 0), 0, 0)
                cut_b = dot(factor, jnp.concatenate([bh, bl, bh], 0), 0, 0)
                left[t] = left[t][block:] - cut_a[start + block :]
                right[t] = right[t][block:] - cut_b[start + block :]
    return [jnp.concatenate(rows, 0) for rows in done]


def probe_body(left_ref, sketch_ref, out_ref):
    for k in range(left_ref.shape[0]):
        for t in range(out_ref.shape[1]):
            cols = slice(128 * t, 128 * t + 128)
            out_ref[k, t] = dot(left_ref[k, :, cols], sketch_ref[:, cols], 0, 0)


def forward_body(
    place_ref, own, f1, b1, f2, b2, f3, b3, f4, b4,
    right_ref, probe_ref, tall_ref, tright_ref, sketch_ref,
    part_ref, pair_ref, pivot_ref, factor,
):
    group, live, groups = place_ref[0], place_ref[1], place_ref[2]
    slots = right_ref.shape[0]
    n = own.shape[1]

    def put(ref, first, distance, with_right, with_left):
        at = pl.multiple_of(lax.rem(group + distance, groups) * n, n)
        for k in range(slots):
            if with_right:
                factor[pl.ds(at, n), 128 * k : 128 * k + 128] = ref[k]
            if with_left:
                pivot_ref[pl.ds(at, n), 128 * k : 128 * k + 128] = ref[k + first]

    put(own, slots, 0, True, True)
    for s, (f, b) in enumerate(((f1, b1), (f2, b2), (f3, b3))):
        put(f, slots, groups - 1 - s, True, True)
        put(b, slots, 1 + s, True, True)
    put(f4, 0, 4, True, False)
    put(b4, 0, 4, False, True)
    mixed = []
    for k in range(slots):
        pair = dot(factor[:, 128 * k : 128 * k + 128], right_ref[k], 0, 0)
        pair_ref[k] = pair
        row = []
        for t in range(2):
            cols = slice(128 * t, 128 * t + 128)
            value = fine_dot(pair[:, cols], probe_ref[k, t], 1, 0)
            row.append(jnp.where(k < live, value, 0.0).astype(LOW))
        mixed.append(jnp.concatenate(row, 1))
    update = dot(pivot_ref[...], jnp.concatenate(mixed, 0), 1, 0)
    for t in range(2):
        cols = slice(128 * t, 128 * t + 128)
        core = dot(tright_ref[:, cols], sketch_ref[:, cols], 0, 0).astype(LOW)
        target = dot(tall_ref[:, cols], core, 1, 0)
        part_ref[:, cols] = (target - update[:, cols]).astype(LOW)


def backward_body(
    place_ref, all_ref, own_ref, pivot_ref, pair_ref, left_ref, tall_ref, tright_ref,
    basis_ref, term_ref, direct_ref,
):
    live = place_ref[1]
    slots, rows = left_ref.shape[0], all_ref.shape[0]
    turned, grams = [], []
    for t in range(2):
        s = all_ref[:, 128 * t : 128 * t + 128]
        grams.append(dot(s, s, 0, 0) / rows)
    inverse = inverse_factors(grams)
    for t in range(2):
        cols = slice(128 * t, 128 * t + 128)
        wh, wl = halves(inverse[t])
        s = all_ref[:, cols]
        basis = dot(wh, s, 1, 1) + dot(wl, s, 1, 1)
        turned = basis.astype(LOW)
        basis_ref[:, cols] = fine_dot(own_ref[:, cols], inverse[t], 1, 1)
        back = dot(turned, pivot_ref[...], 1, 0)
        total = None
        for k in range(slots):
            folded = fine_dot(back[:, 128 * k : 128 * k + 128], pair_ref[k, :, cols], 1, 0)
            folded = jnp.where(k < live, folded, 0.0).astype(LOW)
            term = dot(left_ref[k, :, cols], folded, 1, 1)
            total = term if total is None else total + term
        term_ref[:, cols] = (-total).astype(LOW)
        target_back = dot(turned, tall_ref[:, cols], 1, 0).astype(LOW)
        direct_ref[:, cols] = dot(tright_ref[:, cols], target_back, 1, 1)


SMEM = pl.BlockSpec(memory_space=pltpu.SMEM)
WHOLE = pl.BlockSpec()


def shift(x, axis, by):
    n = lax.axis_size(axis)
    return lax.ppermute(x, axis, [(i, (i + by) % n) for i in range(n)])


def to_all(x):
    n = lax.axis_size(INNER)
    return lax.all_to_all(jnp.broadcast_to(x[None], (n, *x.shape)), INNER, 0, 0, tiled=True)


def shards(
    row_left, row_right, col_left, col_right, sketch_cols, target_left, target_right, live_counts
):
    slots, rows, width = col_left.shape
    block = target_left.shape[0]
    n = lax.axis_size(INNER)
    place = jnp.stack(
        [lax.axis_index("grp"), live_counts[0], jnp.int32(lax.axis_size("grp"))]
    ).astype(jnp.int32)
    own = jnp.concatenate([row_right, row_left], 0)
    ups, downs, up, down = [], [], own, own
    for _ in range(3):
        up, down = shift(up, "grp", 1), shift(down, "grp", -1)
        ups.append(up)
        downs.append(down)
    ups.append(shift(up[:slots], "grp", 1))
    downs.append(shift(down[slots:], "grp", -1))
    all_left = to_all(target_left).reshape(rows, width)
    probe = pl.pallas_call(
        probe_body,
        out_shape=jax.ShapeDtypeStruct((slots, 2, 128, 128), FULL),
        name="probe",
    )(col_left, sketch_cols)
    own_sketch = lax.dynamic_slice_in_dim(
        sketch_cols, lax.axis_index(INNER) * block, block, 0
    )
    chunks = [own]
    for u, d in zip(ups, downs):
        chunks += [u, d]
    part, pair, pivot = pl.pallas_call(
        forward_body,
        in_specs=[SMEM] + [WHOLE] * 14,
        out_shape=(
            jax.ShapeDtypeStruct((rows, width), LOW),
            jax.ShapeDtypeStruct((slots, 128, width), FULL),
            jax.ShapeDtypeStruct((rows, slots * 128), LOW),
        ),
        scratch_shapes=[pltpu.VMEM((rows, slots * 128), LOW)],
        name="forward",
    )(place, *chunks, col_right, probe, all_left, target_right, own_sketch)
    pieces = lax.all_to_all(part.reshape(n, block, width), INNER, 0, 0, tiled=True)
    own_sum = jnp.sum(pieces.astype(FULL), 0)
    whole = to_all(own_sum.astype(LOW)).reshape(rows, width)
    basis, term, direct = pl.pallas_call(
        backward_body,
        in_specs=[SMEM] + [WHOLE] * 7,
        out_shape=(
            jax.ShapeDtypeStruct((block, width), FULL),
            jax.ShapeDtypeStruct((rows, width), LOW),
            jax.ShapeDtypeStruct((block, width), FULL),
        ),
        name="backward",
    )(place, whole, own_sum, pivot, pair, col_left, all_left, target_right)
    pieces = lax.all_to_all(term.reshape(n, block, width), INNER, 0, 0, tiled=True)
    coeffs = (jnp.sum(pieces.astype(FULL), 0) + direct) / rows
    return basis, coeffs


def solution(mesh):
    finer = Mesh(
        mesh.devices.reshape(mesh.shape["grp"], 8, 4, 2), ("grp", "inner_0", "inner_1", "inner_2")
    )
    return jax.shard_map(
        shards,
        mesh=finer,
        in_specs=(
            P(INNER, "grp", None),
            P(INNER, "grp", None),
            P(INNER, None, "grp"),
            P(INNER, None, "grp"),
            P(None, "grp"),
            P(INNER, "grp"),
            P(INNER, "grp"),
            P(INNER),
        ),
        out_specs=(P(INNER, "grp"), P(INNER, "grp")),
        check_vma=False,
    )
```

time: 272 us -> 171 us (0.63)
  waiting for transfers between devices: 69.2 us -> 9.66 us
  other arithmetic: 53.6 us -> 2.13 us
  Pallas kernels: 0 us -> 32.1 us
  blocking collectives: 53.2 us -> 74.8 us
  local copies, waits for them, and re-layouts: 20.9 us -> 5.56 us
  between operations: 15.1 us -> 1.54 us
  matrix products: 12.9 us -> 0 us
    all_to_all x7 -> x1, waiting for transfers between devices: 62.6 us -> 0.01 us  [to_all(): lax.all_to_all(jnp.broadcast_to(x[None], (n, *x.shape)), INNER, 0, 0, til...]
    another operation x7 -> x1, other arithmetic: 44.7 us -> 0.6 us  [shards(): jnp.stack([lax.axis_index('grp'), live_counts[0], jnp.int32(lax.axis_size...]
    pallas_call x0 -> x3, Pallas kernels: none -> 32.1 us  [the longest x1 23.3 us: shards(): pl.pallas_call(backward_body, in_specs=[SMEM] + [WHOLE] * 7, out_shape=(j...]
    all_to_all x7 -> x1, starting transfers between devices: 44.6 us -> 13.8 us  [to_all(): lax.all_to_all(jnp.broadcast_to(x[None], (n, *x.shape)), INNER, 0, 0, til...]
    ppermute x0 -> x8, starting transfers between devices: none -> 28.2 us  [shift(): return lax.ppermute(x, axis, [(i, (i + by) % n) for i in range(n)])]
    all_to_all x7 -> x3, blocking collectives: 53.2 us -> 74.8 us  [the longest x1 28.1 us: shards(): lax.all_to_all(part.reshape(n, block, width), INNER, 0, 0, tiled=True)]
    dot_general x12 -> x0, matrix products: 10.9 us -> none  [the longest x1 2.5 us: shards(): jnp.einsum('knr,knc->krc', pivot_right, col_right, preferred_element_type...]
    ppermute x0 -> x8, waiting for transfers between devices: none -> 9.65 us  [shift(): return lax.ppermute(x, axis, [(i, (i + by) % n) for i in range(n)])]
  transfers between devices with their start and end apart: 8 -> 9, of which waited for: 8 -> 3; matrix products, arithmetic and copies ran while one was open for 6% -> 2% of each run, Pallas kernels for 0% -> 2%
where the time goes in v1:
time: 171 us; the launch traced here: 168 us
  blocking collectives  74.8 us (44%)
  starting transfers between devices  42 us (25%)
  Pallas kernels  32.1 us (19%)
  waiting for transfers between devices  9.66 us (6%)
  local copies, waits for them, and re-layouts  5.56 us (3%)
  other arithmetic  2.13 us (1%)
    ppermute x8, starting transfers between devices, shift(): return lax.ppermute(x, axis, [(i, (i + by) % n) for i in range(n)])  28.2 us
    all_to_all x1, blocking collectives, shards(): lax.all_to_all(part.reshape(n, block, width), INNER, 0, 0, tiled=True)  28.1 us
    all_to_all x1, blocking collectives, shards(): lax.all_to_all(term.reshape(n, block, width), INNER, 0, 0, tiled=True)  23.4 us
    all_to_all x1, blocking collectives, to_all(): lax.all_to_all(jnp.broadcast_to(x[None], (n, *x.shape)), INNER, 0, 0, til...  23.3 us
    pallas_call x1, Pallas kernels, shards(): pl.pallas_call(backward_body, in_specs=[SMEM] + [WHOLE] * 7, out_shape=(j...  23.3 us
    all_to_all x1, starting transfers between devices, to_all(): lax.all_to_all(jnp.broadcast_to(x[None], (n, *x.shape)), INNER, 0, 0, til...  13.8 us
    ppermute x8, waiting for transfers between devices, shift(): return lax.ppermute(x, axis, [(i, (i + by) % n) for i in range(n)])  9.65 us
    pallas_call x1, Pallas kernels, shards(): pl.pallas_call(forward_body, in_specs=[SMEM] + [WHOLE] * 14, out_shape=(j...  5.58 us
  transfers between devices with their start and end apart: 9, of which 3 were waited for; matrix products, arithmetic and copies ran while one was open for 2% of the time, Pallas kernels for 2%

profile of v1, /device:TPU:56, one launch (start us, length us, event | category | flops | bytes accessed | tf_op | source)
XLA Modules:
  0.0 167.7 jit_solution(17034375285055953640)
XLA Ops:
  0.6 1.5 broadcast_in_dim.4
  2.2 13.8 %all-to-all-start = ((bf16[64,16,256]{2,1,0:T(8,128)(2,1)}), bf16[64,16,256]{2,1,0:T(8,128)(2,1)S(1)}, u32[]{:S(2)}, u32[]{:S(2)}) async-start(bf16[64,16,256]{2,1,0:T(8,128)(2,1)} %broadcast_in_dim.4), calls=%async_computation | async-start | bytes 1048576 | tf_op jit(solution)/shard_map/all_to_all | solution.py:162
  15.9 0.9 constant_dynamic-update-slice_fusion.1
  16.9 0.9 constant_dynamic-update-slice_fusion.own
  17.8 3.3 %collective-permute-start.1 = (bf16[8,128,128]{2,1,0:T(8,128)(2,1)S(1)}, bf16[8,128,128]{2,1,0:T(8,128)(2,1)S(1)}, u32[]{:S(2)}, u32[]{:S(2)}) collective-permute-start(bf16[8,128,128]{2,1,0:T(8,128)(2,1)S(1)} %constant_dynamic-update-slice_fusion.own), channel_id=1, source_target_pairs={{0,448},{64,0},{128,64},{192,128},{256,192},{320,256},{384,320},{4... | collective-permute-start | bytes 786440 | tf_op jit(solution)/shard_map/ppermute | solution.py:157
  21.1 3.8 %collective-permute-start = (bf16[8,128,128]{2,1,0:T(8,128)(2,1)S(1)}, bf16[8,128,128]{2,1,0:T(8,128)(2,1)S(1)}, u32[]{:S(2)}, u32[]{:S(2)}) collective-permute-start(bf16[8,128,128]{2,1,0:T(8,128)(2,1)S(1)} %constant_dynamic-update-slice_fusion.own), channel_id=1, source_target_pairs={{0,64},{64,128},{128,192},{192,256},{256,320},{320,384},{384,448},... | collective-permute-start | bytes 786440 | tf_op jit(solution)/shard_map/ppermute | solution.py:157
  24.9 4.3 %collective-permute-done.1.b1 = bf16[8,128,128]{2,1,0:T(8,128)(2,1)S(1)} collective-permute-done((bf16[8,128,128]{2,1,0:T(8,128)(2,1)S(1)}, bf16[8,128,128]{2,1,0:T(8,128)(2,1)S(1)}, u32[]{:S(2)}, u32[]{:S(2)}) %collective-permute-start.1) | collective-permute-done | bytes 262176 | tf_op jit(solution)/shard_map/ppermute | solution.py:157
  29.2 2.0 %collective-permute-start.3 = (bf16[8,128,128]{2,1,0:T(8,128)(2,1)S(1)}, bf16[8,128,128]{2,1,0:T(8,128)(2,1)S(1)}, u32[]{:S(2)}, u32[]{:S(2)}) collective-permute-start(bf16[8,128,128]{2,1,0:T(8,128)(2,1)S(1)} %collective-permute-done.1.b1), channel_id=1, source_target_pairs={{0,448},{64,0},{128,64},{192,128},{256,192},{320,256},{384,320},{4... | collective-permute-start | bytes 786440 | tf_op jit(solution)/shard_map/ppermute | solution.py:157
  31.2 5.0 %collective-permute-start.2 = (bf16[8,128,128]{2,1,0:T(8,128)(2,1)S(1)}, bf16[8,128,128]{2,1,0:T(8,128)(2,1)S(1)}, u32[]{:S(2)}, u32[]{:S(2)}) collective-permute-start(bf16[8,128,128]{2,1,0:T(8,128)(2,1)S(1)} %collective-permute-done.f1), channel_id=1, source_target_pairs={{0,64},{64,128},{128,192},{192,256},{256,320},{320,384},{384,448},... | collective-permute-start | bytes 786440 | tf_op jit(solution)/shard_map/ppermute | solution.py:157
  36.3 3.4 %collective-permute-done.3.b2 = bf16[8,128,128]{2,1,0:T(8,128)(2,1)S(1)} collective-permute-done((bf16[8,128,128]{2,1,0:T(8,128)(2,1)S(1)}, bf16[8,128,128]{2,1,0:T(8,128)(2,1)S(1)}, u32[]{:S(2)}, u32[]{:S(2)}) %collective-permute-start.3) | collective-permute-done | bytes 262176 | tf_op jit(solution)/shard_map/ppermute | solution.py:157
  39.7 1.9 %collective-permute-start.5 = (bf16[8,128,128]{2,1,0:T(8,128)(2,1)S(1)}, bf16[8,128,128]{2,1,0:T(8,128)(2,1)S(1)}, u32[]{:S(2)}, u32[]{:S(2)}) collective-permute-start(bf16[8,128,128]{2,1,0:T(8,128)(2,1)S(1)} %collective-permute-done.3.b2), channel_id=1, source_target_pairs={{0,448},{64,0},{128,64},{192,128},{256,192},{320,256},{384,320},{4... | collective-permute-start | bytes 786440 | tf_op jit(solution)/shard_map/ppermute | solution.py:157
  41.6 5.1 %collective-permute-start.4 = (bf16[8,128,128]{2,1,0:T(8,128)(2,1)S(1)}, bf16[8,128,128]{2,1,0:T(8,128)(2,1)S(1)}, u32[]{:S(2)}, u32[]{:S(2)}) collective-permute-start(bf16[8,128,128]{2,1,0:T(8,128)(2,1)S(1)} %collective-permute-done.2.f2), channel_id=1, source_target_pairs={{0,64},{64,128},{128,192},{192,256},{256,320},{320,384},{384,448},... | collective-permute-start | bytes 786440 | tf_op jit(solution)/shard_map/ppermute | solution.py:157
  47.4 1.9 %collective-permute-done.5.b3 = bf16[8,128,128]{2,1,0:T(8,128)(2,1)S(1)} collective-permute-done((bf16[8,128,128]{2,1,0:T(8,128)(2,1)S(1)}, bf16[8,128,128]{2,1,0:T(8,128)(2,1)S(1)}, u32[]{:S(2)}, u32[]{:S(2)}) %collective-permute-start.5) | collective-permute-done | bytes 262176 | tf_op jit(solution)/shard_map/ppermute | solution.py:157
  49.3 1.9 %collective-permute-start.7 = (bf16[4,128,128]{2,1,0:T(8,128)(2,1)S(1)}, bf16[4,128,128]{2,1,0:T(8,128)(2,1)S(1)}, u32[]{:S(2)}, u32[]{:S(2)}) collective-permute-start(bf16[4,128,128]{2,1,0:T(8,128)(2,1)S(1)} %slice.9), channel_id=1, source_target_pairs={{0,448},{64,0},{128,64},{192,128},{256,192},{320,256},{384,320},{4... | collective-permute-start | bytes 393224 | tf_op jit(solution)/shard_map/ppermute | solution.py:157
  51.3 5.1 %collective-permute-start.6 = (bf16[4,128,128]{2,1,0:T(8,128)(2,1)S(1)}, bf16[4,128,128]{2,1,0:T(8,128)(2,1)S(1)}, u32[]{:S(2)}, u32[]{:S(2)}) collective-permute-start(bf16[4,128,128]{2,1,0:T(8,128)(2,1)S(1)} %slice.8), channel_id=1, source_target_pairs={{0,64},{64,128},{128,192},{192,256},{256,320},{320,384},{384,448},... | collective-permute-start | bytes 393224 | tf_op jit(solution)/shard_map/ppermute | solution.py:157
  56.5 0.6 pad_add_fusion.place_ref
  57.0 3.3 %probe.1.probe_ref = f32[4,2,128,128]{3,2,1,0:T(8,128)} custom-call(bf16[4,1024,256]{2,1,0:T(8,128)(2,1)} %left_ref.3, bf16[1024,256]{1,0:T(8,128)(2,1)} %sketch_ref.1), custom_call_target="tpu_custom_call" | custom-call | tf_op jit(solution)/shard_map/probe/pallas_call | solution.py:183
  60.3 1.3 constant_dynamic-slice_fusion.sketch_ref
  62.5 5.6 %forward.1 = (bf16[1024,256]{1,0:T(8,128)(2,1)}, f32[4,128,256]{2,1,0:T(8,128)}, bf16[1024,512]{1,0:T(8,128)(2,1)}) custom-call(s32[3]{0:T(128)} %pad_add_fusion.place_ref, bf16[8,128,128]{2,1,0:T(8,128)(2,1)} %copy-done.3, bf16[8,128,128]{2,1,0:T(8,128)(2,1)} %copy-done.5, bf16[8,128,128]{2,1,0:T(8,128)(2,1)} %copy-done.4, bf16[8,128,128]{2,1,0:T(8,128)(2,1)} %copy-done.7, ...), custom_call_target="tpu_custom_call" | custom-call | tf_op jit(solution)/shard_map/forward/pallas_call | solution.py:194
  68.1 28.1 %all_to_all.20 = bf16[64,16,256]{2,1,0:T(8,128)(2,1)S(1)} all-to-all(bf16[64,16,256]{2,1,0:T(8,128)(2,1)} %bitcast.8), channel_id=1, replica_groups=mesh['grp'=8,'inner_0'=8,'inner_1'=4,'inner_2'=2] {'inner_0','inner_1','..., dimensions={0} | all-to-all | bytes 1048576 | tf_op jit(solution)/shard_map/all_to_all | solution.py:205
  96.4 23.3 %all_to_all.21 = bf16[64,16,256]{2,1,0:T(8,128)(2,1)} all-to-all(bf16[64,16,256]{2,1,0:T(8,128)(2,1)S(1)} %broadcast_in_dim.5), channel_id=1, replica_groups=mesh['grp'=8,'inner_0'=8,'inner_1'=4,'inner_2'=2] {'inner_0','inner_1','..., dimensions={0} | all-to-all | bytes 1048576 | tf_op jit(solution)/shard_map/all_to_all | solution.py:162
  119.7 23.3 %backward.1 = (f32[16,256]{1,0:T(8,128)}, bf16[1024,256]{1,0:T(8,128)(2,1)}, f32[16,256]{1,0:T(8,128)}) custom-call(s32[3]{0:T(128)} %pad_add_fusion.place_ref, bf16[1024,256]{1,0:T(8,128)(2,1)} %bitcast.7, f32[16,256]{1,0:T(8,128)} %copy-done.8, bf16[1024,512]{1,0:T(8,128)(2,1)} %get-tuple-element.9.pivot_ref, f32[4,128,256]{2,1,0:T(8,128)} %get-tuple-element.10.pair_ref, ...), custom_call_target="tpu_custom_call" | custom-call | tf_op jit(solution)/shard_map/backward/pallas_call | solution.py:208
  142.9 23.4 %all_to_all.22 = bf16[64,16,256]{2,1,0:T(8,128)(2,1)S(1)} all-to-all(bf16[64,16,256]{2,1,0:T(8,128)(2,1)} %bitcast.9), channel_id=1, replica_groups=mesh['grp'=8,'inner_0'=8,'inner_1'=4,'inner_2'=2] {'inner_0','inner_1','..., dimensions={0} | all-to-all | bytes 1048576 | tf_op jit(solution)/shard_map/all_to_all | solution.py:218
  166.4 1.3 add_multiply_fusion
  (34 shorter events, 1.1 us)
Async XLA Ops:
  2.2 59.5 %all-to-all-start = ((bf16[64,16,256]{2,1,0:T(8,128)(2,1)}), bf16[64,16,256]{2,1,0:T(8,128)(2,1)S(1)}, u32[]{:S(2)}, u32[]{:S(2)}) async-start(bf16[64,16,256]{2,1,0:T(8,128)(2,1)} %broadcast_in_dim.4), calls=%async_computation | async-start | bytes 1048576 | tf_op jit(solution)/shard_map/all_to_all | solution.py:162
  17.8 43.9 %copy-start.3 = (bf16[8,128,128]{2,1,0:T(8,128)(2,1)}, bf16[8,128,128]{2,1,0:T(8,128)(2,1)S(1)}, u32[]{:S(2)}) copy-start(bf16[8,128,128]{2,1,0:T(8,128)(2,1)S(1)} %constant_dynamic-update-slice_fusion.own) | copy-start | bytes 786436
  17.8 11.4 %collective-permute-start.1 = (bf16[8,128,128]{2,1,0:T(8,128)(2,1)S(1)}, bf16[8,128,128]{2,1,0:T(8,128)(2,1)S(1)}, u32[]{:S(2)}, u32[]{:S(2)}) collective-permute-start(bf16[8,128,128]{2,1,0:T(8,128)(2,1)S(1)} %constant_dynamic-update-slice_fusion.own), channel_id=1, source_target_pairs={{0,448},{64,0},{128,64},{192,128},{256,192},{320,256},{384,320},{4... | collective-permute-start | bytes 786440 | tf_op jit(solution)/shard_map/ppermute | solution.py:157
  21.1 10.2 %collective-permute-start = (bf16[8,128,128]{2,1,0:T(8,128)(2,1)S(1)}, bf16[8,128,128]{2,1,0:T(8,128)(2,1)S(1)}, u32[]{:S(2)}, u32[]{:S(2)}) collective-permute-start(bf16[8,128,128]{2,1,0:T(8,128)(2,1)S(1)} %constant_dynamic-update-slice_fusion.own), channel_id=1, source_target_pairs={{0,64},{64,128},{128,192},{192,256},{256,320},{320,384},{384,448},... | collective-permute-start | bytes 786440 | tf_op jit(solution)/shard_map/ppermute | solution.py:157
  29.2 32.5 %copy-start.4 = (bf16[8,128,128]{2,1,0:T(8,128)(2,1)}, bf16[8,128,128]{2,1,0:T(8,128)(2,1)S(1)}, u32[]{:S(2)}) copy-start(bf16[8,128,128]{2,1,0:T(8,128)(2,1)S(1)} %collective-permute-done.1.b1) | copy-start | bytes 786436
  29.2 10.5 %collective-permute-start.3 = (bf16[8,128,128]{2,1,0:T(8,128)(2,1)S(1)}, bf16[8,128,128]{2,1,0:T(8,128)(2,1)S(1)}, u32[]{:S(2)}, u32[]{:S(2)}) collective-permute-start(bf16[8,128,128]{2,1,0:T(8,128)(2,1)S(1)} %collective-permute-done.1.b1), channel_id=1, source_target_pairs={{0,448},{64,0},{128,64},{192,128},{256,192},{320,256},{384,320},{4... | collective-permute-start | bytes 786440 | tf_op jit(solution)/shard_map/ppermute | solution.py:157
  31.2 30.4 %copy-start.5 = (bf16[8,128,128]{2,1,0:T(8,128)(2,1)}, bf16[8,128,128]{2,1,0:T(8,128)(2,1)S(1)}, u32[]{:S(2)}) copy-start(bf16[8,128,128]{2,1,0:T(8,128)(2,1)S(1)} %collective-permute-done.f1) | copy-start | bytes 786436
  31.2 10.4 %collective-permute-start.2 = (bf16[8,128,128]{2,1,0:T(8,128)(2,1)S(1)}, bf16[8,128,128]{2,1,0:T(8,128)(2,1)S(1)}, u32[]{:S(2)}, u32[]{:S(2)}) collective-permute-start(bf16[8,128,128]{2,1,0:T(8,128)(2,1)S(1)} %collective-permute-done.f1), channel_id=1, source_target_pairs={{0,64},{64,128},{128,192},{192,256},{256,320},{320,384},{384,448},... | collective-permute-start | bytes 786440 | tf_op jit(solution)/shard_map/ppermute | solution.py:157
  39.7 22.0 %copy-start.6 = (bf16[8,128,128]{2,1,0:T(8,128)(2,1)}, bf16[8,128,128]{2,1,0:T(8,128)(2,1)S(1)}, u32[]{:S(2)}) copy-start(bf16[8,128,128]{2,1,0:T(8,128)(2,1)S(1)} %collective-permute-done.3.b2) | copy-start | bytes 786436
  39.7 9.6 %collective-permute-start.5 = (bf16[8,128,128]{2,1,0:T(8,128)(2,1)S(1)}, bf16[8,128,128]{2,1,0:T(8,128)(2,1)S(1)}, u32[]{:S(2)}, u32[]{:S(2)}) collective-permute-start(bf16[8,128,128]{2,1,0:T(8,128)(2,1)S(1)} %collective-permute-done.3.b2), channel_id=1, source_target_pairs={{0,448},{64,0},{128,64},{192,128},{256,192},{320,256},{384,320},{4... | collective-permute-start | bytes 786440 | tf_op jit(solution)/shard_map/ppermute | solution.py:157
  41.6 20.1 %copy-start.7 = (bf16[8,128,128]{2,1,0:T(8,128)(2,1)}, bf16[8,128,128]{2,1,0:T(8,128)(2,1)S(1)}, u32[]{:S(2)}) copy-start(bf16[8,128,128]{2,1,0:T(8,128)(2,1)S(1)} %collective-permute-done.2.f2) | copy-start | bytes 786436
  41.6 9.7 %collective-permute-start.4 = (bf16[8,128,128]{2,1,0:T(8,128)(2,1)S(1)}, bf16[8,128,128]{2,1,0:T(8,128)(2,1)S(1)}, u32[]{:S(2)}, u32[]{:S(2)}) collective-permute-start(bf16[8,128,128]{2,1,0:T(8,128)(2,1)S(1)} %collective-permute-done.2.f2), channel_id=1, source_target_pairs={{0,64},{64,128},{128,192},{192,256},{256,320},{320,384},{384,448},... | collective-permute-start | bytes 786440 | tf_op jit(solution)/shard_map/ppermute | solution.py:157
  49.3 12.4 %copy-start.1 = (bf16[8,128,128]{2,1,0:T(8,128)(2,1)}, bf16[8,128,128]{2,1,0:T(8,128)(2,1)S(1)}, u32[]{:S(2)}) copy-start(bf16[8,128,128]{2,1,0:T(8,128)(2,1)S(1)} %collective-permute-done.5.b3) | copy-start | bytes 786436
  49.3 12.3 %collective-permute-start.7 = (bf16[4,128,128]{2,1,0:T(8,128)(2,1)S(1)}, bf16[4,128,128]{2,1,0:T(8,128)(2,1)S(1)}, u32[]{:S(2)}, u32[]{:S(2)}) collective-permute-start(bf16[4,128,128]{2,1,0:T(8,128)(2,1)S(1)} %slice.9), channel_id=1, source_target_pairs={{0,448},{64,0},{128,64},{192,128},{256,192},{320,256},{384,320},{4... | collective-permute-start | bytes 393224 | tf_op jit(solution)/shard_map/ppermute | solution.py:157
  51.3 10.4 %copy-start.2 = (bf16[8,128,128]{2,1,0:T(8,128)(2,1)}, bf16[8,128,128]{2,1,0:T(8,128)(2,1)S(1)}, u32[]{:S(2)}) copy-start(bf16[8,128,128]{2,1,0:T(8,128)(2,1)S(1)} %collective-permute-done.4.f3) | copy-start | bytes 786436
  51.3 10.3 %collective-permute-start.6 = (bf16[4,128,128]{2,1,0:T(8,128)(2,1)S(1)}, bf16[4,128,128]{2,1,0:T(8,128)(2,1)S(1)}, u32[]{:S(2)}, u32[]{:S(2)}) collective-permute-start(bf16[4,128,128]{2,1,0:T(8,128)(2,1)S(1)} %slice.8), channel_id=1, source_target_pairs={{0,64},{64,128},{128,192},{192,256},{256,320},{320,384},{384,448},... | collective-permute-start | bytes 393224 | tf_op jit(solution)/shard_map/ppermute | solution.py:157
  61.6 0.7 copy-start.9
  61.6 0.7 copy-start.10
  61.6 0.9 copy-start
  96.3 23.3 %copy-start.8 = (f32[16,256]{1,0:T(8,128)}, f32[16,256]{1,0:T(8,128)S(1)}, u32[]{:S(2)}) copy-start(f32[16,256]{1,0:T(8,128)S(1)} %convert_reduce_fusion.1.own_ref) | copy-start | bytes 49156

commit v2 on v1

v2 whole, which is shorter than its diff:
```python
import jax
import jax.numpy as jnp
from jax import lax
from jax.experimental import pallas as pl
from jax.experimental.pallas import tpu as pltpu
from jax.sharding import Mesh
from jax.sharding import PartitionSpec as P

INNER = ("inner_0", "inner_1", "inner_2")
LOW = jnp.bfloat16
FULL = jnp.float32


def dot(a, b, ca, cb):
    return lax.dot_general(a, b, (((ca,), (cb,)), ((), ())), preferred_element_type=FULL)


def halves(x):
    high = x.astype(LOW)
    return high, (x - high.astype(FULL)).astype(LOW)


def fine_dot(a, b, ca, cb):
    ah, al = halves(a)
    bh, bl = halves(b)
    return dot(ah, bh, ca, cb) + (dot(ah, bl, ca, cb) + dot(al, bh, ca, cb))


def spread(x, i):
    return jnp.broadcast_to(x[i : i + 1, :], x.shape)


def inverse_factors(grams):
    n, panel = grams[0].shape[0], 4
    count, groups = len(grams), n // 8
    sub = lax.broadcasted_iota(jnp.int32, (8, n), 0)
    lane = lax.broadcasted_iota(jnp.int32, (8, n), 1)
    left = [[g[8 * i : 8 * i + 8] for i in range(groups)] for g in grams]
    right = [[(lane == sub + 8 * i).astype(FULL) for i in range(groups)] for _ in grams]
    upper, lower = [[] for _ in grams], [[] for _ in grams]
    for p in range(groups):
        end = (p // panel + 1) * panel
        raw = [[[None] * 8 for _ in range(p, end)] for _ in grams]
        for some in (range(p, p + 1), range(p + 1, end)):
            for k in range(8):
                for t in range(count):
                    for g in some:
                        column = left[t][g][:, 8 * p + k : 8 * p + k + 1]
                        raw[t][g - p][k] = jnp.broadcast_to(column, (8, n))
        for t in range(count):
            a, b, col, pivots = left[t][p], right[t][p], list(raw[t][0]), None
            for k in range(8):
                pivot = spread(col[k], k)
                pivots = pivot if pivots is None else jnp.where(sub == k, pivot, pivots)
                if k < 7:
                    f = jnp.where(sub > k, col[k], 0.0) * (1.0 / pivot)
                    for i in range(k + 1, 8):
                        col[i] = col[i] - f * spread(col[i], k)
                    a, b = a - f * spread(a, k), b - f * spread(b, k)
            root = lax.rsqrt(pivots)
            upper[t].append(a * root)
            lower[t].append(b * root)
            if p + 1 < end:
                ratio = 1.0 / pivots
                y, z = a * ratio, b * ratio
                for i in range(7, 0, -1):
                    f = jnp.where(sub < i, col[i] * ratio, 0.0)
                    y, z = y - f * spread(y, i), z - f * spread(z, i)
                for g in range(p + 1, end):
                    for k in range(8):
                        c = raw[t][g - p][k]
                        left[t][g] = left[t][g] - c * spread(y, k)
                        right[t][g] = right[t][g] - c * spread(z, k)
        if p + 1 == end and end < groups:
            for t in range(count):
                ah, al = halves(jnp.concatenate(upper[t][end - panel :], 0))
                bh, bl = halves(jnp.concatenate(lower[t][end - panel :], 0))
                factor = jnp.concatenate([ah, ah, al], 0)
                cut_a = dot(factor, jnp.concatenate([ah, al, ah], 0), 0, 0)
                cut_b = dot(factor, jnp.concatenate([bh, bl, bh], 0), 0, 0)
                for g in range(end, groups):
                    left[t][g] = left[t][g] - cut_a[8 * g : 8 * g + 8]
                    right[t][g] = right[t][g] - cut_b[8 * g : 8 * g + 8]
    return [jnp.concatenate(rows, 0) for rows in lower]


def probe_body(left_ref, sketch_ref, out_ref):
    for k in range(left_ref.shape[0]):
        for t in range(out_ref.shape[1]):
            cols = slice(128 * t, 128 * t + 128)
            out_ref[k, t] = dot(left_ref[k, :, cols], sketch_ref[:, cols], 0, 0)


def early_body(place_ref, own, f1, b1, f2, b2, f3, b3, right_ref, pair_ref, pivot_ref, factor):
    group, groups = place_ref[0], place_ref[2]
    slots, n = right_ref.shape[0], own.shape[1]

    def put(ref, distance):
        at = pl.multiple_of(lax.rem(group + distance, groups) * n, n)
        for k in range(slots):
            cols = slice(128 * k, 128 * k + 128)
            if ref is None:
                factor[pl.ds(at, n), cols] = jnp.zeros((n, 128), LOW)
                pivot_ref[pl.ds(at, n), cols] = jnp.zeros((n, 128), LOW)
            else:
                factor[pl.ds(at, n), cols] = ref[k]
                pivot_ref[pl.ds(at, n), cols] = ref[k + slots]

    put(own, 0)
    for s, (f, b) in enumerate(((f1, b1), (f2, b2), (f3, b3))):
        put(f, groups - 1 - s)
        put(b, 1 + s)
    put(None, groups // 2)
    for k in range(slots):
        pair_ref[k] = dot(factor[:, 128 * k : 128 * k + 128], right_ref[k], 0, 0)


def forward_body(
    place_ref, f4, b4, early_ref, pivot_ref, right_ref, probe_ref, tall_ref, tright_ref,
    sketch_ref, keep_ref, send_ref, pair_ref, part,
):
    group, live, groups, core = place_ref[0], place_ref[1], place_ref[2], place_ref[3]
    slots, n, half = right_ref.shape[0], f4.shape[1], keep_ref.shape[0]
    at = pl.multiple_of(lax.rem(group + groups // 2, groups) * n, n)
    mixed = []
    for k in range(slots):
        pair = early_ref[k] + dot(f4[k], right_ref[k], 0, 0)
        pair_ref[k] = pair
        row = []
        for t in range(2):
            cols = slice(128 * t, 128 * t + 128)
            value = fine_dot(pair[:, cols], probe_ref[k, t], 1, 0)
            row.append(jnp.where(k < live, -value, 0.0).astype(LOW))
        mixed.append(jnp.concatenate(row, 1))
    mixed = jnp.concatenate(mixed, 0)
    update = dot(pivot_ref[...], mixed, 1, 0)
    for t in range(2):
        cols = slice(128 * t, 128 * t + 128)
        core_part = dot(tright_ref[:, cols], sketch_ref[:, cols], 0, 0).astype(LOW)
        part[:, cols] = update[:, cols] + dot(tall_ref[:, cols], core_part, 1, 0)
    last = jnp.concatenate([b4[k] for k in range(slots)], 1)
    part[pl.ds(at, n), :] += dot(last, mixed, 1, 0)
    whole = part[...].reshape(half, 2, 16, part.shape[1])
    keep_ref[...] = jnp.where(core == 0, whole[:, 0], whole[:, 1])
    send_ref[...] = jnp.where(core == 0, whole[:, 1], whole[:, 0])


def backward_body(
    place_ref, mine_ref, other_ref, own_ref, tright_ref, b4,
    pivot_any, pair_any, left_any, tall_any,
    basis_ref, term_ref, direct_ref,
    whole, pivot_ref, pair_ref, left_ref, tall_ref, sems,
):
    group, live, groups, core = place_ref[0], place_ref[1], place_ref[2], place_ref[3]
    copies = [
        pltpu.make_async_copy(source, target, sems.at[i])
        for i, (source, target) in enumerate(
            ((pivot_any, pivot_ref), (tall_any, tall_ref), (pair_any, pair_ref), (left_any, left_ref))
        )
    ]
    for c in copies:
        c.start()
    slots, rows, n = left_ref.shape[0], whole.shape[0], b4.shape[1]
    mine, other = mine_ref[...], other_ref[...]
    even, odd = jnp.where(core == 0, mine, other), jnp.where(core == 0, other, mine)
    whole[...] = jnp.concatenate([even[:, None], odd[:, None]], 1).reshape(rows, whole.shape[1])
    turned, grams = [], []
    for t in range(2):
        s = whole[:, 128 * t : 128 * t + 128]
        turned.append(s.T)
        grams.append(dot(turned[t], s, 1, 0) / rows)
    for c in copies:
        c.wait()
    at = pl.multiple_of(lax.rem(group + groups // 2, groups) * n, n)
    last = jnp.concatenate([b4[k] for k in range(slots)], 1)
    seen, seen_target = [], []
    for t in range(2):
        cols = slice(128 * t, 128 * t + 128)
        seen.append(
            dot(turned[t], pivot_ref[...], 1, 0) + dot(whole[pl.ds(at, n), cols], last, 0, 0)
        )
        seen_target.append(dot(turned[t], tall_ref[:, cols], 1, 0))
    inverse = inverse_factors(grams)
    for t in range(2):
        cols = slice(128 * t, 128 * t + 128)
        basis_ref[:, cols] = fine_dot(own_ref[:, cols], inverse[t], 1, 1)
        back = fine_dot(inverse[t], seen[t], 1, 0)
        total = None
        for k in range(slots):
            folded = fine_dot(back[:, 128 * k : 128 * k + 128], pair_ref[k, :, cols], 1, 0)
            folded = jnp.where(k < live, -folded, 0.0).astype(LOW)
            term = dot(left_ref[k, :, cols], folded, 1, 1)
            total = term if total is None else total + term
        term_ref[:, cols] = total.astype(LOW)
        target_back = fine_dot(inverse[t], seen_target[t], 1, 0).astype(LOW)
        direct_ref[:, cols] = dot(tright_ref[:, cols], target_back, 1, 1)


SMEM = pl.BlockSpec(memory_space=pltpu.SMEM)
WHOLE = pl.BlockSpec()
PLACED = pl.BlockSpec(memory_space=pl.ANY)


def shift(x, axis, by):
    n = lax.axis_size(axis)
    return lax.ppermute(x, axis, [(i, (i + by) % n) for i in range(n)])


def to_all(x, axes):
    n = lax.axis_size(axes)
    return lax.all_to_all(jnp.broadcast_to(x[None], (n, *x.shape)), axes, 0, 0, tiled=True)


def whole_block(x):
    return pl.BlockSpec(x.shape, lambda i, place: (0,) * x.ndim)


def shards(
    row_left, row_right, col_left, col_right, sketch_cols, target_left, target_right, live_counts
):
    slots, rows, width = col_left.shape
    block = target_left.shape[0]
    groups, chunk = lax.axis_size("grp"), row_left.shape[1]
    n, far = lax.axis_size(INNER), INNER[:2]
    place = jnp.stack(
        [lax.axis_index("grp"), live_counts[0], jnp.int32(groups), lax.axis_index(INNER[2])]
    ).astype(jnp.int32)
    own = jnp.concatenate([row_right, row_left], 0)
    chunks, up, down = [own], own, own
    for step in range(3):
        up, down = shift(up, "grp", 1), shift(down, "grp", -1)
        if step == 0:
            up, down, target_left = lax.optimization_barrier((up, down, target_left))
            all_left = to_all(target_left, INNER).reshape(rows, width)
            probe = pl.pallas_call(
                probe_body,
                out_shape=jax.ShapeDtypeStruct((slots, 2, 128, 128), FULL),
                name="probe",
            )(col_left, sketch_cols)
            own_sketch = lax.dynamic_slice_in_dim(
                sketch_cols, lax.axis_index(INNER) * block, block, 0
            )
        if step == 1:
            up, down, probe, own_sketch, place = lax.optimization_barrier(
                (up, down, probe, own_sketch, place)
            )
        chunks += [up, down]
    last_up, last_down = shift(up[:slots], "grp", 1), shift(down[slots:], "grp", -1)
    early, pivot = pl.pallas_call(
        early_body,
        in_specs=[SMEM] + [WHOLE] * 8,
        out_shape=(
            jax.ShapeDtypeStruct((slots, 128, width), FULL),
            jax.ShapeDtypeStruct((rows, slots * 128), LOW),
        ),
        scratch_shapes=[pltpu.VMEM((rows, slots * 128), LOW)],
        name="early",
    )(place, *chunks, col_right)
    ins = (last_up, last_down, early, pivot, col_right, probe, all_left, target_right, own_sketch)
    specs = [whole_block(x) for x in ins]
    specs[4] = pl.BlockSpec(
        (slots, chunk, width),
        lambda i, place: (0, lax.rem(place[0] + place[2] // 2, place[2]), 0),
    )
    outs = (
        jax.ShapeDtypeStruct((n // 2, block, width), FULL),
        jax.ShapeDtypeStruct((n // 2, block, width), FULL),
        jax.ShapeDtypeStruct((slots, 128, width), FULL),
    )
    keep, send, pair = pl.pallas_call(
        forward_body,
        grid_spec=pltpu.PrefetchScalarGridSpec(
            num_scalar_prefetch=1,
            grid=(1,),
            in_specs=specs,
            out_specs=[whole_block(x) for x in outs],
            scratch_shapes=[pltpu.VMEM((rows, width), FULL)],
        ),
        out_shape=outs,
        name="forward",
    )(place, *ins)
    summed = keep + shift(send, INNER[2], 1)
    own_sum = jnp.sum(lax.all_to_all(summed, far, 0, 0, tiled=True), 0)
    mine = to_all(own_sum.astype(LOW), far)
    other = shift(mine, INNER[2], 1)
    basis, term, direct = pl.pallas_call(
        backward_body,
        in_specs=[SMEM] + [WHOLE] * 5 + [PLACED] * 4,
        out_shape=(
            jax.ShapeDtypeStruct((block, width), FULL),
            jax.ShapeDtypeStruct((rows, width), LOW),
            jax.ShapeDtypeStruct((block, width), FULL),
        ),
        scratch_shapes=[
            pltpu.VMEM((rows, width), LOW),
            pltpu.VMEM(pivot.shape, LOW),
            pltpu.VMEM(pair.shape, FULL),
            pltpu.VMEM(col_left.shape, LOW),
            pltpu.VMEM(all_left.shape, LOW),
            pltpu.SemaphoreType.DMA((4,)),
        ],
        name="backward",
    )(place, mine, other, own_sum, target_right, last_down, pivot, pair, col_left, all_left)
    pieces = lax.all_to_all(term.reshape(n, block, width), INNER, 0, 0, tiled=True)
    coeffs = (jnp.sum(pieces.astype(FULL), 0) + direct) / rows
    return basis, coeffs


def solution(mesh):
    finer = Mesh(
        mesh.devices.reshape(mesh.shape["grp"], 8, 4, 2), ("grp", "inner_0", "inner_1", "inner_2")
    )
    return jax.shard_map(
        shards,
        mesh=finer,
        in_specs=(
            P(INNER, "grp", None),
            P(INNER, "grp", None),
            P(INNER, None, "grp"),
            P(INNER, None, "grp"),
            P(None, "grp"),
            P(INNER, "grp"),
            P(INNER, "grp"),
            P(INNER),
        ),
        out_specs=(P(INNER, "grp"), P(INNER, "grp")),
        check_vma=False,
    )
```

time: 171 us -> 165 us (0.965)
  the two profiles are of different devices: /device:TPU:56 before, /device:TPU:1 now
where the time goes in v2:
time: 165 us; the launch traced here: 164 us
  blocking collectives  63.4 us (38%)
  starting transfers between devices  54.9 us (33%)
  Pallas kernels  23.8 us (14%)
  waiting for transfers between devices  11.1 us (7%)
  local copies, waits for them, and re-layouts  6.29 us (4%)
  other arithmetic  3.26 us (2%)
    ppermute x10, starting transfers between devices, shift(): return lax.ppermute(x, axis, [(i, (i + by) % n) for i in range(n)])  38.1 us
    all_to_all x1, blocking collectives, shards(): own_sum = jnp.sum(lax.all_to_all(summed, far, 0, 0, tiled=True), 0)  25.9 us
    all_to_all x1, blocking collectives, shards(): lax.all_to_all(term.reshape(n, block, width), INNER, 0, 0, tiled=True)  22.3 us
    all_to_all x1, starting transfers between devices, to_all(): lax.all_to_all(jnp.broadcast_to(x[None], (n, *x.shape)), axes, 0, 0, tile...  16.8 us
    all_to_all x1, blocking collectives, to_all(): lax.all_to_all(jnp.broadcast_to(x[None], (n, *x.shape)), axes, 0, 0, tile...  15.1 us
    ppermute x10, waiting for transfers between devices, shift(): return lax.ppermute(x, axis, [(i, (i + by) % n) for i in range(n)])  11.1 us
    pallas_call x1, Pallas kernels, shards(): pl.pallas_call(backward_body, in_specs=[SMEM] + [WHOLE] * 5 + [PLACED] *...  10.9 us
    pallas_call x1, Pallas kernels, shards(): pl.pallas_call(forward_body, grid_spec=pltpu.PrefetchScalarGridSpec(num_s...  5.53 us
  transfers between devices with their start and end apart: 11, of which 7 were waited for; matrix products, arithmetic and copies ran while one was open for 1% of the time, Pallas kernels for 4%

profile of v2, /device:TPU:1, one launch (start us, length us, event | category | flops | bytes accessed | tf_op | source)
XLA Modules:
  0.0 164.2 jit_solution(5375275234872879809)
XLA Ops:
  2.5 4.0 %collective-permute-start = (bf16[8,128,128]{2,1,0:T(8,128)(2,1)S(1)}, bf16[8,128,128]{2,1,0:T(8,128)(2,1)S(1)}, u32[]{:S(2)}, u32[]{:S(2)}) collective-permute-start(bf16[8,128,128]{2,1,0:T(8,128)(2,1)S(1)} %constant_dynamic-update-slice_fusion.own), channel_id=1, source_target_pairs={{0,64},{64,128},{128,192},{192,256},{256,320},{320,384},{384,448},... | collective-permute-start | bytes 786440 | tf_op jit(solution)/shard_map/ppermute | solution.py:206
  6.5 3.8 %collective-permute-start.1 = (bf16[8,128,128]{2,1,0:T(8,128)(2,1)S(1)}, bf16[8,128,128]{2,1,0:T(8,128)(2,1)S(1)}, u32[]{:S(2)}, u32[]{:S(2)}) collective-permute-start(bf16[8,128,128]{2,1,0:T(8,128)(2,1)S(1)} %constant_dynamic-update-slice_fusion.own), channel_id=1, source_target_pairs={{0,448},{64,0},{128,64},{192,128},{256,192},{320,256},{384,320},{4... | collective-permute-start | bytes 786440 | tf_op jit(solution)/shard_map/ppermute | solution.py:206
  10.3 1.8 %collective-permute-done.f1 = bf16[8,128,128]{2,1,0:T(8,128)(2,1)S(1)} collective-permute-done((bf16[8,128,128]{2,1,0:T(8,128)(2,1)S(1)}, bf16[8,128,128]{2,1,0:T(8,128)(2,1)S(1)}, u32[]{:S(2)}, u32[]{:S(2)}) %collective-permute-start) | collective-permute-done | bytes 262176 | tf_op jit(solution)/shard_map/ppermute | solution.py:206
  12.2 1.5 collective-permute-done.1.b1
  13.6 1.5 broadcast_in_dim.4
  15.2 16.8 %all-to-all-start = ((bf16[64,16,256]{2,1,0:T(8,128)(2,1)}), bf16[64,16,256]{2,1,0:T(8,128)(2,1)S(1)}, u32[]{:S(2)}, u32[]{:S(2)}) async-start(bf16[64,16,256]{2,1,0:T(8,128)(2,1)} %broadcast_in_dim.4), calls=%async_computation | async-start | bytes 1048576 | tf_op jit(solution)/shard_map/all_to_all | solution.py:211
  32.0 3.2 %collective-permute-start.2 = (bf16[8,128,128]{2,1,0:T(8,128)(2,1)S(1)}, bf16[8,128,128]{2,1,0:T(8,128)(2,1)S(1)}, u32[]{:S(2)}, u32[]{:S(2)}) collective-permute-start(bf16[8,128,128]{2,1,0:T(8,128)(2,1)S(1)} %collective-permute-done.f1), channel_id=1, source_target_pairs={{0,64},{64,128},{128,192},{192,256},{256,320},{320,384},{384,448},... | collective-permute-start | bytes 786440 | tf_op jit(solution)/shard_map/ppermute | solution.py:206
  35.2 3.7 %collective-permute-start.3 = (bf16[8,128,128]{2,1,0:T(8,128)(2,1)S(1)}, bf16[8,128,128]{2,1,0:T(8,128)(2,1)S(1)}, u32[]{:S(2)}, u32[]{:S(2)}) collective-permute-start(bf16[8,128,128]{2,1,0:T(8,128)(2,1)S(1)} %collective-permute-done.1.b1), channel_id=1, source_target_pairs={{0,448},{64,0},{128,64},{192,128},{256,192},{320,256},{384,320},{4... | collective-permute-start | bytes 786440 | tf_op jit(solution)/shard_map/ppermute | solution.py:206
  39.6 3.2 %probe.1.probe_ref = f32[4,2,128,128]{3,2,1,0:T(8,128)} custom-call(bf16[4,1024,256]{2,1,0:T(8,128)(2,1)} %left_any.1, bf16[1024,256]{1,0:T(8,128)(2,1)} %sketch_ref.1), custom_call_target="tpu_custom_call" | custom-call | tf_op jit(solution)/shard_map/probe/pallas_call | solution.py:235
  45.4 4.0 %collective-permute-start.6 = (bf16[8,128,128]{2,1,0:T(8,128)(2,1)S(1)}, bf16[8,128,128]{2,1,0:T(8,128)(2,1)S(1)}, u32[]{:S(2)}, u32[]{:S(2)}) collective-permute-start(bf16[8,128,128]{2,1,0:T(8,128)(2,1)S(1)} %collective-permute-done.3.b2), channel_id=1, source_target_pairs={{0,448},{64,0},{128,64},{192,128},{256,192},{320,256},{384,320},{4... | collective-permute-start | bytes 786440 | tf_op jit(solution)/shard_map/ppermute | solution.py:206
  49.5 2.4 %collective-permute-start.4 = (bf16[8,128,128]{2,1,0:T(8,128)(2,1)S(1)}, bf16[8,128,128]{2,1,0:T(8,128)(2,1)S(1)}, u32[]{:S(2)}, u32[]{:S(2)}) collective-permute-start(bf16[8,128,128]{2,1,0:T(8,128)(2,1)S(1)} %collective-permute-done.2.f2), channel_id=1, source_target_pairs={{0,64},{64,128},{128,192},{192,256},{256,320},{320,384},{384,448},... | collective-permute-start | bytes 786440 | tf_op jit(solution)/shard_map/ppermute | solution.py:206
  51.9 3.4 %collective-permute-done.6.b3 = bf16[8,128,128]{2,1,0:T(8,128)(2,1)S(1)} collective-permute-done((bf16[8,128,128]{2,1,0:T(8,128)(2,1)S(1)}, bf16[8,128,128]{2,1,0:T(8,128)(2,1)S(1)}, u32[]{:S(2)}, u32[]{:S(2)}) %collective-permute-start.6) | collective-permute-done | bytes 262176 | tf_op jit(solution)/shard_map/ppermute | solution.py:206
  55.4 3.8 %collective-permute-start.7 = (bf16[4,128,128]{2,1,0:T(8,128)(2,1)S(1)}, bf16[4,128,128]{2,1,0:T(8,128)(2,1)S(1)}, u32[]{:S(2)}, u32[]{:S(2)}) collective-permute-start(bf16[4,128,128]{2,1,0:T(8,128)(2,1)S(1)} %slice.9), channel_id=1, source_target_pairs={{0,448},{64,0},{128,64},{192,128},{256,192},{320,256},{384,320},{4... | collective-permute-start | bytes 393224 | tf_op jit(solution)/shard_map/ppermute | solution.py:206
  59.2 1.9 %collective-permute-start.5 = (bf16[4,128,128]{2,1,0:T(8,128)(2,1)S(1)}, bf16[4,128,128]{2,1,0:T(8,128)(2,1)S(1)}, u32[]{:S(2)}, u32[]{:S(2)}) collective-permute-start(bf16[4,128,128]{2,1,0:T(8,128)(2,1)S(1)} %slice.8), channel_id=1, source_target_pairs={{0,64},{64,128},{128,192},{192,256},{256,320},{320,384},{384,448},... | collective-permute-start | bytes 393224 | tf_op jit(solution)/shard_map/ppermute | solution.py:206
  61.2 4.1 %early.1 = (f32[4,128,256]{2,1,0:T(8,128)}, bf16[1024,512]{1,0:T(8,128)(2,1)}) custom-call(s32[4]{0:T(128)} %pad_add_fusion.place_ref, bf16[8,128,128]{2,1,0:T(8,128)(2,1)} %copy-done.4, bf16[8,128,128]{2,1,0:T(8,128)(2,1)} %copy-done.6, bf16[8,128,128]{2,1,0:T(8,128)(2,1)} %copy-done.7, bf16[8,128,128]{2,1,0:T(8,128)(2,1)} %copy-done.8, ...), custom_call_target="tpu_custom_call" | custom-call | tf_op jit(solution)/shard_map/early/pallas_call | solution.py:249
  67.0 5.5 %forward.1 = (f32[32,16,256]{2,1,0:T(8,128)}, f32[32,16,256]{2,1,0:T(8,128)}, f32[4,128,256]{2,1,0:T(8,128)}) custom-call(s32[4]{0:T(128)} %pad_add_fusion.place_ref, bf16[4,128,128]{2,1,0:T(8,128)(2,1)} %copy-done.12, bf16[4,128,128]{2,1,0:T(8,128)(2,1)} %copy-done.5, f32[4,128,256]{2,1,0:T(8,128)} %get-tuple-element.23.early_ref, ...), custom_call_target="tpu_custom_call" | custom-call | tf_op jit(solution)/shard_map/forward/pallas_call | solution.py:270
  72.5 5.5 %collective-permute-start.8 = (f32[32,16,256]{2,1,0:T(8,128)}, f32[32,16,256]{2,1,0:T(8,128)S(1)}, u32[]{:S(2)}, u32[]{:S(2)}) collective-permute-start(f32[32,16,256]{2,1,0:T(8,128)} %get-tuple-element.29), channel_id=1, source_target_pairs={{0,1},{1,0},{2,3},{3,2},{4,5},{5,4},{6,7},{7,6},{8,9},{9,8},{10,11... | collective-permute-start | bytes 1572872 | tf_op jit(solution)/shard_map/ppermute | solution.py:206
  78.0 1.7 %collective-permute-done.8 = f32[32,16,256]{2,1,0:T(8,128)S(1)} collective-permute-done((f32[32,16,256]{2,1,0:T(8,128)}, f32[32,16,256]{2,1,0:T(8,128)S(1)}, u32[]{:S(2)}, u32[]{:S(2)}) %collective-permute-start.8) | collective-permute-done | bytes 524320 | tf_op jit(solution)/shard_map/ppermute | solution.py:206
  80.9 25.9 %all_to_all.20 = f32[32,16,256]{2,1,0:T(8,128)S(1)} all-to-all(f32[32,16,256]{2,1,0:T(8,128)S(1)} %add.18), channel_id=1, replica_groups=mesh['grp'=8,'inner_0'=8,'inner_1'=4,'inner_2'=2] {'inner_0','inner_1'}, dimensions={0} | all-to-all | bytes 1048576 | tf_op jit(solution)/shard_map/all_to_all | solution.py:283
  106.9 15.1 %all_to_all.21.mine_ref = bf16[32,16,256]{2,1,0:T(8,128)(2,1)S(1)} all-to-all(bf16[32,16,256]{2,1,0:T(8,128)(2,1)S(1)} %broadcast_in_dim.5), channel_id=1, replica_groups=mesh['grp'=8,'inner_0'=8,'inner_1'=4,'inner_2'=2] {'inner_0','inner_1'}, dimensions={0} | all-to-all | bytes 524288 | tf_op jit(solution)/shard_map/all_to_all | solution.py:211
  122.0 5.7 %collective-permute-start.9 = (bf16[32,16,256]{2,1,0:T(8,128)(2,1)S(1)}, bf16[32,16,256]{2,1,0:T(8,128)(2,1)S(1)}, u32[]{:S(2)}, u32[]{:S(2)}) collective-permute-start(bf16[32,16,256]{2,1,0:T(8,128)(2,1)S(1)} %all_to_all.21.mine_ref), channel_id=1, source_target_pairs={{0,1},{1,0},{2,3},{3,2},{4,5},{5,4},{6,7},{7,6},{8,9},{9,8},{10,11... | collective-permute-start | bytes 786440 | tf_op jit(solution)/shard_map/ppermute | solution.py:206
  129.5 10.9 %backward.1 = (f32[16,256]{1,0:T(8,128)}, bf16[1024,256]{1,0:T(8,128)(2,1)}, f32[16,256]{1,0:T(8,128)}) custom-call(s32[4]{0:T(128)} %pad_add_fusion.place_ref, bf16[32,16,256]{2,1,0:T(8,128)(2,1)} %copy-done.1, bf16[32,16,256]{2,1,0:T(8,128)(2,1)} %copy-done.10, f32[16,256]{1,0:T(8,128)} %copy-done.11, bf16[16,256]{1,0:T(8,128)(2,1)} %tright_ref.3, ...), custom_call_target="tpu_custom_call" | custom-call | tf_op jit(solution)/shard_map/backward/pallas_call | solution.py:286
  140.5 22.3 %all_to_all.22 = bf16[64,16,256]{2,1,0:T(8,128)(2,1)S(1)} all-to-all(bf16[64,16,256]{2,1,0:T(8,128)(2,1)} %bitcast.6), channel_id=1, replica_groups=mesh['grp'=8,'inner_0'=8,'inner_1'=4,'inner_2'=2] {'inner_0','inner_1','..., dimensions={0} | all-to-all | bytes 1048576 | tf_op jit(solution)/shard_map/all_to_all | solution.py:304
  162.9 1.3 add_multiply_fusion
  (44 shorter events, 9.3 us)
Async XLA Ops:
  2.5 40.4 %copy-start.4 = (bf16[8,128,128]{2,1,0:T(8,128)(2,1)}, bf16[8,128,128]{2,1,0:T(8,128)(2,1)S(1)}, u32[]{:S(2)}) copy-start(bf16[8,128,128]{2,1,0:T(8,128)(2,1)S(1)} %constant_dynamic-update-slice_fusion.own) | copy-start | bytes 786436
  2.5 9.7 %collective-permute-start = (bf16[8,128,128]{2,1,0:T(8,128)(2,1)S(1)}, bf16[8,128,128]{2,1,0:T(8,128)(2,1)S(1)}, u32[]{:S(2)}, u32[]{:S(2)}) collective-permute-start(bf16[8,128,128]{2,1,0:T(8,128)(2,1)S(1)} %constant_dynamic-update-slice_fusion.own), channel_id=1, source_target_pairs={{0,64},{64,128},{128,192},{192,256},{256,320},{320,384},{384,448},... | collective-permute-start | bytes 786440 | tf_op jit(solution)/shard_map/ppermute | solution.py:206
  6.5 7.1 %collective-permute-start.1 = (bf16[8,128,128]{2,1,0:T(8,128)(2,1)S(1)}, bf16[8,128,128]{2,1,0:T(8,128)(2,1)S(1)}, u32[]{:S(2)}, u32[]{:S(2)}) collective-permute-start(bf16[8,128,128]{2,1,0:T(8,128)(2,1)S(1)} %constant_dynamic-update-slice_fusion.own), channel_id=1, source_target_pairs={{0,448},{64,0},{128,64},{192,128},{256,192},{320,256},{384,320},{4... | collective-permute-start | bytes 786440 | tf_op jit(solution)/shard_map/ppermute | solution.py:206
  12.2 30.7 %copy-start.6 = (bf16[8,128,128]{2,1,0:T(8,128)(2,1)}, bf16[8,128,128]{2,1,0:T(8,128)(2,1)S(1)}, u32[]{:S(2)}) copy-start(bf16[8,128,128]{2,1,0:T(8,128)(2,1)S(1)} %collective-permute-done.f1) | copy-start | bytes 786436
  13.6 29.2 %copy-start.7 = (bf16[8,128,128]{2,1,0:T(8,128)(2,1)}, bf16[8,128,128]{2,1,0:T(8,128)(2,1)S(1)}, u32[]{:S(2)}) copy-start(bf16[8,128,128]{2,1,0:T(8,128)(2,1)S(1)} %collective-permute-done.1.b1) | copy-start | bytes 786436
  15.2 50.9 %all-to-all-start = ((bf16[64,16,256]{2,1,0:T(8,128)(2,1)}), bf16[64,16,256]{2,1,0:T(8,128)(2,1)S(1)}, u32[]{:S(2)}, u32[]{:S(2)}) async-start(bf16[64,16,256]{2,1,0:T(8,128)(2,1)} %broadcast_in_dim.4), calls=%async_computation | async-start | bytes 1048576 | tf_op jit(solution)/shard_map/all_to_all | solution.py:211
  32.0 12.8 %collective-permute-start.2 = (bf16[8,128,128]{2,1,0:T(8,128)(2,1)S(1)}, bf16[8,128,128]{2,1,0:T(8,128)(2,1)S(1)}, u32[]{:S(2)}, u32[]{:S(2)}) collective-permute-start(bf16[8,128,128]{2,1,0:T(8,128)(2,1)S(1)} %collective-permute-done.f1), channel_id=1, source_target_pairs={{0,64},{64,128},{128,192},{192,256},{256,320},{320,384},{384,448},... | collective-permute-start | bytes 786440 | tf_op jit(solution)/shard_map/ppermute | solution.py:206
  35.2 10.2 %collective-permute-start.3 = (bf16[8,128,128]{2,1,0:T(8,128)(2,1)S(1)}, bf16[8,128,128]{2,1,0:T(8,128)(2,1)S(1)}, u32[]{:S(2)}, u32[]{:S(2)}) collective-permute-start(bf16[8,128,128]{2,1,0:T(8,128)(2,1)S(1)} %collective-permute-done.1.b1), channel_id=1, source_target_pairs={{0,448},{64,0},{128,64},{192,128},{256,192},{320,256},{384,320},{4... | collective-permute-start | bytes 786440 | tf_op jit(solution)/shard_map/ppermute | solution.py:206
  44.8 16.3 %copy-start.8 = (bf16[8,128,128]{2,1,0:T(8,128)(2,1)}, bf16[8,128,128]{2,1,0:T(8,128)(2,1)S(1)}, u32[]{:S(2)}) copy-start(bf16[8,128,128]{2,1,0:T(8,128)(2,1)S(1)} %collective-permute-done.2.f2) | copy-start | bytes 786436
  45.4 15.7 %copy-start.9 = (bf16[8,128,128]{2,1,0:T(8,128)(2,1)}, bf16[8,128,128]{2,1,0:T(8,128)(2,1)S(1)}, u32[]{:S(2)}) copy-start(bf16[8,128,128]{2,1,0:T(8,128)(2,1)S(1)} %collective-permute-done.3.b2) | copy-start | bytes 786436
  45.4 9.9 %collective-permute-start.6 = (bf16[8,128,128]{2,1,0:T(8,128)(2,1)S(1)}, bf16[8,128,128]{2,1,0:T(8,128)(2,1)S(1)}, u32[]{:S(2)}, u32[]{:S(2)}) collective-permute-start(bf16[8,128,128]{2,1,0:T(8,128)(2,1)S(1)} %collective-permute-done.3.b2), channel_id=1, source_target_pairs={{0,448},{64,0},{128,64},{192,128},{256,192},{320,256},{384,320},{4... | collective-permute-start | bytes 786440 | tf_op jit(solution)/shard_map/ppermute | solution.py:206
  49.5 9.7 %collective-permute-start.4 = (bf16[8,128,128]{2,1,0:T(8,128)(2,1)S(1)}, bf16[8,128,128]{2,1,0:T(8,128)(2,1)S(1)}, u32[]{:S(2)}, u32[]{:S(2)}) collective-permute-start(bf16[8,128,128]{2,1,0:T(8,128)(2,1)S(1)} %collective-permute-done.2.f2), channel_id=1, source_target_pairs={{0,64},{64,128},{128,192},{192,256},{256,320},{320,384},{384,448},... | collective-permute-start | bytes 786440 | tf_op jit(solution)/shard_map/ppermute | solution.py:206
  55.4 5.8 %copy-start.2 = (bf16[8,128,128]{2,1,0:T(8,128)(2,1)}, bf16[8,128,128]{2,1,0:T(8,128)(2,1)S(1)}, u32[]{:S(2)}) copy-start(bf16[8,128,128]{2,1,0:T(8,128)(2,1)S(1)} %collective-permute-done.6.b3) | copy-start | bytes 786436
  55.4 9.8 %collective-permute-start.7 = (bf16[4,128,128]{2,1,0:T(8,128)(2,1)S(1)}, bf16[4,128,128]{2,1,0:T(8,128)(2,1)S(1)}, u32[]{:S(2)}, u32[]{:S(2)}) collective-permute-start(bf16[4,128,128]{2,1,0:T(8,128)(2,1)S(1)} %slice.9), channel_id=1, source_target_pairs={{0,448},{64,0},{128,64},{192,128},{256,192},{320,256},{384,320},{4... | collective-permute-start | bytes 393224 | tf_op jit(solution)/shard_map/ppermute | solution.py:206
  59.2 2.0 %copy-start.3 = (bf16[8,128,128]{2,1,0:T(8,128)(2,1)}, bf16[8,128,128]{2,1,0:T(8,128)(2,1)S(1)}, u32[]{:S(2)}) copy-start(bf16[8,128,128]{2,1,0:T(8,128)(2,1)S(1)} %collective-permute-done.4.f3) | copy-start | bytes 786436
  59.2 6.9 %collective-permute-start.5 = (bf16[4,128,128]{2,1,0:T(8,128)(2,1)S(1)}, bf16[4,128,128]{2,1,0:T(8,128)(2,1)S(1)}, u32[]{:S(2)}, u32[]{:S(2)}) collective-permute-start(bf16[4,128,128]{2,1,0:T(8,128)(2,1)S(1)} %slice.8), channel_id=1, source_target_pairs={{0,64},{64,128},{128,192},{192,256},{256,320},{320,384},{384,448},... | collective-permute-start | bytes 393224 | tf_op jit(solution)/shard_map/ppermute | solution.py:206
  65.2 0.9 copy-start.5
  66.1 0.7 copy-start.12
  66.1 0.8 copy-start
  72.5 7.2 %collective-permute-start.8 = (f32[32,16,256]{2,1,0:T(8,128)}, f32[32,16,256]{2,1,0:T(8,128)S(1)}, u32[]{:S(2)}, u32[]{:S(2)}) collective-permute-start(f32[32,16,256]{2,1,0:T(8,128)} %get-tuple-element.29), channel_id=1, source_target_pairs={{0,1},{1,0},{2,3},{3,2},{4,5},{5,4},{6,7},{7,6},{8,9},{9,8},{10,11... | collective-permute-start | bytes 1572872 | tf_op jit(solution)/shard_map/ppermute | solution.py:206
  106.8 22.0 %copy-start.11 = (f32[16,256]{1,0:T(8,128)}, f32[16,256]{1,0:T(8,128)S(1)}, u32[]{:S(2)}) copy-start(f32[16,256]{1,0:T(8,128)S(1)} %reduce_sum.18.own_ref) | copy-start | bytes 49156
  122.0 6.8 %copy-start.1 = (bf16[32,16,256]{2,1,0:T(8,128)(2,1)}, bf16[32,16,256]{2,1,0:T(8,128)(2,1)S(1)}, u32[]{:S(2)}) copy-start(bf16[32,16,256]{2,1,0:T(8,128)(2,1)S(1)} %all_to_all.21.mine_ref) | copy-start | bytes 786436
  122.0 6.8 %collective-permute-start.9 = (bf16[32,16,256]{2,1,0:T(8,128)(2,1)S(1)}, bf16[32,16,256]{2,1,0:T(8,128)(2,1)S(1)}, u32[]{:S(2)}, u32[]{:S(2)}) collective-permute-start(bf16[32,16,256]{2,1,0:T(8,128)(2,1)S(1)} %all_to_all.21.mine_ref), channel_id=1, source_target_pairs={{0,1},{1,0},{2,3},{3,2},{4,5},{5,4},{6,7},{7,6},{8,9},{9,8},{10,11... | collective-permute-start | bytes 786440 | tf_op jit(solution)/shard_map/ppermute | solution.py:206
  128.8 0.7 copy-start.10

commit v3 on v2

--- a/solution.py
+++ b/solution.py
@@ -116,15 +116,15 @@
 
 
 def forward_body(
-    place_ref, f4, b4, early_ref, pivot_ref, right_ref, probe_ref, tall_ref, tright_ref,
-    sketch_ref, keep_ref, send_ref, pair_ref, part,
+    place_ref, f4, b4, early_ref, pivot_ref, probe_ref, sketch_ref, right_ref, tright_ref,
+    keep_ref, send_ref, pair_ref, core_ref, part,
 ):
     group, live, groups, core = place_ref[0], place_ref[1], place_ref[2], place_ref[3]
     slots, n, half = right_ref.shape[0], f4.shape[1], keep_ref.shape[0]
     at = pl.multiple_of(lax.rem(group + groups // 2, groups) * n, n)
     mixed = []
     for k in range(slots):
-        pair = early_ref[k] + dot(f4[k], right_ref[k], 0, 0)
+        pair = early_ref[k] + dot(f4[k], right_ref[k, pl.ds(at, n), :], 0, 0)
         pair_ref[k] = pair
         row = []
         for t in range(2):
@@ -133,57 +133,76 @@
             row.append(jnp.where(k < live, -value, 0.0).astype(LOW))
         mixed.append(jnp.concatenate(row, 1))
     mixed = jnp.concatenate(mixed, 0)
-    update = dot(pivot_ref[...], mixed, 1, 0)
-    for t in range(2):
-        cols = slice(128 * t, 128 * t + 128)
-        core_part = dot(tright_ref[:, cols], sketch_ref[:, cols], 0, 0).astype(LOW)
-        part[:, cols] = update[:, cols] + dot(tall_ref[:, cols], core_part, 1, 0)
+    part[...] = dot(pivot_ref[...], mixed, 1, 0)
     last = jnp.concatenate([b4[k] for k in range(slots)], 1)
-    part[pl.ds(at, n), :] += dot(last, mixed, 1, 0)
+    part[pl.ds(at, n), :] = dot(last, mixed, 1, 0)
+    cores = [
+        dot(tright_ref[:, 128 * t : 128 * t + 128], sketch_ref[:, 128 * t : 128 * t + 128], 0, 0)
+        for t in range(2)
+    ]
+    core_ref[...] = jnp.concatenate(halves(jnp.concatenate(cores, 0).reshape(half, 8, 128)), 1)
     whole = part[...].reshape(half, 2, 16, part.shape[1])
     keep_ref[...] = jnp.where(core == 0, whole[:, 0], whole[:, 1])
     send_ref[...] = jnp.where(core == 0, whole[:, 1], whole[:, 0])
 
 
+def merge_body(keep_ref, come_ref, core_ref, out_ref):
+    width = keep_ref.shape[2]
+    out_ref[:, :, :width] = (keep_ref[...] + come_ref[...]).astype(LOW)
+    out_ref[:, :, width:] = core_ref[...]
+
+
+def own_body(pieces_ref, tleft_ref, sum_ref, out_ref):
+    width = sum_ref.shape[1]
+    total = jnp.sum(pieces_ref[...].astype(FULL), 0)
+    sum_ref[...] = total[:, :width]
+    core = jnp.concatenate(halves(total[:8, width:] + total[8:, width:]), 0)
+    row = jnp.concatenate([total[:, :width].astype(LOW), tleft_ref[...], core], 1)
+    out_ref[...] = jnp.broadcast_to(row[None], out_ref.shape)
+
+
 def backward_body(
-    place_ref, mine_ref, other_ref, own_ref, tright_ref, b4,
-    pivot_any, pair_any, left_any, tall_any,
-    basis_ref, term_ref, direct_ref,
-    whole, pivot_ref, pair_ref, left_ref, tall_ref, sems,
+    place_ref, mine_ref, other_ref, own_ref, b4, pivot_ref, pair_ref, tleft_ref, tright_ref,
+    left_ref, basis_ref, term_ref, direct_ref, turn_high, turn_low, tall,
 ):
     group, live, groups, core = place_ref[0], place_ref[1], place_ref[2], place_ref[3]
-    copies = [
-        pltpu.make_async_copy(source, target, sems.at[i])
-        for i, (source, target) in enumerate(
-            ((pivot_any, pivot_ref), (tall_any, tall_ref), (pair_any, pair_ref), (left_any, left_ref))
-        )
-    ]
-    for c in copies:
-        c.start()
-    slots, rows, n = left_ref.shape[0], whole.shape[0], b4.shape[1]
-    mine, other = mine_ref[...], other_ref[...]
-    even, odd = jnp.where(core == 0, mine, other), jnp.where(core == 0, other, mine)
-    whole[...] = jnp.concatenate([even[:, None], odd[:, None]], 1).reshape(rows, whole.shape[1])
-    turned, grams = [], []
-    for t in range(2):
-        s = whole[:, 128 * t : 128 * t + 128]
-        turned.append(s.T)
-        grams.append(dot(turned[t], s, 1, 0) / rows)
-    for c in copies:
-        c.wait()
+    slots, rows, n = left_ref.shape[0], tall.shape[0], b4.shape[1]
+    width = own_ref.shape[1]
+
+    def ordered(cols):
+        mine, other = mine_ref[:, :, cols], other_ref[:, :, cols]
+        even, odd = jnp.where(core == 0, mine, other), jnp.where(core == 0, other, mine)
+        return jnp.concatenate([even[:, None], odd[:, None]], 1).reshape(rows, -1)
+
+    tall[...] = ordered(slice(width, 2 * width))
+    parts = mine_ref[:, :, 2 * width :].astype(FULL) + other_ref[:, :, 2 * width :].astype(FULL)
+    cores = (parts[:, :8] + parts[:, 8:]).reshape(2 * 128, 128).astype(LOW)
     at = pl.multiple_of(lax.rem(group + groups // 2, groups) * n, n)
     last = jnp.concatenate([b4[k] for k in range(slots)], 1)
-    seen, seen_target = [], []
+    whole, own, grams, seen, seen_target = [], [], [], [], []
     for t in range(2):
         cols = slice(128 * t, 128 * t + 128)
-        seen.append(
-            dot(turned[t], pivot_ref[...], 1, 0) + dot(whole[pl.ds(at, n), cols], last, 0, 0)
-        )
-        seen_target.append(dot(turned[t], tall_ref[:, cols], 1, 0))
+        target_core = cores[cols]
+        s = ordered(cols).astype(FULL) + dot(tall[:, cols], target_core, 1, 0)
+        own.append(own_ref[:, cols] + dot(tleft_ref[:, cols], target_core, 1, 0))
+        turned = s.T
+        high, low = halves(turned)
+        grams.append(dot(high, s.astype(LOW), 1, 0) / rows)
+        turn_high[t] = high
+        turn_low[t] = low
+    for t in range(2):
+        cols = slice(128 * t, 128 * t + 128)
+        both = jnp.concatenate([turn_high[t], turn_low[t]], 0)
+        product = dot(both, pivot_ref[...], 1, 0)
+        tail = jnp.concatenate([turn_high[t, :, pl.ds(at, n)], turn_low[t, :, pl.ds(at, n)]], 0)
+        product = product + dot(tail, last, 1, 0)
+        seen.append(product[:128] + product[128:])
+        product = dot(both, tall[:, cols], 1, 0)
+        seen_target.append(product[:128] + product[128:])
     inverse = inverse_factors(grams)
     for t in range(2):
         cols = slice(128 * t, 128 * t + 128)
-        basis_ref[:, cols] = fine_dot(own_ref[:, cols], inverse[t], 1, 1)
+        basis_ref[:, cols] = fine_dot(own[t], inverse[t], 1, 1)
         back = fine_dot(inverse[t], seen[t], 1, 0)
         total = None
         for k in range(slots):
@@ -197,8 +216,7 @@
 
 
 SMEM = pl.BlockSpec(memory_space=pltpu.SMEM)
-WHOLE = pl.BlockSpec()
-PLACED = pl.BlockSpec(memory_space=pl.ANY)
+VMEM = pl.BlockSpec(memory_space=pltpu.VMEM)
 
 
 def shift(x, axis, by):
@@ -206,22 +224,30 @@
     return lax.ppermute(x, axis, [(i, (i + by) % n) for i in range(n)])
 
 
-def to_all(x, axes):
-    n = lax.axis_size(axes)
-    return lax.all_to_all(jnp.broadcast_to(x[None], (n, *x.shape)), axes, 0, 0, tiled=True)
-
-
-def whole_block(x):
-    return pl.BlockSpec(x.shape, lambda i, place: (0,) * x.ndim)
+def near(x):
+    return pltpu.with_memory_space_constraint(x, pltpu.VMEM)
+
+
+def kernel(body, name, outs, scratch, place, *arrays, given=()):
+    first = () if place is None else (place,)
+    return pl.pallas_call(
+        body,
+        in_specs=[SMEM] * len(first) + [VMEM] * (len(arrays) + len(given)),
+        out_specs=[VMEM] * len(outs),
+        out_shape=[pltpu.VMEM(*o) for o in outs],
+        scratch_shapes=[pltpu.VMEM(*o) for o in scratch],
+        name=name,
+        compiler_params=pltpu.CompilerParams(vmem_limit_bytes=24 << 20),
+    )(*first, *[near(x) for x in arrays], *given)
 
 
 def shards(
     row_left, row_right, col_left, col_right, sketch_cols, target_left, target_right, live_counts
 ):
     slots, rows, width = col_left.shape
-    block = target_left.shape[0]
-    groups, chunk = lax.axis_size("grp"), row_left.shape[1]
-    n, far = lax.axis_size(INNER), INNER[:2]
+    block, factors = target_left.shape[0], slots * 128
+    n, far, groups = lax.axis_size(INNER), INNER[:2], lax.axis_size("grp")
+    half = n // 2
     place = jnp.stack(
         [lax.axis_index("grp"), live_counts[0], jnp.int32(groups), lax.axis_index(INNER[2])]
     ).astype(jnp.int32)
@@ -230,13 +256,14 @@
     for step in range(3):
         up, down = shift(up, "grp", 1), shift(down, "grp", -1)
         if step == 0:
-            up, down, target_left = lax.optimization_barrier((up, down, target_left))
-            all_left = to_all(target_left, INNER).reshape(rows, width)
-            probe = pl.pallas_call(
+            (probe,) = kernel(
                 probe_body,
-                out_shape=jax.ShapeDtypeStruct((slots, 2, 128, 128), FULL),
-                name="probe",
-            )(col_left, sketch_cols)
+                "probe",
+                [((slots, 2, 128, 128), FULL)],
+                [],
+                None,
+                given=(col_left, sketch_cols),
+            )
             own_sketch = lax.dynamic_slice_in_dim(
                 sketch_cols, lax.axis_index(INNER) * block, block, 0
             )
@@ -246,61 +273,59 @@
             )
         chunks += [up, down]
     last_up, last_down = shift(up[:slots], "grp", 1), shift(down[slots:], "grp", -1)
-    early, pivot = pl.pallas_call(
+    early, pivot = kernel(
         early_body,
-        in_specs=[SMEM] + [WHOLE] * 8,
-        out_shape=(
-            jax.ShapeDtypeStruct((slots, 128, width), FULL),
-            jax.ShapeDtypeStruct((rows, slots * 128), LOW),
-        ),
-        scratch_shapes=[pltpu.VMEM((rows, slots * 128), LOW)],
-        name="early",
-    )(place, *chunks, col_right)
-    ins = (last_up, last_down, early, pivot, col_right, probe, all_left, target_right, own_sketch)
-    specs = [whole_block(x) for x in ins]
-    specs[4] = pl.BlockSpec(
-        (slots, chunk, width),
-        lambda i, place: (0, lax.rem(place[0] + place[2] // 2, place[2]), 0),
-    )
-    outs = (
-        jax.ShapeDtypeStruct((n // 2, block, width), FULL),
-        jax.ShapeDtypeStruct((n // 2, block, width), FULL),
-        jax.ShapeDtypeStruct((slots, 128, width), FULL),
-    )
-    keep, send, pair = pl.pallas_call(
+        "early",
+        [((slots, 128, width), FULL), ((rows, factors), LOW)],
+        [((rows, factors), LOW)],
+        place,
+        *chunks,
+        given=(col_right,),
+    )
+    piece = (half, block, width)
+    keep, send, pair, core = kernel(
         forward_body,
-        grid_spec=pltpu.PrefetchScalarGridSpec(
-            num_scalar_prefetch=1,
-            grid=(1,),
-            in_specs=specs,
-            out_specs=[whole_block(x) for x in outs],
-            scratch_shapes=[pltpu.VMEM((rows, width), FULL)],
-        ),
-        out_shape=outs,
-        name="forward",
-    )(place, *ins)
-    summed = keep + shift(send, INNER[2], 1)
-    own_sum = jnp.sum(lax.all_to_all(summed, far, 0, 0, tiled=True), 0)
-    mine = to_all(own_sum.astype(LOW), far)
+        "forward",
+        [(piece, FULL), (piece, FULL), ((slots, 128, width), FULL), ((half, block, 128), LOW)],
+        [((rows, width), FULL)],
+        place,
+        last_up,
+        last_down,
+        early,
+        pivot,
+        probe,
+        own_sketch,
+        given=(col_right, target_right),
+    )
+    (merged,) = kernel(
+        merge_body, "merge", [((half, block, width + 128), LOW)], [], None,
+        keep, shift(send, INNER[2], 1), core,
+    )
+    own_sum, mine = kernel(
+        own_body,
+        "own",
+        [((block, width), FULL), ((half, block, 2 * width + 128), LOW)],
+        [],
+        None,
+        lax.all_to_all(merged, far, 0, 0, tiled=True),
+        given=(target_left,),
+    )
+    mine = lax.all_to_all(mine, far, 0, 0, tiled=True)
     other = shift(mine, INNER[2], 1)
-    basis, term, direct = pl.pallas_call(
+    basis, term, direct = kernel(
         backward_body,
-        in_specs=[SMEM] + [WHOLE] * 5 + [PLACED] * 4,
-        out_shape=(
-            jax.ShapeDtypeStruct((block, width), FULL),
-            jax.ShapeDtypeStruct((rows, width), LOW),
-            jax.ShapeDtypeStruct((block, width), FULL),
-        ),
-        scratch_shapes=[
-            pltpu.VMEM((rows, width), LOW),
-            pltpu.VMEM(pivot.shape, LOW),
-            pltpu.VMEM(pair.shape, FULL),
-            pltpu.VMEM(col_left.shape, LOW),
-            pltpu.VMEM(all_left.shape, LOW),
-            pltpu.SemaphoreType.DMA((4,)),
-        ],
-        name="backward",
-    )(place, mine, other, own_sum, target_right, last_down, pivot, pair, col_left, all_left)
+        "backward",
+        [((block, width), FULL), ((rows, width), LOW), ((block, width), FULL)],
+        [((2, 128, rows), LOW), ((2, 128, rows), LOW), ((rows, width), LOW)],
+        place,
+        mine,
+        other,
+        own_sum,
+        last_down,
+        pivot,
+        pair,
+        given=(target_left, target_right, col_left),
+    )
     pieces = lax.all_to_all(term.reshape(n, block, width), INNER, 0, 0, tiled=True)
     coeffs = (jnp.sum(pieces.astype(FULL), 0) + direct) / rows
     return basis, coeffs

time: 165 us -> 145 us (0.88)
  the two profiles are of different devices: /device:TPU:1 before, /device:TPU:56 now
where the time goes in v3:
time: 145 us; the launch traced here: 143 us
  blocking collectives  52.2 us (36%)
  starting transfers between devices  40.4 us (28%)
  waiting for transfers between devices  30.3 us (21%)
  Pallas kernels  13 us (9%)
  local copies, waits for them, and re-layouts  5.27 us (4%)
  between operations  1.5 us (1%)
    ppermute x10, starting transfers between devices, shift(): return lax.ppermute(x, axis, [(i, (i + by) % n) for i in range(n)])  34.7 us
    all_to_all x1, blocking collectives, shards(): lax.all_to_all(merged, far, 0, 0, tiled=True)  28.6 us
    all_to_all x1, blocking collectives, shards(): mine = lax.all_to_all(mine, far, 0, 0, tiled=True)  23.6 us
    all_to_all x1, waiting for transfers between devices, shards(): lax.all_to_all(term.reshape(n, block, width), INNER, 0, 0, tiled=True)  17 us
    ppermute x10, waiting for transfers between devices, shift(): return lax.ppermute(x, axis, [(i, (i + by) % n) for i in range(n)])  13.3 us
    pallas_call x6, Pallas kernels, kernel(): pl.pallas_call(body, in_specs=[SMEM] * len(first) + [VMEM] * (len(arrays)...  13 us
    all_to_all x1, starting transfers between devices, shards(): lax.all_to_all(term.reshape(n, block, width), INNER, 0, 0, tiled=True)  5.62 us
    unnamed x14, local copies, waits for them, and re-layouts  4.32 us
  transfers between devices with their start and end apart: 11, of which 7 were waited for; matrix products, arithmetic and copies ran while one was open for 0% of the time, Pallas kernels for 2%

profile of v3, /device:TPU:56, one launch (start us, length us, event | category | flops | bytes accessed | tf_op | source)
XLA Modules:
  0.0 143.3 jit_solution(14415423470002330617)
XLA Ops:
  0.6 1.1 constant_dynamic-update-slice_fusion.1
  2.6 3.3 %collective-permute-start.2 = (bf16[8,128,128]{2,1,0:T(8,128)(2,1)S(1)}, bf16[8,128,128]{2,1,0:T(8,128)(2,1)S(1)}, u32[]{:S(2)}, u32[]{:S(2)}) collective-permute-start(bf16[8,128,128]{2,1,0:T(8,128)(2,1)S(1)} %constant_dynamic-update-slice_fusion.own), channel_id=1, source_target_pairs={{0,448},{64,0},{128,64},{192,128},{256,192},{320,256},{384,320},{4... | collective-permute-start | bytes 786440 | tf_op jit(solution)/shard_map/ppermute | solution.py:224
  5.9 5.7 %collective-permute-start = (bf16[8,128,128]{2,1,0:T(8,128)(2,1)S(1)}, bf16[8,128,128]{2,1,0:T(8,128)(2,1)S(1)}, u32[]{:S(2)}, u32[]{:S(2)}) collective-permute-start(bf16[8,128,128]{2,1,0:T(8,128)(2,1)S(1)} %constant_dynamic-update-slice_fusion.own), channel_id=1, source_target_pairs={{0,64},{64,128},{128,192},{192,256},{256,320},{320,384},{384,448},... | collective-permute-start | bytes 786440 | tf_op jit(solution)/shard_map/ppermute | solution.py:224
  11.6 2.4 %collective-permute-done.2.b1 = bf16[8,128,128]{2,1,0:T(8,128)(2,1)S(1)} collective-permute-done((bf16[8,128,128]{2,1,0:T(8,128)(2,1)S(1)}, bf16[8,128,128]{2,1,0:T(8,128)(2,1)S(1)}, u32[]{:S(2)}, u32[]{:S(2)}) %collective-permute-start.2) | collective-permute-done | bytes 262176 | tf_op jit(solution)/shard_map/ppermute | solution.py:224
  14.0 1.9 %collective-permute-start.3 = (bf16[8,128,128]{2,1,0:T(8,128)(2,1)S(1)}, bf16[8,128,128]{2,1,0:T(8,128)(2,1)S(1)}, u32[]{:S(2)}, u32[]{:S(2)}) collective-permute-start(bf16[8,128,128]{2,1,0:T(8,128)(2,1)S(1)} %collective-permute-done.2.b1), channel_id=1, source_target_pairs={{0,448},{64,0},{128,64},{192,128},{256,192},{320,256},{384,320},{4... | collective-permute-start | bytes 786440 | tf_op jit(solution)/shard_map/ppermute | solution.py:224
  15.9 5.1 %collective-permute-start.1 = (bf16[8,128,128]{2,1,0:T(8,128)(2,1)S(1)}, bf16[8,128,128]{2,1,0:T(8,128)(2,1)S(1)}, u32[]{:S(2)}, u32[]{:S(2)}) collective-permute-start(bf16[8,128,128]{2,1,0:T(8,128)(2,1)S(1)} %collective-permute-done.f1), channel_id=1, source_target_pairs={{0,64},{64,128},{128,192},{192,256},{256,320},{320,384},{384,448},... | collective-permute-start | bytes 786440 | tf_op jit(solution)/shard_map/ppermute | solution.py:224
  21.7 1.6 %copy-done.1 = bf16[4,1024,256]{2,1,0:T(8,128)(2,1)S(1)} copy-done((bf16[4,1024,256]{2,1,0:T(8,128)(2,1)S(1)}, bf16[4,1024,256]{2,1,0:T(8,128)(2,1)}, u32[]{:S(2)}) %copy-start.1) | copy-done | bytes 2097176
  25.2 5.3 %collective-permute-start.4 = (bf16[8,128,128]{2,1,0:T(8,128)(2,1)S(1)}, bf16[8,128,128]{2,1,0:T(8,128)(2,1)S(1)}, u32[]{:S(2)}, u32[]{:S(2)}) collective-permute-start(bf16[8,128,128]{2,1,0:T(8,128)(2,1)S(1)} %collective-permute-done.1.f2), channel_id=1, source_target_pairs={{0,64},{64,128},{128,192},{192,256},{256,320},{320,384},{384,448},... | collective-permute-start | bytes 786440 | tf_op jit(solution)/shard_map/ppermute | solution.py:224
  30.5 1.9 %collective-permute-start.6 = (bf16[8,128,128]{2,1,0:T(8,128)(2,1)S(1)}, bf16[8,128,128]{2,1,0:T(8,128)(2,1)S(1)}, u32[]{:S(2)}, u32[]{:S(2)}) collective-permute-start(bf16[8,128,128]{2,1,0:T(8,128)(2,1)S(1)} %collective-permute-done.3.b2), channel_id=1, source_target_pairs={{0,448},{64,0},{128,64},{192,128},{256,192},{320,256},{384,320},{4... | collective-permute-start | bytes 786440 | tf_op jit(solution)/shard_map/ppermute | solution.py:224
  32.5 1.9 %collective-permute-done.4.f3 = bf16[8,128,128]{2,1,0:T(8,128)(2,1)S(1)} collective-permute-done((bf16[8,128,128]{2,1,0:T(8,128)(2,1)S(1)}, bf16[8,128,128]{2,1,0:T(8,128)(2,1)S(1)}, u32[]{:S(2)}, u32[]{:S(2)}) %collective-permute-start.4) | collective-permute-done | bytes 262176 | tf_op jit(solution)/shard_map/ppermute | solution.py:224
  34.4 5.7 %collective-permute-start.5 = (bf16[4,128,128]{2,1,0:T(8,128)(2,1)S(1)}, bf16[4,128,128]{2,1,0:T(8,128)(2,1)S(1)}, u32[]{:S(2)}, u32[]{:S(2)}) collective-permute-start(bf16[4,128,128]{2,1,0:T(8,128)(2,1)S(1)} %slice.8), channel_id=1, source_target_pairs={{0,64},{64,128},{128,192},{192,256},{256,320},{320,384},{384,448},... | collective-permute-start | bytes 393224 | tf_op jit(solution)/shard_map/ppermute | solution.py:224
  40.3 1.9 %collective-permute-start.7 = (bf16[4,128,128]{2,1,0:T(8,128)(2,1)S(1)}, bf16[4,128,128]{2,1,0:T(8,128)(2,1)S(1)}, u32[]{:S(2)}, u32[]{:S(2)}) collective-permute-start(bf16[4,128,128]{2,1,0:T(8,128)(2,1)S(1)} %slice.9), channel_id=1, source_target_pairs={{0,448},{64,0},{128,64},{192,128},{256,192},{320,256},{384,320},{4... | collective-permute-start | bytes 393224 | tf_op jit(solution)/shard_map/ppermute | solution.py:224
  42.3 1.4 early.1
  43.7 4.7 %collective-permute-done.7.b4 = bf16[4,128,128]{2,1,0:T(8,128)(2,1)S(1)} collective-permute-done((bf16[4,128,128]{2,1,0:T(8,128)(2,1)S(1)}, bf16[4,128,128]{2,1,0:T(8,128)(2,1)S(1)}, u32[]{:S(2)}, u32[]{:S(2)}) %collective-permute-start.7) | collective-permute-done | bytes 131104 | tf_op jit(solution)/shard_map/ppermute | solution.py:224
  48.4 2.0 %forward.1 = (f32[32,16,256]{2,1,0:T(8,128)S(1)}, f32[32,16,256]{2,1,0:T(8,128)S(1)}, f32[4,128,256]{2,1,0:T(8,128)S(1)}, bf16[32,16,128]{2,1,0:T(8,128)(2,1)S(1)}) custom-call(s32[4]{0:T(128)S(1)} %pad_add_fusion.place_ref, bf16[4,128,128]{2,1,0:T(8,128)(2,1)S(1)} %collective-permute-done.5.f4, bf16[4,128,128]{2,1,0:T(8,128)(2,1)S(1)} %collective-permute-done.7.b4, ...), custom_call_target="tpu_custom_call" | custom-call | tf_op jit(solution)/shard_map/forward/pallas_call | solution.py:233
  50.5 2.1 %collective-permute-start.8 = (f32[32,16,256]{2,1,0:T(8,128)S(1)}, f32[32,16,256]{2,1,0:T(8,128)S(1)}, u32[]{:S(2)}, u32[]{:S(2)}) collective-permute-start(f32[32,16,256]{2,1,0:T(8,128)S(1)} %get-tuple-element.26), channel_id=1, source_target_pairs={{0,1},{1,0},{2,3},{3,2},{4,5},{5,4},{6,7},{7,6},{8,9},{9,8},{10,11... | collective-permute-start | bytes 1572872 | tf_op jit(solution)/shard_map/ppermute | solution.py:224
  52.5 1.9 %collective-permute-done.8.come_ref = f32[32,16,256]{2,1,0:T(8,128)S(1)} collective-permute-done((f32[32,16,256]{2,1,0:T(8,128)S(1)}, f32[32,16,256]{2,1,0:T(8,128)S(1)}, u32[]{:S(2)}, u32[]{:S(2)}) %collective-permute-start.8) | collective-permute-done | bytes 524320 | tf_op jit(solution)/shard_map/ppermute | solution.py:224
  54.5 28.6 %all_to_all.15.pieces_ref = bf16[32,16,384]{2,1,0:T(8,128)(2,1)S(1)} all-to-all(bf16[32,16,384]{2,1,0:T(8,128)(2,1)S(1)} %merge.1), channel_id=1, replica_groups=mesh['grp'=8,'inner_0'=8,'inner_1'=4,'inner_2'=2] {'inner_0','inner_1'}, dimensions={0} | all-to-all | bytes 786432 | tf_op jit(solution)/shard_map/all_to_all | solution.py:310
  83.2 23.6 %all_to_all.16.mine_ref = bf16[32,16,640]{2,1,0:T(8,128)(2,1)S(1)} all-to-all(bf16[32,16,640]{2,1,0:T(8,128)(2,1)S(1)} %get-tuple-element.28), channel_id=1, replica_groups=mesh['grp'=8,'inner_0'=8,'inner_1'=4,'inner_2'=2] {'inner_0','inner_1'}, dimensions={0} | all-to-all | bytes 1310720 | tf_op jit(solution)/shard_map/all_to_all | solution.py:313
  106.8 1.9 %collective-permute-start.9 = (bf16[32,16,640]{2,1,0:T(8,128)(2,1)S(1)}, bf16[32,16,640]{2,1,0:T(8,128)(2,1)S(1)}, u32[]{:S(2)}, u32[]{:S(2)}) collective-permute-start(bf16[32,16,640]{2,1,0:T(8,128)(2,1)S(1)} %all_to_all.16.mine_ref), channel_id=1, source_target_pairs={{0,1},{1,0},{2,3},{3,2},{4,5},{5,4},{6,7},{7,6},{8,9},{9,8},{10,11... | collective-permute-start | bytes 1966088 | tf_op jit(solution)/shard_map/ppermute | solution.py:224
  108.7 2.1 %collective-permute-done.9.other_ref = bf16[32,16,640]{2,1,0:T(8,128)(2,1)S(1)} collective-permute-done((bf16[32,16,640]{2,1,0:T(8,128)(2,1)S(1)}, bf16[32,16,640]{2,1,0:T(8,128)(2,1)S(1)}, u32[]{:S(2)}, u32[]{:S(2)}) %collective-permute-start.9) | collective-permute-done | bytes 655392 | tf_op jit(solution)/shard_map/ppermute | solution.py:224
  110.8 8.6 %backward.1 = (f32[16,256]{1,0:T(8,128)S(1)}, bf16[1024,256]{1,0:T(8,128)(2,1)}, f32[16,256]{1,0:T(8,128)S(1)}) custom-call(s32[4]{0:T(128)S(1)} %pad_add_fusion.place_ref, bf16[32,16,640]{2,1,0:T(8,128)(2,1)S(1)} %all_to_all.16.mine_ref, bf16[32,16,640]{2,1,0:T(8,128)(2,1)S(1)} %collective-permute-done.9.other_ref, ...), custom_call_target="tpu_custom_call" | custom-call | tf_op jit(solution)/shard_map/backward/pallas_call | solution.py:233
  119.4 5.6 %all-to-all-start.2 = ((bf16[64,16,256]{2,1,0:T(8,128)(2,1)}), bf16[64,16,256]{2,1,0:T(8,128)(2,1)S(1)}, u32[]{:S(2)}, u32[]{:S(2)}) async-start(bf16[64,16,256]{2,1,0:T(8,128)(2,1)} %bitcast.2), calls=%async_computation.2 | async-start | bytes 1048576 | tf_op jit(solution)/shard_map/all_to_all | solution.py:329
  125.6 17.0 %all-to-all-done.2 = bf16[64,16,256]{2,1,0:T(8,128)(2,1)S(1)} async-done(((bf16[64,16,256]{2,1,0:T(8,128)(2,1)}), bf16[64,16,256]{2,1,0:T(8,128)(2,1)S(1)}, u32[]{:S(2)}, u32[]{:S(2)}) %all-to-all-start.2) | async-done | bytes 524320 | tf_op jit(solution)/shard_map/all_to_all | solution.py:329
  (27 shorter events, 4.6 us)
Async XLA Ops:
  0.6 41.6 %copy-start = (bf16[4,1024,256]{2,1,0:T(8,128)(2,1)S(1)}, bf16[4,1024,256]{2,1,0:T(8,128)(2,1)}, u32[]{:S(2)}) copy-start(bf16[4,1024,256]{2,1,0:T(8,128)(2,1)} %right_ref.3) | copy-start | bytes 6291460
  2.6 11.4 %collective-permute-start.2 = (bf16[8,128,128]{2,1,0:T(8,128)(2,1)S(1)}, bf16[8,128,128]{2,1,0:T(8,128)(2,1)S(1)}, u32[]{:S(2)}, u32[]{:S(2)}) collective-permute-start(bf16[8,128,128]{2,1,0:T(8,128)(2,1)S(1)} %constant_dynamic-update-slice_fusion.own), channel_id=1, source_target_pairs={{0,448},{64,0},{128,64},{192,128},{256,192},{320,256},{384,320},{4... | collective-permute-start | bytes 786440 | tf_op jit(solution)/shard_map/ppermute | solution.py:224
  5.9 10.0 %collective-permute-start = (bf16[8,128,128]{2,1,0:T(8,128)(2,1)S(1)}, bf16[8,128,128]{2,1,0:T(8,128)(2,1)S(1)}, u32[]{:S(2)}, u32[]{:S(2)}) collective-permute-start(bf16[8,128,128]{2,1,0:T(8,128)(2,1)S(1)} %constant_dynamic-update-slice_fusion.own), channel_id=1, source_target_pairs={{0,64},{64,128},{128,192},{192,256},{256,320},{320,384},{384,448},... | collective-permute-start | bytes 786440 | tf_op jit(solution)/shard_map/ppermute | solution.py:224
  14.0 11.2 %collective-permute-start.3 = (bf16[8,128,128]{2,1,0:T(8,128)(2,1)S(1)}, bf16[8,128,128]{2,1,0:T(8,128)(2,1)S(1)}, u32[]{:S(2)}, u32[]{:S(2)}) collective-permute-start(bf16[8,128,128]{2,1,0:T(8,128)(2,1)S(1)} %collective-permute-done.2.b1), channel_id=1, source_target_pairs={{0,448},{64,0},{128,64},{192,128},{256,192},{320,256},{384,320},{4... | collective-permute-start | bytes 786440 | tf_op jit(solution)/shard_map/ppermute | solution.py:224
  15.9 9.3 %collective-permute-start.1 = (bf16[8,128,128]{2,1,0:T(8,128)(2,1)S(1)}, bf16[8,128,128]{2,1,0:T(8,128)(2,1)S(1)}, u32[]{:S(2)}, u32[]{:S(2)}) collective-permute-start(bf16[8,128,128]{2,1,0:T(8,128)(2,1)S(1)} %collective-permute-done.f1), channel_id=1, source_target_pairs={{0,64},{64,128},{128,192},{192,256},{256,320},{320,384},{384,448},... | collective-permute-start | bytes 786440 | tf_op jit(solution)/shard_map/ppermute | solution.py:224
  21.7 1.6 %copy-start.1 = (bf16[4,1024,256]{2,1,0:T(8,128)(2,1)S(1)}, bf16[4,1024,256]{2,1,0:T(8,128)(2,1)}, u32[]{:S(2)}) copy-start(bf16[4,1024,256]{2,1,0:T(8,128)(2,1)} %left_ref.3) | copy-start | bytes 6291460
  23.3 1.0 copy-start.3
  25.2 9.2 %collective-permute-start.4 = (bf16[8,128,128]{2,1,0:T(8,128)(2,1)S(1)}, bf16[8,128,128]{2,1,0:T(8,128)(2,1)S(1)}, u32[]{:S(2)}, u32[]{:S(2)}) collective-permute-start(bf16[8,128,128]{2,1,0:T(8,128)(2,1)S(1)} %collective-permute-done.1.f2), channel_id=1, source_target_pairs={{0,64},{64,128},{128,192},{192,256},{256,320},{320,384},{384,448},... | collective-permute-start | bytes 786440 | tf_op jit(solution)/shard_map/ppermute | solution.py:224
  30.5 9.8 %collective-permute-start.6 = (bf16[8,128,128]{2,1,0:T(8,128)(2,1)S(1)}, bf16[8,128,128]{2,1,0:T(8,128)(2,1)S(1)}, u32[]{:S(2)}, u32[]{:S(2)}) collective-permute-start(bf16[8,128,128]{2,1,0:T(8,128)(2,1)S(1)} %collective-permute-done.3.b2), channel_id=1, source_target_pairs={{0,448},{64,0},{128,64},{192,128},{256,192},{320,256},{384,320},{4... | collective-permute-start | bytes 786440 | tf_op jit(solution)/shard_map/ppermute | solution.py:224
  34.4 14.0 %copy-start.4 = (bf16[16,256]{1,0:T(8,128)(2,1)S(1)}, bf16[16,256]{1,0:T(8,128)(2,1)}, u32[]{:S(2)}) copy-start(bf16[16,256]{1,0:T(8,128)(2,1)} %tright_ref.3) | copy-start | bytes 24580
  34.4 9.2 %collective-permute-start.5 = (bf16[4,128,128]{2,1,0:T(8,128)(2,1)S(1)}, bf16[4,128,128]{2,1,0:T(8,128)(2,1)S(1)}, u32[]{:S(2)}, u32[]{:S(2)}) collective-permute-start(bf16[4,128,128]{2,1,0:T(8,128)(2,1)S(1)} %slice.8), channel_id=1, source_target_pairs={{0,64},{64,128},{128,192},{192,256},{256,320},{320,384},{384,448},... | collective-permute-start | bytes 393224 | tf_op jit(solution)/shard_map/ppermute | solution.py:224
  40.3 8.1 %collective-permute-start.7 = (bf16[4,128,128]{2,1,0:T(8,128)(2,1)S(1)}, bf16[4,128,128]{2,1,0:T(8,128)(2,1)S(1)}, u32[]{:S(2)}, u32[]{:S(2)}) collective-permute-start(bf16[4,128,128]{2,1,0:T(8,128)(2,1)S(1)} %slice.9), channel_id=1, source_target_pairs={{0,448},{64,0},{128,64},{192,128},{256,192},{320,256},{384,320},{4... | collective-permute-start | bytes 393224 | tf_op jit(solution)/shard_map/ppermute | solution.py:224
  50.5 32.6 %copy-start.5 = (bf16[16,256]{1,0:T(8,128)(2,1)S(1)}, bf16[16,256]{1,0:T(8,128)(2,1)}, u32[]{:S(2)}) copy-start(bf16[16,256]{1,0:T(8,128)(2,1)} %tleft_ref.3) | copy-start | bytes 24580
  50.5 60.3 %copy-start.2 = (bf16[4,1024,256]{2,1,0:T(8,128)(2,1)S(1)}, bf16[4,1024,256]{2,1,0:T(8,128)(2,1)}, u32[]{:S(2)}) copy-start(bf16[4,1024,256]{2,1,0:T(8,128)(2,1)} %left_ref.3) | copy-start | bytes 6291460
  50.5 3.9 %collective-permute-start.8 = (f32[32,16,256]{2,1,0:T(8,128)S(1)}, f32[32,16,256]{2,1,0:T(8,128)S(1)}, u32[]{:S(2)}, u32[]{:S(2)}) collective-permute-start(f32[32,16,256]{2,1,0:T(8,128)S(1)} %get-tuple-element.26), channel_id=1, source_target_pairs={{0,1},{1,0},{2,3},{3,2},{4,5},{5,4},{6,7},{7,6},{8,9},{9,8},{10,11... | collective-permute-start | bytes 1572872 | tf_op jit(solution)/shard_map/ppermute | solution.py:224
  106.8 4.0 %collective-permute-start.9 = (bf16[32,16,640]{2,1,0:T(8,128)(2,1)S(1)}, bf16[32,16,640]{2,1,0:T(8,128)(2,1)S(1)}, u32[]{:S(2)}, u32[]{:S(2)}) collective-permute-start(bf16[32,16,640]{2,1,0:T(8,128)(2,1)S(1)} %all_to_all.16.mine_ref), channel_id=1, source_target_pairs={{0,1},{1,0},{2,3},{3,2},{4,5},{5,4},{6,7},{7,6},{8,9},{9,8},{10,11... | collective-permute-start | bytes 1966088 | tf_op jit(solution)/shard_map/ppermute | solution.py:224
  119.4 23.3 %all-to-all-start.2 = ((bf16[64,16,256]{2,1,0:T(8,128)(2,1)}), bf16[64,16,256]{2,1,0:T(8,128)(2,1)S(1)}, u32[]{:S(2)}, u32[]{:S(2)}) async-start(bf16[64,16,256]{2,1,0:T(8,128)(2,1)} %bitcast.2), calls=%async_computation.2 | async-start | bytes 1048576 | tf_op jit(solution)/shard_map/all_to_all | solution.py:329

commit v4 on v3

--- a/solution.py
+++ b/solution.py
@@ -1,3 +1,5 @@
+import functools
+
 import jax
 import jax.numpy as jnp
 from jax import lax
@@ -84,15 +86,37 @@
     return [jnp.concatenate(rows, 0) for rows in lower]
 
 
-def probe_body(left_ref, sketch_ref, out_ref):
-    for k in range(left_ref.shape[0]):
-        for t in range(out_ref.shape[1]):
+def join_body(right_any, left_any, out_ref, sems):
+    slots = right_any.shape[0]
+    copies = [
+        pltpu.make_async_copy(right_any, out_ref.at[:slots], sems.at[0]),
+        pltpu.make_async_copy(left_any, out_ref.at[slots:], sems.at[1]),
+    ]
+    for c in copies:
+        c.start()
+    for c in copies:
+        c.wait()
+
+
+def probe_body(left_any, sketch_any, out_ref, left_ref, sketch_ref, sems, *, first):
+    count = out_ref.shape[0]
+    copies = [pltpu.make_async_copy(sketch_any, sketch_ref, sems.at[count])]
+    for k in range(count):
+        copies.append(
+            pltpu.make_async_copy(left_any.at[first + k], left_ref.at[k], sems.at[k])
+        )
+    for c in copies:
+        c.start()
+    copies[0].wait()
+    for k in range(count):
+        copies[1 + k].wait()
+        for t in range(2):
             cols = slice(128 * t, 128 * t + 128)
             out_ref[k, t] = dot(left_ref[k, :, cols], sketch_ref[:, cols], 0, 0)
 
 
 def early_body(place_ref, own, f1, b1, f2, b2, f3, b3, right_ref, pair_ref, pivot_ref, factor):
-    group, groups = place_ref[0], place_ref[2]
+    group, groups, core = place_ref[0], place_ref[2], place_ref[3]
     slots, n = right_ref.shape[0], own.shape[1]
 
     def put(ref, distance):
@@ -108,15 +132,15 @@
 
     put(own, 0)
     for s, (f, b) in enumerate(((f1, b1), (f2, b2), (f3, b3))):
-        put(f, groups - 1 - s)
-        put(b, 1 + s)
+        put(f, jnp.where(core == 0, groups - 1 - s, 1 + s))
+        put(b, jnp.where(core == 0, 1 + s, groups - 1 - s))
     put(None, groups // 2)
     for k in range(slots):
         pair_ref[k] = dot(factor[:, 128 * k : 128 * k + 128], right_ref[k], 0, 0)
 
 
 def forward_body(
-    place_ref, f4, b4, early_ref, pivot_ref, probe_ref, sketch_ref, right_ref, tright_ref,
+    place_ref, f4, b4, early_ref, pivot_ref, probe_low, probe_high, sketch_ref, right_ref, tright_ref,
     keep_ref, send_ref, pair_ref, core_ref, part,
 ):
     group, live, groups, core = place_ref[0], place_ref[1], place_ref[2], place_ref[3]
@@ -129,7 +153,8 @@
         row = []
         for t in range(2):
             cols = slice(128 * t, 128 * t + 128)
-            value = fine_dot(pair[:, cols], probe_ref[k, t], 1, 0)
+            probe = probe_low if k < probe_low.shape[0] else probe_high
+            value = fine_dot(pair[:, cols], probe[k % probe_low.shape[0], t], 1, 0)
             row.append(jnp.where(k < live, -value, 0.0).astype(LOW))
         mixed.append(jnp.concatenate(row, 1))
     mixed = jnp.concatenate(mixed, 0)
@@ -146,6 +171,14 @@
     send_ref[...] = jnp.where(core == 0, whole[:, 1], whole[:, 0])
 
 
+def add_body(keep_ref, come_ref, out_ref):
+    out_ref[...] = (keep_ref[...] + come_ref[...]).astype(LOW)
+
+
+def last_body(pieces_ref, direct_ref, out_ref, *, rows):
+    out_ref[...] = (jnp.sum(pieces_ref[...].astype(FULL), 0) + direct_ref[...]) / rows
+
+
 def merge_body(keep_ref, come_ref, core_ref, out_ref):
     width = keep_ref.shape[2]
     out_ref[:, :, :width] = (keep_ref[...] + come_ref[...]).astype(LOW)
@@ -163,7 +196,7 @@
 
 def backward_body(
     place_ref, mine_ref, other_ref, own_ref, b4, pivot_ref, pair_ref, tleft_ref, tright_ref,
-    left_ref, basis_ref, term_ref, direct_ref, turn_high, turn_low, tall,
+    left_ref, basis_ref, keep_ref, send_ref, direct_ref, turn_high, turn_low, tall,
 ):
     group, live, groups, core = place_ref[0], place_ref[1], place_ref[2], place_ref[3]
     slots, rows, n = left_ref.shape[0], tall.shape[0], b4.shape[1]
@@ -210,7 +243,9 @@
             folded = jnp.where(k < live, -folded, 0.0).astype(LOW)
             term = dot(left_ref[k, :, cols], folded, 1, 1)
             total = term if total is None else total + term
-        term_ref[:, cols] = total.astype(LOW)
+        total = total.reshape(keep_ref.shape[0], 2, 16, 128)
+        keep_ref[:, :, cols] = jnp.where(core == 0, total[:, 0], total[:, 1])
+        send_ref[:, :, cols] = jnp.where(core == 0, total[:, 1], total[:, 0])
         target_back = fine_dot(inverse[t], seen_target[t], 1, 0).astype(LOW)
         direct_ref[:, cols] = dot(tright_ref[:, cols], target_back, 1, 1)
 
@@ -224,21 +259,49 @@
     return lax.ppermute(x, axis, [(i, (i + by) % n) for i in range(n)])
 
 
+def around(x, by):
+    n = lax.axis_size("grp")
+    pairs = [
+        (2 * i + core, 2 * ((i + (by if core == 0 else -by)) % n) + core)
+        for i in range(n)
+        for core in range(2)
+    ]
+    return lax.ppermute(x, ("grp", INNER[2]), pairs)
+
+
 def near(x):
     return pltpu.with_memory_space_constraint(x, pltpu.VMEM)
 
 
-def kernel(body, name, outs, scratch, place, *arrays, given=()):
+def kernel(body, name, outs, scratch, place, *arrays, given=(), leave=None):
     first = () if place is None else (place,)
     return pl.pallas_call(
         body,
         in_specs=[SMEM] * len(first) + [VMEM] * (len(arrays) + len(given)),
         out_specs=[VMEM] * len(outs),
-        out_shape=[pltpu.VMEM(*o) for o in outs],
+        out_shape=[
+            (jax.ShapeDtypeStruct if o[0] == leave else pltpu.VMEM)(*o) for o in outs
+        ],
         scratch_shapes=[pltpu.VMEM(*o) for o in scratch],
         name=name,
         compiler_params=pltpu.CompilerParams(vmem_limit_bytes=24 << 20),
     )(*first, *[near(x) for x in arrays], *given)
+
+
+def probed(col_left, sketch_cols, first, count):
+    return pl.pallas_call(
+        functools.partial(probe_body, first=first),
+        in_specs=[pl.BlockSpec(memory_space=pltpu.HBM)] * 2,
+        out_specs=VMEM,
+        out_shape=pltpu.VMEM((count, 2, 128, 128), FULL),
+        scratch_shapes=[
+            pltpu.VMEM((count, *col_left.shape[1:]), LOW),
+            pltpu.VMEM(sketch_cols.shape, LOW),
+            pltpu.SemaphoreType.DMA((count + 1,)),
+        ],
+        name="probe",
+        compiler_params=pltpu.CompilerParams(vmem_limit_bytes=24 << 20),
+    )(*(pltpu.with_memory_space_constraint(x, pltpu.HBM) for x in (col_left, sketch_cols)))
 
 
 def shards(
@@ -251,28 +314,30 @@
     place = jnp.stack(
         [lax.axis_index("grp"), live_counts[0], jnp.int32(groups), lax.axis_index(INNER[2])]
     ).astype(jnp.int32)
-    own = jnp.concatenate([row_right, row_left], 0)
-    chunks, up, down = [own], own, own
+    own = pl.pallas_call(
+        join_body,
+        in_specs=[pl.BlockSpec(memory_space=pltpu.HBM)] * 2,
+        out_specs=VMEM,
+        out_shape=pltpu.VMEM((2 * slots, *row_left.shape[1:]), LOW),
+        scratch_shapes=[pltpu.SemaphoreType.DMA((2,))],
+        name="join",
+        compiler_params=pltpu.CompilerParams(vmem_limit_bytes=24 << 20),
+    )(*(pltpu.with_memory_space_constraint(x, pltpu.HBM) for x in (row_right, row_left)))
+    chunks, probes, up, down = [own], [], own, own
     for step in range(3):
-        up, down = shift(up, "grp", 1), shift(down, "grp", -1)
+        up, down = around(up, 1), around(down, -1)
         if step == 0:
-            (probe,) = kernel(
-                probe_body,
-                "probe",
-                [((slots, 2, 128, 128), FULL)],
-                [],
-                None,
-                given=(col_left, sketch_cols),
-            )
             own_sketch = lax.dynamic_slice_in_dim(
                 sketch_cols, lax.axis_index(INNER) * block, block, 0
             )
-        if step == 1:
+        if step < 2:
+            probe = probed(col_left, sketch_cols, step * (slots // 2), slots // 2)
             up, down, probe, own_sketch, place = lax.optimization_barrier(
                 (up, down, probe, own_sketch, place)
             )
+            probes.append(probe)
         chunks += [up, down]
-    last_up, last_down = shift(up[:slots], "grp", 1), shift(down[slots:], "grp", -1)
+    last_up, last_down = around(up[:slots], 1), around(down[slots:], -1)
     early, pivot = kernel(
         early_body,
         "early",
@@ -293,7 +358,7 @@
         last_down,
         early,
         pivot,
-        probe,
+        *probes,
         own_sketch,
         given=(col_right, target_right),
     )
@@ -312,10 +377,10 @@
     )
     mine = lax.all_to_all(mine, far, 0, 0, tiled=True)
     other = shift(mine, INNER[2], 1)
-    basis, term, direct = kernel(
+    basis, keep, send, direct = kernel(
         backward_body,
         "backward",
-        [((block, width), FULL), ((rows, width), LOW), ((block, width), FULL)],
+        [((block, width), FULL), (piece, FULL), (piece, FULL), ((block, width), FULL)],
         [((2, 128, rows), LOW), ((2, 128, rows), LOW), ((rows, width), LOW)],
         place,
         mine,
@@ -326,8 +391,17 @@
         pair,
         given=(target_left, target_right, col_left),
     )
-    pieces = lax.all_to_all(term.reshape(n, block, width), INNER, 0, 0, tiled=True)
-    coeffs = (jnp.sum(pieces.astype(FULL), 0) + direct) / rows
+    (merged,) = kernel(add_body, "add", [(piece, LOW)], [], None, keep, shift(send, INNER[2], 1))
+    (coeffs,) = kernel(
+        functools.partial(last_body, rows=rows),
+        "last",
+        [((block, width), FULL)],
+        [],
+        None,
+        lax.all_to_all(merged, far, 0, 0, tiled=True),
+        direct,
+        leave=(block, width),
+    )
     return basis, coeffs
 
 

time: 145 us -> 143 us (0.986)
  Pallas kernels: 13 us -> 17.6 us
  local copies, waits for them, and re-layouts: 5.27 us -> 1.48 us
  blocking collectives: 52.2 us -> 48.8 us
  waiting for transfers between devices: 30.3 us -> 31.9 us
    ppermute x0 -> x8, starting transfers between devices: none -> 29.5 us  [around(): return lax.ppermute(x, ('grp', INNER[2]), pairs)]
    ppermute x10 -> x3, starting transfers between devices: 34.7 us -> 6 us  [shift(): return lax.ppermute(x, axis, [(i, (i + by) % n) for i in range(n)])]
    ppermute x0 -> x8, waiting for transfers between devices: none -> 13.6 us  [around(): return lax.ppermute(x, ('grp', INNER[2]), pairs)]
    ppermute x10 -> x3, waiting for transfers between devices: 13.3 us -> 5.7 us  [shift(): return lax.ppermute(x, axis, [(i, (i + by) % n) for i in range(n)])]
    pallas_call x0 -> x3, Pallas kernels: none -> 4.8 us  [the longest x2 3.82 us: probed(): pl.pallas_call(functools.partial(probe_body, first=first), in_specs=[pl.B...]
    all_to_all x1, waiting for transfers between devices: 17 us -> 12.6 us  [shards(): lax.all_to_all(merged, far, 0, 0, tiled=True)]
    unnamed x14 -> x9, local copies, waits for them, and re-layouts: 4.32 us -> 0.63 us
    all_to_all x1, blocking collectives: 28.6 us -> 25.2 us  [shards(): lax.all_to_all(merged, far, 0, 0, tiled=True)]
  transfers between devices with their start and end apart: 11 -> 12, of which waited for: 7 -> 9; matrix products, arithmetic and copies ran while one was open for 0% -> 1% of each run, Pallas kernels for 2% -> 4%
where the time goes in v4:
time: 143 us; the launch traced here: 142 us
  blocking collectives  48.8 us (34%)
  starting transfers between devices  40.5 us (28%)
  waiting for transfers between devices  31.9 us (22%)
  Pallas kernels  17.6 us (12%)
  between operations  1.51 us (1%)
  local copies, waits for them, and re-layouts  1.48 us (1%)
    ppermute x8, starting transfers between devices, around(): return lax.ppermute(x, ('grp', INNER[2]), pairs)  29.5 us
    all_to_all x1, blocking collectives, shards(): lax.all_to_all(merged, far, 0, 0, tiled=True)  25.2 us
    all_to_all x1, blocking collectives, shards(): mine = lax.all_to_all(mine, far, 0, 0, tiled=True)  23.6 us
    ppermute x8, waiting for transfers between devices, around(): return lax.ppermute(x, ('grp', INNER[2]), pairs)  13.6 us
    pallas_call x7, Pallas kernels, kernel(): pl.pallas_call(body, in_specs=[SMEM] * len(first) + [VMEM] * (len(arrays)...  12.8 us
    all_to_all x1, waiting for transfers between devices, shards(): lax.all_to_all(merged, far, 0, 0, tiled=True)  12.6 us
    ppermute x3, starting transfers between devices, shift(): return lax.ppermute(x, axis, [(i, (i + by) % n) for i in range(n)])  6 us
    ppermute x3, waiting for transfers between devices, shift(): return lax.ppermute(x, axis, [(i, (i + by) % n) for i in range(n)])  5.7 us
  transfers between devices with their start and end apart: 12, of which 9 were waited for; matrix products, arithmetic and copies ran while one was open for 1% of the time, Pallas kernels for 4%

profile of v4, /device:TPU:56, one launch (start us, length us, event | category | flops | bytes accessed | tf_op | source)
XLA Modules:
  0.0 141.9 jit_solution(10638139354462289655)
XLA Ops:
  1.6 3.3 %collective-permute-start.1 = (bf16[8,128,128]{2,1,0:T(8,128)(2,1)S(1)}, bf16[8,128,128]{2,1,0:T(8,128)(2,1)S(1)}, u32[]{:S(2)}, u32[]{:S(2)}) collective-permute-start(bf16[8,128,128]{2,1,0:T(8,128)(2,1)S(1)} %join.1.own), channel_id=1, source_target_pairs={{0,448},{1,65},{64,0},{65,129},{128,64},{129,193},{192,128},{193,2... | collective-permute-start | bytes 786440 | tf_op jit(solution)/shard_map/ppermute | solution.py:269
  4.9 5.7 %collective-permute-start = (bf16[8,128,128]{2,1,0:T(8,128)(2,1)S(1)}, bf16[8,128,128]{2,1,0:T(8,128)(2,1)S(1)}, u32[]{:S(2)}, u32[]{:S(2)}) collective-permute-start(bf16[8,128,128]{2,1,0:T(8,128)(2,1)S(1)} %join.1.own), channel_id=1, source_target_pairs={{0,64},{1,449},{64,128},{65,1},{128,192},{129,65},{192,256},{193,1... | collective-permute-start | bytes 786440 | tf_op jit(solution)/shard_map/ppermute | solution.py:269
  11.2 1.9 %probe.2.probe_low = f32[2,2,128,128]{3,2,1,0:T(8,128)S(1)} custom-call(bf16[4,1024,256]{2,1,0:T(8,128)(2,1)} %left_ref.1, bf16[1024,256]{1,0:T(8,128)(2,1)} %sketch_any.3), custom_call_target="tpu_custom_call" | custom-call | tf_op jit(solution)/shard_map/probe/pallas_call | solution.py:292
  14.7 5.3 %collective-permute-start.2 = (bf16[8,128,128]{2,1,0:T(8,128)(2,1)S(1)}, bf16[8,128,128]{2,1,0:T(8,128)(2,1)S(1)}, u32[]{:S(2)}, u32[]{:S(2)}) collective-permute-start(bf16[8,128,128]{2,1,0:T(8,128)(2,1)S(1)} %collective-permute-done.f1), channel_id=1, source_target_pairs={{0,64},{1,449},{64,128},{65,1},{128,192},{129,65},{192,256},{193,1... | collective-permute-start | bytes 786440 | tf_op jit(solution)/shard_map/ppermute | solution.py:269
  20.0 1.9 %collective-permute-start.3 = (bf16[8,128,128]{2,1,0:T(8,128)(2,1)S(1)}, bf16[8,128,128]{2,1,0:T(8,128)(2,1)S(1)}, u32[]{:S(2)}, u32[]{:S(2)}) collective-permute-start(bf16[8,128,128]{2,1,0:T(8,128)(2,1)S(1)} %collective-permute-done.1.b1), channel_id=1, source_target_pairs={{0,448},{1,65},{64,0},{65,129},{128,64},{129,193},{192,128},{193,2... | collective-permute-start | bytes 786440 | tf_op jit(solution)/shard_map/ppermute | solution.py:269
  22.0 1.9 %probe.3.probe_high = f32[2,2,128,128]{3,2,1,0:T(8,128)S(1)} custom-call(bf16[4,1024,256]{2,1,0:T(8,128)(2,1)} %left_ref.1, bf16[1024,256]{1,0:T(8,128)(2,1)} %sketch_any.3), custom_call_target="tpu_custom_call" | custom-call | tf_op jit(solution)/shard_map/probe/pallas_call | solution.py:292
  23.9 2.3 %collective-permute-done.2.f2 = bf16[8,128,128]{2,1,0:T(8,128)(2,1)S(1)} collective-permute-done((bf16[8,128,128]{2,1,0:T(8,128)(2,1)S(1)}, bf16[8,128,128]{2,1,0:T(8,128)(2,1)S(1)}, u32[]{:S(2)}, u32[]{:S(2)}) %collective-permute-start.2) | collective-permute-done | bytes 262176 | tf_op jit(solution)/shard_map/ppermute | solution.py:269
  26.2 3.3 %collective-permute-done.3.b2 = bf16[8,128,128]{2,1,0:T(8,128)(2,1)S(1)} collective-permute-done((bf16[8,128,128]{2,1,0:T(8,128)(2,1)S(1)}, bf16[8,128,128]{2,1,0:T(8,128)(2,1)S(1)}, u32[]{:S(2)}, u32[]{:S(2)}) %collective-permute-start.3) | collective-permute-done | bytes 262176 | tf_op jit(solution)/shard_map/ppermute | solution.py:269
  29.5 2.3 %collective-permute-start.4 = (bf16[8,128,128]{2,1,0:T(8,128)(2,1)S(1)}, bf16[8,128,128]{2,1,0:T(8,128)(2,1)S(1)}, u32[]{:S(2)}, u32[]{:S(2)}) collective-permute-start(bf16[8,128,128]{2,1,0:T(8,128)(2,1)S(1)} %collective-permute-done.2.f2), channel_id=1, source_target_pairs={{0,64},{1,449},{64,128},{65,1},{128,192},{129,65},{192,256},{193,1... | collective-permute-start | bytes 786440 | tf_op jit(solution)/shard_map/ppermute | solution.py:269
  31.8 3.6 %collective-permute-start.6 = (bf16[8,128,128]{2,1,0:T(8,128)(2,1)S(1)}, bf16[8,128,128]{2,1,0:T(8,128)(2,1)S(1)}, u32[]{:S(2)}, u32[]{:S(2)}) collective-permute-start(bf16[8,128,128]{2,1,0:T(8,128)(2,1)S(1)} %collective-permute-done.3.b2), channel_id=1, source_target_pairs={{0,448},{1,65},{64,0},{65,129},{128,64},{129,193},{192,128},{193,2... | collective-permute-start | bytes 786440 | tf_op jit(solution)/shard_map/ppermute | solution.py:269
  35.4 2.6 %collective-permute-done.4.f3 = bf16[8,128,128]{2,1,0:T(8,128)(2,1)S(1)} collective-permute-done((bf16[8,128,128]{2,1,0:T(8,128)(2,1)S(1)}, bf16[8,128,128]{2,1,0:T(8,128)(2,1)S(1)}, u32[]{:S(2)}, u32[]{:S(2)}) %collective-permute-start.4) | collective-permute-done | bytes 262176 | tf_op jit(solution)/shard_map/ppermute | solution.py:269
  38.0 5.6 %collective-permute-start.5 = (bf16[4,128,128]{2,1,0:T(8,128)(2,1)S(1)}, bf16[4,128,128]{2,1,0:T(8,128)(2,1)S(1)}, u32[]{:S(2)}, u32[]{:S(2)}) collective-permute-start(bf16[4,128,128]{2,1,0:T(8,128)(2,1)S(1)} %slice.8), channel_id=1, source_target_pairs={{0,64},{1,449},{64,128},{65,1},{128,192},{129,65},{192,256},{193,1... | collective-permute-start | bytes 393224 | tf_op jit(solution)/shard_map/ppermute | solution.py:269
  43.6 1.9 %collective-permute-start.7 = (bf16[4,128,128]{2,1,0:T(8,128)(2,1)S(1)}, bf16[4,128,128]{2,1,0:T(8,128)(2,1)S(1)}, u32[]{:S(2)}, u32[]{:S(2)}) collective-permute-start(bf16[4,128,128]{2,1,0:T(8,128)(2,1)S(1)} %slice.9), channel_id=1, source_target_pairs={{0,448},{1,65},{64,0},{65,129},{128,64},{129,193},{192,128},{193,2... | collective-permute-start | bytes 393224 | tf_op jit(solution)/shard_map/ppermute | solution.py:269
  46.9 4.7 %collective-permute-done.7.b4 = bf16[4,128,128]{2,1,0:T(8,128)(2,1)S(1)} collective-permute-done((bf16[4,128,128]{2,1,0:T(8,128)(2,1)S(1)}, bf16[4,128,128]{2,1,0:T(8,128)(2,1)S(1)}, u32[]{:S(2)}, u32[]{:S(2)}) %collective-permute-start.7) | collective-permute-done | bytes 131104 | tf_op jit(solution)/shard_map/ppermute | solution.py:269
  51.7 2.0 %forward.1 = (f32[32,16,256]{2,1,0:T(8,128)S(1)}, f32[32,16,256]{2,1,0:T(8,128)S(1)}, f32[4,128,256]{2,1,0:T(8,128)S(1)}, bf16[32,16,128]{2,1,0:T(8,128)(2,1)S(1)}) custom-call(s32[4]{0:T(128)S(1)} %pad_add_fusion.place_ref, bf16[4,128,128]{2,1,0:T(8,128)(2,1)S(1)} %collective-permute-done.5.f4, bf16[4,128,128]{2,1,0:T(8,128)(2,1)S(1)} %collective-permute-done.7.b4, ...), custom_call_target="tpu_custom_call" | custom-call | tf_op jit(solution)/shard_map/forward/pallas_call | solution.py:278
  53.7 2.1 %collective-permute-start.8 = (f32[32,16,256]{2,1,0:T(8,128)S(1)}, f32[32,16,256]{2,1,0:T(8,128)S(1)}, u32[]{:S(2)}, u32[]{:S(2)}) collective-permute-start(f32[32,16,256]{2,1,0:T(8,128)S(1)} %get-tuple-element.37), channel_id=1, source_target_pairs={{0,1},{1,0},{2,3},{3,2},{4,5},{5,4},{6,7},{7,6},{8,9},{9,8},{10,11... | collective-permute-start | bytes 1572872 | tf_op jit(solution)/shard_map/ppermute | solution.py:259
  57.8 25.2 %all_to_all.15.pieces_ref = bf16[32,16,384]{2,1,0:T(8,128)(2,1)S(1)} all-to-all(bf16[32,16,384]{2,1,0:T(8,128)(2,1)S(1)} %merge.1), channel_id=1, replica_groups=mesh['grp'=8,'inner_0'=8,'inner_1'=4,'inner_2'=2] {'inner_0','inner_1'}, dimensions={0} | all-to-all | bytes 786432 | tf_op jit(solution)/shard_map/all_to_all | solution.py:375
  83.0 23.6 %all_to_all.16.mine_ref = bf16[32,16,640]{2,1,0:T(8,128)(2,1)S(1)} all-to-all(bf16[32,16,640]{2,1,0:T(8,128)(2,1)S(1)} %get-tuple-element.39), channel_id=1, replica_groups=mesh['grp'=8,'inner_0'=8,'inner_1'=4,'inner_2'=2] {'inner_0','inner_1'}, dimensions={0} | all-to-all | bytes 1310720 | tf_op jit(solution)/shard_map/all_to_all | solution.py:378
  106.6 1.9 %collective-permute-start.9 = (bf16[32,16,640]{2,1,0:T(8,128)(2,1)S(1)}, bf16[32,16,640]{2,1,0:T(8,128)(2,1)S(1)}, u32[]{:S(2)}, u32[]{:S(2)}) collective-permute-start(bf16[32,16,640]{2,1,0:T(8,128)(2,1)S(1)} %all_to_all.16.mine_ref), channel_id=1, source_target_pairs={{0,1},{1,0},{2,3},{3,2},{4,5},{5,4},{6,7},{7,6},{8,9},{9,8},{10,11... | collective-permute-start | bytes 1966088 | tf_op jit(solution)/shard_map/ppermute | solution.py:259
  108.5 2.1 %collective-permute-done.9.other_ref = bf16[32,16,640]{2,1,0:T(8,128)(2,1)S(1)} collective-permute-done((bf16[32,16,640]{2,1,0:T(8,128)(2,1)S(1)}, bf16[32,16,640]{2,1,0:T(8,128)(2,1)S(1)}, u32[]{:S(2)}, u32[]{:S(2)}) %collective-permute-start.9) | collective-permute-done | bytes 655392 | tf_op jit(solution)/shard_map/ppermute | solution.py:259
  110.6 7.8 %backward.1 = (f32[16,256]{1,0:T(8,128)S(1)}, f32[32,16,256]{2,1,0:T(8,128)S(1)}, f32[32,16,256]{2,1,0:T(8,128)S(1)}, f32[16,256]{1,0:T(8,128)S(1)}) custom-call(s32[4]{0:T(128)S(1)} %pad_add_fusion.place_ref, bf16[32,16,640]{2,1,0:T(8,128)(2,1)S(1)} %all_to_all.16.mine_ref, bf16[32,16,640]{2,1,0:T(8,128)(2,1)S(1)} %collective-permute-done.9.other_ref, ...), custom_call_target="tpu_custom_call" | custom-call | tf_op jit(solution)/shard_map/backward/pallas_call | solution.py:278
  118.4 2.0 %collective-permute-start.10 = (f32[32,16,256]{2,1,0:T(8,128)S(1)}, f32[32,16,256]{2,1,0:T(8,128)S(1)}, u32[]{:S(2)}, u32[]{:S(2)}) collective-permute-start(f32[32,16,256]{2,1,0:T(8,128)S(1)} %get-tuple-element.44), channel_id=1, source_target_pairs={{0,1},{1,0},{2,3},{3,2},{4,5},{5,4},{6,7},{7,6},{8,9},{9,8},{10,11... | collective-permute-start | bytes 1572872 | tf_op jit(solution)/shard_map/ppermute | solution.py:259
  123.0 5.0 %all-to-all-start.2 = ((bf16[32,16,256]{2,1,0:T(8,128)(2,1)}), bf16[32,16,256]{2,1,0:T(8,128)(2,1)S(1)}, u32[]{:S(2)}, u32[]{:S(2)}) async-start(bf16[32,16,256]{2,1,0:T(8,128)(2,1)} %add.19), calls=%async_computation.2 | async-start | bytes 524288 | tf_op jit(solution)/shard_map/all_to_all | solution.py:401
  128.6 12.6 %all-to-all-done.2.pieces_ref = bf16[32,16,256]{2,1,0:T(8,128)(2,1)S(1)} async-done(((bf16[32,16,256]{2,1,0:T(8,128)(2,1)}), bf16[32,16,256]{2,1,0:T(8,128)(2,1)S(1)}, u32[]{:S(2)}, u32[]{:S(2)}) %all-to-all-start.2) | async-done | bytes 262176 | tf_op jit(solution)/shard_map/all_to_all | solution.py:401
  (25 shorter events, 9.8 us)
Async XLA Ops:
  1.6 13.1 %collective-permute-start.1 = (bf16[8,128,128]{2,1,0:T(8,128)(2,1)S(1)}, bf16[8,128,128]{2,1,0:T(8,128)(2,1)S(1)}, u32[]{:S(2)}, u32[]{:S(2)}) collective-permute-start(bf16[8,128,128]{2,1,0:T(8,128)(2,1)S(1)} %join.1.own), channel_id=1, source_target_pairs={{0,448},{1,65},{64,0},{65,129},{128,64},{129,193},{192,128},{193,2... | collective-permute-start | bytes 786440 | tf_op jit(solution)/shard_map/ppermute | solution.py:269
  4.9 9.8 %collective-permute-start = (bf16[8,128,128]{2,1,0:T(8,128)(2,1)S(1)}, bf16[8,128,128]{2,1,0:T(8,128)(2,1)S(1)}, u32[]{:S(2)}, u32[]{:S(2)}) collective-permute-start(bf16[8,128,128]{2,1,0:T(8,128)(2,1)S(1)} %join.1.own), channel_id=1, source_target_pairs={{0,64},{1,449},{64,128},{65,1},{128,192},{129,65},{192,256},{193,1... | collective-permute-start | bytes 786440 | tf_op jit(solution)/shard_map/ppermute | solution.py:269
  13.2 32.4 %copy-start.1 = (bf16[4,1024,256]{2,1,0:T(8,128)(2,1)S(1)}, bf16[4,1024,256]{2,1,0:T(8,128)(2,1)}, u32[]{:S(2)}) copy-start(bf16[4,1024,256]{2,1,0:T(8,128)(2,1)} %right_ref.3) | copy-start | bytes 6291460
  14.7 11.5 %collective-permute-start.2 = (bf16[8,128,128]{2,1,0:T(8,128)(2,1)S(1)}, bf16[8,128,128]{2,1,0:T(8,128)(2,1)S(1)}, u32[]{:S(2)}, u32[]{:S(2)}) collective-permute-start(bf16[8,128,128]{2,1,0:T(8,128)(2,1)S(1)} %collective-permute-done.f1), channel_id=1, source_target_pairs={{0,64},{1,449},{64,128},{65,1},{128,192},{129,65},{192,256},{193,1... | collective-permute-start | bytes 786440 | tf_op jit(solution)/shard_map/ppermute | solution.py:269
  20.0 9.5 %collective-permute-start.3 = (bf16[8,128,128]{2,1,0:T(8,128)(2,1)S(1)}, bf16[8,128,128]{2,1,0:T(8,128)(2,1)S(1)}, u32[]{:S(2)}, u32[]{:S(2)}) collective-permute-start(bf16[8,128,128]{2,1,0:T(8,128)(2,1)S(1)} %collective-permute-done.1.b1), channel_id=1, source_target_pairs={{0,448},{1,65},{64,0},{65,129},{128,64},{129,193},{192,128},{193,2... | collective-permute-start | bytes 786440 | tf_op jit(solution)/shard_map/ppermute | solution.py:269
  29.5 8.4 %collective-permute-start.4 = (bf16[8,128,128]{2,1,0:T(8,128)(2,1)S(1)}, bf16[8,128,128]{2,1,0:T(8,128)(2,1)S(1)}, u32[]{:S(2)}, u32[]{:S(2)}) collective-permute-start(bf16[8,128,128]{2,1,0:T(8,128)(2,1)S(1)} %collective-permute-done.2.f2), channel_id=1, source_target_pairs={{0,64},{1,449},{64,128},{65,1},{128,192},{129,65},{192,256},{193,1... | collective-permute-start | bytes 786440 | tf_op jit(solution)/shard_map/ppermute | solution.py:269
  31.8 11.8 %collective-permute-start.6 = (bf16[8,128,128]{2,1,0:T(8,128)(2,1)S(1)}, bf16[8,128,128]{2,1,0:T(8,128)(2,1)S(1)}, u32[]{:S(2)}, u32[]{:S(2)}) collective-permute-start(bf16[8,128,128]{2,1,0:T(8,128)(2,1)S(1)} %collective-permute-done.3.b2), channel_id=1, source_target_pairs={{0,448},{1,65},{64,0},{65,129},{128,64},{129,193},{192,128},{193,2... | collective-permute-start | bytes 786440 | tf_op jit(solution)/shard_map/ppermute | solution.py:269
  37.9 13.7 %copy-start.2 = (bf16[16,256]{1,0:T(8,128)(2,1)S(1)}, bf16[16,256]{1,0:T(8,128)(2,1)}, u32[]{:S(2)}) copy-start(bf16[16,256]{1,0:T(8,128)(2,1)} %tright_ref.3) | copy-start | bytes 24580
  38.0 9.0 %collective-permute-start.5 = (bf16[4,128,128]{2,1,0:T(8,128)(2,1)S(1)}, bf16[4,128,128]{2,1,0:T(8,128)(2,1)S(1)}, u32[]{:S(2)}, u32[]{:S(2)}) collective-permute-start(bf16[4,128,128]{2,1,0:T(8,128)(2,1)S(1)} %slice.8), channel_id=1, source_target_pairs={{0,64},{1,449},{64,128},{65,1},{128,192},{129,65},{192,256},{193,1... | collective-permute-start | bytes 393224 | tf_op jit(solution)/shard_map/ppermute | solution.py:269
  43.6 8.1 %collective-permute-start.7 = (bf16[4,128,128]{2,1,0:T(8,128)(2,1)S(1)}, bf16[4,128,128]{2,1,0:T(8,128)(2,1)S(1)}, u32[]{:S(2)}, u32[]{:S(2)}) collective-permute-start(bf16[4,128,128]{2,1,0:T(8,128)(2,1)S(1)} %slice.9), channel_id=1, source_target_pairs={{0,448},{1,65},{64,0},{65,129},{128,64},{129,193},{192,128},{193,2... | collective-permute-start | bytes 393224 | tf_op jit(solution)/shard_map/ppermute | solution.py:269
  53.7 29.2 %copy-start.3 = (bf16[16,256]{1,0:T(8,128)(2,1)S(1)}, bf16[16,256]{1,0:T(8,128)(2,1)}, u32[]{:S(2)}) copy-start(bf16[16,256]{1,0:T(8,128)(2,1)} %tleft_ref.3) | copy-start | bytes 24580
  53.7 56.9 %copy-start = (bf16[4,1024,256]{2,1,0:T(8,128)(2,1)S(1)}, bf16[4,1024,256]{2,1,0:T(8,128)(2,1)}, u32[]{:S(2)}) copy-start(bf16[4,1024,256]{2,1,0:T(8,128)(2,1)} %left_ref.1) | copy-start | bytes 6291460
  53.7 3.9 %collective-permute-start.8 = (f32[32,16,256]{2,1,0:T(8,128)S(1)}, f32[32,16,256]{2,1,0:T(8,128)S(1)}, u32[]{:S(2)}, u32[]{:S(2)}) collective-permute-start(f32[32,16,256]{2,1,0:T(8,128)S(1)} %get-tuple-element.37), channel_id=1, source_target_pairs={{0,1},{1,0},{2,3},{3,2},{4,5},{5,4},{6,7},{7,6},{8,9},{9,8},{10,11... | collective-permute-start | bytes 1572872 | tf_op jit(solution)/shard_map/ppermute | solution.py:259
  106.6 4.0 %collective-permute-start.9 = (bf16[32,16,640]{2,1,0:T(8,128)(2,1)S(1)}, bf16[32,16,640]{2,1,0:T(8,128)(2,1)S(1)}, u32[]{:S(2)}, u32[]{:S(2)}) collective-permute-start(bf16[32,16,640]{2,1,0:T(8,128)(2,1)S(1)} %all_to_all.16.mine_ref), channel_id=1, source_target_pairs={{0,1},{1,0},{2,3},{3,2},{4,5},{5,4},{6,7},{7,6},{8,9},{9,8},{10,11... | collective-permute-start | bytes 1966088 | tf_op jit(solution)/shard_map/ppermute | solution.py:259
  118.4 3.8 %collective-permute-start.10 = (f32[32,16,256]{2,1,0:T(8,128)S(1)}, f32[32,16,256]{2,1,0:T(8,128)S(1)}, u32[]{:S(2)}, u32[]{:S(2)}) collective-permute-start(f32[32,16,256]{2,1,0:T(8,128)S(1)} %get-tuple-element.44), channel_id=1, source_target_pairs={{0,1},{1,0},{2,3},{3,2},{4,5},{5,4},{6,7},{7,6},{8,9},{9,8},{10,11... | collective-permute-start | bytes 1572872 | tf_op jit(solution)/shard_map/ppermute | solution.py:259
  123.0 18.3 %all-to-all-start.2 = ((bf16[32,16,256]{2,1,0:T(8,128)(2,1)}), bf16[32,16,256]{2,1,0:T(8,128)(2,1)S(1)}, u32[]{:S(2)}, u32[]{:S(2)}) async-start(bf16[32,16,256]{2,1,0:T(8,128)(2,1)} %add.19), calls=%async_computation.2 | async-start | bytes 524288 | tf_op jit(solution)/shard_map/all_to_all | solution.py:401

commit v5 on v4

--- a/solution.py
+++ b/solution.py
@@ -116,7 +116,7 @@
 
 
 def early_body(place_ref, own, f1, b1, f2, b2, f3, b3, right_ref, pair_ref, pivot_ref, factor):
-    group, groups, core = place_ref[0], place_ref[2], place_ref[3]
+    group, groups = place_ref[0], place_ref[2]
     slots, n = right_ref.shape[0], own.shape[1]
 
     def put(ref, distance):
@@ -132,8 +132,8 @@
 
     put(own, 0)
     for s, (f, b) in enumerate(((f1, b1), (f2, b2), (f3, b3))):
-        put(f, jnp.where(core == 0, groups - 1 - s, 1 + s))
-        put(b, jnp.where(core == 0, 1 + s, groups - 1 - s))
+        put(f, groups - 1 - s)
+        put(b, 1 + s)
     put(None, groups // 2)
     for k in range(slots):
         pair_ref[k] = dot(factor[:, 128 * k : 128 * k + 128], right_ref[k], 0, 0)
@@ -168,11 +168,11 @@
     core_ref[...] = jnp.concatenate(halves(jnp.concatenate(cores, 0).reshape(half, 8, 128)), 1)
     whole = part[...].reshape(half, 2, 16, part.shape[1])
     keep_ref[...] = jnp.where(core == 0, whole[:, 0], whole[:, 1])
-    send_ref[...] = jnp.where(core == 0, whole[:, 1], whole[:, 0])
+    send_ref[...] = jnp.where(core == 0, whole[:, 1], whole[:, 0]).astype(LOW)
 
 
 def add_body(keep_ref, come_ref, out_ref):
-    out_ref[...] = (keep_ref[...] + come_ref[...]).astype(LOW)
+    out_ref[...] = (keep_ref[...] + come_ref[...].astype(FULL)).astype(LOW)
 
 
 def last_body(pieces_ref, direct_ref, out_ref, *, rows):
@@ -181,7 +181,7 @@
 
 def merge_body(keep_ref, come_ref, core_ref, out_ref):
     width = keep_ref.shape[2]
-    out_ref[:, :, :width] = (keep_ref[...] + come_ref[...]).astype(LOW)
+    out_ref[:, :, :width] = (keep_ref[...] + come_ref[...].astype(FULL)).astype(LOW)
     out_ref[:, :, width:] = core_ref[...]
 
 
@@ -245,7 +245,7 @@
             total = term if total is None else total + term
         total = total.reshape(keep_ref.shape[0], 2, 16, 128)
         keep_ref[:, :, cols] = jnp.where(core == 0, total[:, 0], total[:, 1])
-        send_ref[:, :, cols] = jnp.where(core == 0, total[:, 1], total[:, 0])
+        send_ref[:, :, cols] = jnp.where(core == 0, total[:, 1], total[:, 0]).astype(LOW)
         target_back = fine_dot(inverse[t], seen_target[t], 1, 0).astype(LOW)
         direct_ref[:, cols] = dot(tright_ref[:, cols], target_back, 1, 1)
 
@@ -257,16 +257,6 @@
 def shift(x, axis, by):
     n = lax.axis_size(axis)
     return lax.ppermute(x, axis, [(i, (i + by) % n) for i in range(n)])
-
-
-def around(x, by):
-    n = lax.axis_size("grp")
-    pairs = [
-        (2 * i + core, 2 * ((i + (by if core == 0 else -by)) % n) + core)
-        for i in range(n)
-        for core in range(2)
-    ]
-    return lax.ppermute(x, ("grp", INNER[2]), pairs)
 
 
 def near(x):
@@ -325,19 +315,19 @@
     )(*(pltpu.with_memory_space_constraint(x, pltpu.HBM) for x in (row_right, row_left)))
     chunks, probes, up, down = [own], [], own, own
     for step in range(3):
-        up, down = around(up, 1), around(down, -1)
+        up, down = shift(up, "grp", 1), shift(down, "grp", -1)
         if step == 0:
             own_sketch = lax.dynamic_slice_in_dim(
                 sketch_cols, lax.axis_index(INNER) * block, block, 0
             )
         if step < 2:
             probe = probed(col_left, sketch_cols, step * (slots // 2), slots // 2)
-            up, down, probe, own_sketch, place = lax.optimization_barrier(
-                (up, down, probe, own_sketch, place)
+            up, probe, own_sketch, place = lax.optimization_barrier(
+                (up, probe, own_sketch, place)
             )
             probes.append(probe)
         chunks += [up, down]
-    last_up, last_down = around(up[:slots], 1), around(down[slots:], -1)
+    last_up, last_down = shift(up[:slots], "grp", 1), shift(down[slots:], "grp", -1)
     early, pivot = kernel(
         early_body,
         "early",
@@ -351,7 +341,7 @@
     keep, send, pair, core = kernel(
         forward_body,
         "forward",
-        [(piece, FULL), (piece, FULL), ((slots, 128, width), FULL), ((half, block, 128), LOW)],
+        [(piece, FULL), (piece, LOW), ((slots, 128, width), FULL), ((half, block, 128), LOW)],
         [((rows, width), FULL)],
         place,
         last_up,
@@ -380,7 +370,7 @@
     basis, keep, send, direct = kernel(
         backward_body,
         "backward",
-        [((block, width), FULL), (piece, FULL), (piece, FULL), ((block, width), FULL)],
+        [((block, width), FULL), (piece, FULL), (piece, LOW), ((block, width), FULL)],
         [((2, 128, rows), LOW), ((2, 128, rows), LOW), ((rows, width), LOW)],
         place,
         mine,
@@ -392,6 +382,7 @@
         given=(target_left, target_right, col_left),
     )
     (merged,) = kernel(add_body, "add", [(piece, LOW)], [], None, keep, shift(send, INNER[2], 1))
+    merged = near(merged)
     (coeffs,) = kernel(
         functools.partial(last_body, rows=rows),
         "last",

time: 143 us -> 139 us (0.972); the launches traced: 142 us -> 136 us
  waiting for transfers between devices: 31.9 us -> 26.8 us
  blocking collectives: 48.8 us -> 46.7 us
  starting transfers between devices: 40.5 us -> 42 us
    ppermute x3 -> x11, starting transfers between devices: 6 us -> 37 us  [shift(): return lax.ppermute(x, axis, [(i, (i + by) % n) for i in range(n)])]
    ppermute x8 -> x0, starting transfers between devices: 29.5 us -> none  [around(): return lax.ppermute(x, ('grp', INNER[2]), pairs)]
    ppermute x8 -> x0, waiting for transfers between devices: 13.6 us -> none  [around(): return lax.ppermute(x, ('grp', INNER[2]), pairs)]
    ppermute x3 -> x11, waiting for transfers between devices: 5.7 us -> 14.2 us  [shift(): return lax.ppermute(x, axis, [(i, (i + by) % n) for i in range(n)])]
    all_to_all x1, blocking collectives: 25.2 us -> 23.1 us  [shards(): lax.all_to_all(merged, far, 0, 0, tiled=True)]
where the time goes in v5:
time: 139 us; the launch traced here: 136 us
  blocking collectives  46.7 us (34%)
  starting transfers between devices  42 us (30%)
  waiting for transfers between devices  26.8 us (19%)
  Pallas kernels  17.6 us (13%)
  between operations  1.5 us (1%)
  local copies, waits for them, and re-layouts  1.48 us (1%)
    ppermute x11, starting transfers between devices, shift(): return lax.ppermute(x, axis, [(i, (i + by) % n) for i in range(n)])  37 us
    all_to_all x1, blocking collectives, shards(): mine = lax.all_to_all(mine, far, 0, 0, tiled=True)  23.6 us
    all_to_all x1, blocking collectives, shards(): lax.all_to_all(merged, far, 0, 0, tiled=True)  23.1 us
    ppermute x11, waiting for transfers between devices, shift(): return lax.ppermute(x, axis, [(i, (i + by) % n) for i in range(n)])  14.2 us
    pallas_call x7, Pallas kernels, kernel(): pl.pallas_call(body, in_specs=[SMEM] * len(first) + [VMEM] * (len(arrays)...  12.8 us
    all_to_all x1, waiting for transfers between devices, shards(): lax.all_to_all(merged, far, 0, 0, tiled=True)  12.6 us
    all_to_all x1, starting transfers between devices, shards(): lax.all_to_all(merged, far, 0, 0, tiled=True)  5 us
    pallas_call x2, Pallas kernels, probed(): pl.pallas_call(functools.partial(probe_body, first=first), in_specs=[pl.B...  3.82 us
  transfers between devices with their start and end apart: 12, of which 9 were waited for; matrix products, arithmetic and copies ran while one was open for 1% of the time, Pallas kernels for 4%

profile of v5, /device:TPU:56, one launch (start us, length us, event | category | flops | bytes accessed | tf_op | source)
XLA Modules:
  0.0 136.2 jit_solution(2472294926709143273)
XLA Ops:
  1.6 7.0 %collective-permute-start = (bf16[8,128,128]{2,1,0:T(8,128)(2,1)S(1)}, bf16[8,128,128]{2,1,0:T(8,128)(2,1)S(1)}, u32[]{:S(2)}, u32[]{:S(2)}) collective-permute-start(bf16[8,128,128]{2,1,0:T(8,128)(2,1)S(1)} %join.1.own), channel_id=1, source_target_pairs={{0,64},{64,128},{128,192},{192,256},{256,320},{320,384},{384,448},... | collective-permute-start | bytes 786440 | tf_op jit(solution)/shard_map/ppermute | solution.py:259
  8.7 1.9 %collective-permute-start.4 = (bf16[8,128,128]{2,1,0:T(8,128)(2,1)S(1)}, bf16[8,128,128]{2,1,0:T(8,128)(2,1)S(1)}, u32[]{:S(2)}, u32[]{:S(2)}) collective-permute-start(bf16[8,128,128]{2,1,0:T(8,128)(2,1)S(1)} %join.1.own), channel_id=1, source_target_pairs={{0,448},{64,0},{128,64},{192,128},{256,192},{320,256},{384,320},{4... | collective-permute-start | bytes 786440 | tf_op jit(solution)/shard_map/ppermute | solution.py:259
  11.2 1.9 %probe.2.probe_low = f32[2,2,128,128]{3,2,1,0:T(8,128)S(1)} custom-call(bf16[4,1024,256]{2,1,0:T(8,128)(2,1)} %left_ref.1, bf16[1024,256]{1,0:T(8,128)(2,1)} %sketch_any.3), custom_call_target="tpu_custom_call" | custom-call | tf_op jit(solution)/shard_map/probe/pallas_call | solution.py:282
  14.1 5.1 %collective-permute-start.1 = (bf16[8,128,128]{2,1,0:T(8,128)(2,1)S(1)}, bf16[8,128,128]{2,1,0:T(8,128)(2,1)S(1)}, u32[]{:S(2)}, u32[]{:S(2)}) collective-permute-start(bf16[8,128,128]{2,1,0:T(8,128)(2,1)S(1)} %collective-permute-done.f1), channel_id=1, source_target_pairs={{0,64},{64,128},{128,192},{192,256},{256,320},{320,384},{384,448},... | collective-permute-start | bytes 786440 | tf_op jit(solution)/shard_map/ppermute | solution.py:259
  19.2 1.9 %collective-permute-start.5 = (bf16[8,128,128]{2,1,0:T(8,128)(2,1)S(1)}, bf16[8,128,128]{2,1,0:T(8,128)(2,1)S(1)}, u32[]{:S(2)}, u32[]{:S(2)}) collective-permute-start(bf16[8,128,128]{2,1,0:T(8,128)(2,1)S(1)} %collective-permute-done.4.b1), channel_id=1, source_target_pairs={{0,448},{64,0},{128,64},{192,128},{256,192},{320,256},{384,320},{4... | collective-permute-start | bytes 786440 | tf_op jit(solution)/shard_map/ppermute | solution.py:259
  21.2 1.9 %probe.3.probe_high = f32[2,2,128,128]{3,2,1,0:T(8,128)S(1)} custom-call(bf16[4,1024,256]{2,1,0:T(8,128)(2,1)} %left_ref.1, bf16[1024,256]{1,0:T(8,128)(2,1)} %sketch_any.3), custom_call_target="tpu_custom_call" | custom-call | tf_op jit(solution)/shard_map/probe/pallas_call | solution.py:282
  24.0 5.6 %collective-permute-start.2 = (bf16[8,128,128]{2,1,0:T(8,128)(2,1)S(1)}, bf16[8,128,128]{2,1,0:T(8,128)(2,1)S(1)}, u32[]{:S(2)}, u32[]{:S(2)}) collective-permute-start(bf16[8,128,128]{2,1,0:T(8,128)(2,1)S(1)} %collective-permute-done.1.f2), channel_id=1, source_target_pairs={{0,64},{64,128},{128,192},{192,256},{256,320},{320,384},{384,448},... | collective-permute-start | bytes 786440 | tf_op jit(solution)/shard_map/ppermute | solution.py:259
  29.9 1.9 %collective-permute-start.6 = (bf16[8,128,128]{2,1,0:T(8,128)(2,1)S(1)}, bf16[8,128,128]{2,1,0:T(8,128)(2,1)S(1)}, u32[]{:S(2)}, u32[]{:S(2)}) collective-permute-start(bf16[8,128,128]{2,1,0:T(8,128)(2,1)S(1)} %collective-permute-done.5.b2), channel_id=1, source_target_pairs={{0,448},{64,0},{128,64},{192,128},{256,192},{320,256},{384,320},{4... | collective-permute-start | bytes 786440 | tf_op jit(solution)/shard_map/ppermute | solution.py:259
  31.8 3.1 %collective-permute-done.2.f3 = bf16[8,128,128]{2,1,0:T(8,128)(2,1)S(1)} collective-permute-done((bf16[8,128,128]{2,1,0:T(8,128)(2,1)S(1)}, bf16[8,128,128]{2,1,0:T(8,128)(2,1)S(1)}, u32[]{:S(2)}, u32[]{:S(2)}) %collective-permute-start.2) | collective-permute-done | bytes 262176 | tf_op jit(solution)/shard_map/ppermute | solution.py:259
  34.9 5.6 %collective-permute-start.3 = (bf16[4,128,128]{2,1,0:T(8,128)(2,1)S(1)}, bf16[4,128,128]{2,1,0:T(8,128)(2,1)S(1)}, u32[]{:S(2)}, u32[]{:S(2)}) collective-permute-start(bf16[4,128,128]{2,1,0:T(8,128)(2,1)S(1)} %slice.8), channel_id=1, source_target_pairs={{0,64},{64,128},{128,192},{192,256},{256,320},{320,384},{384,448},... | collective-permute-start | bytes 393224 | tf_op jit(solution)/shard_map/ppermute | solution.py:259
  40.7 1.9 %collective-permute-start.7 = (bf16[4,128,128]{2,1,0:T(8,128)(2,1)S(1)}, bf16[4,128,128]{2,1,0:T(8,128)(2,1)S(1)}, u32[]{:S(2)}, u32[]{:S(2)}) collective-permute-start(bf16[4,128,128]{2,1,0:T(8,128)(2,1)S(1)} %slice.9), channel_id=1, source_target_pairs={{0,448},{64,0},{128,64},{192,128},{256,192},{320,256},{384,320},{4... | collective-permute-start | bytes 393224 | tf_op jit(solution)/shard_map/ppermute | solution.py:259
  42.7 1.4 %early.1 = (f32[4,128,256]{2,1,0:T(8,128)S(1)}, bf16[1024,512]{1,0:T(8,128)(2,1)S(1)}) custom-call(s32[4]{0:T(128)S(1)} %pad_add_fusion.place_ref, bf16[8,128,128]{2,1,0:T(8,128)(2,1)S(1)} %join.1.own, bf16[8,128,128]{2,1,0:T(8,128)(2,1)S(1)} %collective-permute-done.f1, bf16[8,128,128]{2,1,0:T(8,128)(2,1)S(1)} %collective-permute-done.4.b1, ...), custom_call_target="tpu_custom_call" | custom-call | tf_op jit(solution)/shard_map/early/pallas_call | solution.py:268
  44.1 4.7 %collective-permute-done.7.b4 = bf16[4,128,128]{2,1,0:T(8,128)(2,1)S(1)} collective-permute-done((bf16[4,128,128]{2,1,0:T(8,128)(2,1)S(1)}, bf16[4,128,128]{2,1,0:T(8,128)(2,1)S(1)}, u32[]{:S(2)}, u32[]{:S(2)}) %collective-permute-start.7) | collective-permute-done | bytes 131104 | tf_op jit(solution)/shard_map/ppermute | solution.py:259
  48.8 2.0 %forward.1 = (f32[32,16,256]{2,1,0:T(8,128)S(1)}, bf16[32,16,256]{2,1,0:T(8,128)(2,1)S(1)}, f32[4,128,256]{2,1,0:T(8,128)S(1)}, bf16[32,16,128]{2,1,0:T(8,128)(2,1)S(1)}) custom-call(s32[4]{0:T(128)S(1)} %pad_add_fusion.place_ref, bf16[4,128,128]{2,1,0:T(8,128)(2,1)S(1)} %collective-permute-done.3.f4, bf16[4,128,128]{2,1,0:T(8,128)(2,1)S(1)} %collective-permute-done.7.b4, ...), custom_call_target="tpu_custom_call" | custom-call | tf_op jit(solution)/shard_map/forward/pallas_call | solution.py:268
  50.9 2.1 %collective-permute-start.8 = (bf16[32,16,256]{2,1,0:T(8,128)(2,1)S(1)}, bf16[32,16,256]{2,1,0:T(8,128)(2,1)S(1)}, u32[]{:S(2)}, u32[]{:S(2)}) collective-permute-start(bf16[32,16,256]{2,1,0:T(8,128)(2,1)S(1)} %get-tuple-element.33), channel_id=1, source_target_pairs={{0,1},{1,0},{2,3},{3,2},{4,5},{5,4},{6,7},{7,6},{8,9},{9,8},{10,11... | collective-permute-start | bytes 786440 | tf_op jit(solution)/shard_map/ppermute | solution.py:259
  52.9 1.5 %collective-permute-done.8.come_ref = bf16[32,16,256]{2,1,0:T(8,128)(2,1)S(1)} collective-permute-done((bf16[32,16,256]{2,1,0:T(8,128)(2,1)S(1)}, bf16[32,16,256]{2,1,0:T(8,128)(2,1)S(1)}, u32[]{:S(2)}, u32[]{:S(2)}) %collective-permute-start.8) | collective-permute-done | bytes 262176 | tf_op jit(solution)/shard_map/ppermute | solution.py:259
  54.5 23.1 %all_to_all.15.pieces_ref = bf16[32,16,384]{2,1,0:T(8,128)(2,1)S(1)} all-to-all(bf16[32,16,384]{2,1,0:T(8,128)(2,1)S(1)} %merge.1), channel_id=1, replica_groups=mesh['grp'=8,'inner_0'=8,'inner_1'=4,'inner_2'=2] {'inner_0','inner_1'}, dimensions={0} | all-to-all | bytes 786432 | tf_op jit(solution)/shard_map/all_to_all | solution.py:365
  77.7 23.6 %all_to_all.16.mine_ref = bf16[32,16,640]{2,1,0:T(8,128)(2,1)S(1)} all-to-all(bf16[32,16,640]{2,1,0:T(8,128)(2,1)S(1)} %get-tuple-element.35), channel_id=1, replica_groups=mesh['grp'=8,'inner_0'=8,'inner_1'=4,'inner_2'=2] {'inner_0','inner_1'}, dimensions={0} | all-to-all | bytes 1310720 | tf_op jit(solution)/shard_map/all_to_all | solution.py:368
  101.3 1.9 %collective-permute-start.9 = (bf16[32,16,640]{2,1,0:T(8,128)(2,1)S(1)}, bf16[32,16,640]{2,1,0:T(8,128)(2,1)S(1)}, u32[]{:S(2)}, u32[]{:S(2)}) collective-permute-start(bf16[32,16,640]{2,1,0:T(8,128)(2,1)S(1)} %all_to_all.16.mine_ref), channel_id=1, source_target_pairs={{0,1},{1,0},{2,3},{3,2},{4,5},{5,4},{6,7},{7,6},{8,9},{9,8},{10,11... | collective-permute-start | bytes 1966088 | tf_op jit(solution)/shard_map/ppermute | solution.py:259
  103.2 2.1 %collective-permute-done.9.other_ref = bf16[32,16,640]{2,1,0:T(8,128)(2,1)S(1)} collective-permute-done((bf16[32,16,640]{2,1,0:T(8,128)(2,1)S(1)}, bf16[32,16,640]{2,1,0:T(8,128)(2,1)S(1)}, u32[]{:S(2)}, u32[]{:S(2)}) %collective-permute-start.9) | collective-permute-done | bytes 655392 | tf_op jit(solution)/shard_map/ppermute | solution.py:259
  105.3 7.8 %backward.1 = (f32[16,256]{1,0:T(8,128)S(1)}, f32[32,16,256]{2,1,0:T(8,128)S(1)}, bf16[32,16,256]{2,1,0:T(8,128)(2,1)S(1)}, f32[16,256]{1,0:T(8,128)S(1)}) custom-call(s32[4]{0:T(128)S(1)} %pad_add_fusion.place_ref, bf16[32,16,640]{2,1,0:T(8,128)(2,1)S(1)} %all_to_all.16.mine_ref, bf16[32,16,640]{2,1,0:T(8,128)(2,1)S(1)} %collective-permute-done.9.other_ref, ...), custom_call_target="tpu_custom_call" | custom-call | tf_op jit(solution)/shard_map/backward/pallas_call | solution.py:268
  113.1 2.0 %collective-permute-start.10 = (bf16[32,16,256]{2,1,0:T(8,128)(2,1)S(1)}, bf16[32,16,256]{2,1,0:T(8,128)(2,1)S(1)}, u32[]{:S(2)}, u32[]{:S(2)}) collective-permute-start(bf16[32,16,256]{2,1,0:T(8,128)(2,1)S(1)} %get-tuple-element.40), channel_id=1, source_target_pairs={{0,1},{1,0},{2,3},{3,2},{4,5},{5,4},{6,7},{7,6},{8,9},{9,8},{10,11... | collective-permute-start | bytes 786440 | tf_op jit(solution)/shard_map/ppermute | solution.py:259
  117.3 5.0 %all-to-all-start.2 = ((bf16[32,16,256]{2,1,0:T(8,128)(2,1)}), bf16[32,16,256]{2,1,0:T(8,128)(2,1)S(1)}, u32[]{:S(2)}, u32[]{:S(2)}) async-start(bf16[32,16,256]{2,1,0:T(8,128)(2,1)} %add.19), calls=%async_computation.2 | async-start | bytes 524288 | tf_op jit(solution)/shard_map/all_to_all | solution.py:392
  122.9 12.6 %all-to-all-done.2.pieces_ref = bf16[32,16,256]{2,1,0:T(8,128)(2,1)S(1)} async-done(((bf16[32,16,256]{2,1,0:T(8,128)(2,1)}), bf16[32,16,256]{2,1,0:T(8,128)(2,1)S(1)}, u32[]{:S(2)}, u32[]{:S(2)}) %all-to-all-start.2) | async-done | bytes 262176 | tf_op jit(solution)/shard_map/all_to_all | solution.py:392
  (25 shorter events, 6.9 us)
Async XLA Ops:
  1.6 12.5 %collective-permute-start = (bf16[8,128,128]{2,1,0:T(8,128)(2,1)S(1)}, bf16[8,128,128]{2,1,0:T(8,128)(2,1)S(1)}, u32[]{:S(2)}, u32[]{:S(2)}) collective-permute-start(bf16[8,128,128]{2,1,0:T(8,128)(2,1)S(1)} %join.1.own), channel_id=1, source_target_pairs={{0,64},{64,128},{128,192},{192,256},{256,320},{320,384},{384,448},... | collective-permute-start | bytes 786440 | tf_op jit(solution)/shard_map/ppermute | solution.py:259
  8.7 10.6 %collective-permute-start.4 = (bf16[8,128,128]{2,1,0:T(8,128)(2,1)S(1)}, bf16[8,128,128]{2,1,0:T(8,128)(2,1)S(1)}, u32[]{:S(2)}, u32[]{:S(2)}) collective-permute-start(bf16[8,128,128]{2,1,0:T(8,128)(2,1)S(1)} %join.1.own), channel_id=1, source_target_pairs={{0,448},{64,0},{128,64},{192,128},{256,192},{320,256},{384,320},{4... | collective-permute-start | bytes 786440 | tf_op jit(solution)/shard_map/ppermute | solution.py:259
  13.2 29.5 %copy-start.1 = (bf16[4,1024,256]{2,1,0:T(8,128)(2,1)S(1)}, bf16[4,1024,256]{2,1,0:T(8,128)(2,1)}, u32[]{:S(2)}) copy-start(bf16[4,1024,256]{2,1,0:T(8,128)(2,1)} %right_ref.3) | copy-start | bytes 6291460
  14.1 9.9 %collective-permute-start.1 = (bf16[8,128,128]{2,1,0:T(8,128)(2,1)S(1)}, bf16[8,128,128]{2,1,0:T(8,128)(2,1)S(1)}, u32[]{:S(2)}, u32[]{:S(2)}) collective-permute-start(bf16[8,128,128]{2,1,0:T(8,128)(2,1)S(1)} %collective-permute-done.f1), channel_id=1, source_target_pairs={{0,64},{64,128},{128,192},{192,256},{256,320},{320,384},{384,448},... | collective-permute-start | bytes 786440 | tf_op jit(solution)/shard_map/ppermute | solution.py:259
  19.2 10.6 %collective-permute-start.5 = (bf16[8,128,128]{2,1,0:T(8,128)(2,1)S(1)}, bf16[8,128,128]{2,1,0:T(8,128)(2,1)S(1)}, u32[]{:S(2)}, u32[]{:S(2)}) collective-permute-start(bf16[8,128,128]{2,1,0:T(8,128)(2,1)S(1)} %collective-permute-done.4.b1), channel_id=1, source_target_pairs={{0,448},{64,0},{128,64},{192,128},{256,192},{320,256},{384,320},{4... | collective-permute-start | bytes 786440 | tf_op jit(solution)/shard_map/ppermute | solution.py:259
  24.0 10.9 %collective-permute-start.2 = (bf16[8,128,128]{2,1,0:T(8,128)(2,1)S(1)}, bf16[8,128,128]{2,1,0:T(8,128)(2,1)S(1)}, u32[]{:S(2)}, u32[]{:S(2)}) collective-permute-start(bf16[8,128,128]{2,1,0:T(8,128)(2,1)S(1)} %collective-permute-done.1.f2), channel_id=1, source_target_pairs={{0,64},{64,128},{128,192},{192,256},{256,320},{320,384},{384,448},... | collective-permute-start | bytes 786440 | tf_op jit(solution)/shard_map/ppermute | solution.py:259
  29.9 10.9 %collective-permute-start.6 = (bf16[8,128,128]{2,1,0:T(8,128)(2,1)S(1)}, bf16[8,128,128]{2,1,0:T(8,128)(2,1)S(1)}, u32[]{:S(2)}, u32[]{:S(2)}) collective-permute-start(bf16[8,128,128]{2,1,0:T(8,128)(2,1)S(1)} %collective-permute-done.5.b2), channel_id=1, source_target_pairs={{0,448},{64,0},{128,64},{192,128},{256,192},{320,256},{384,320},{4... | collective-permute-start | bytes 786440 | tf_op jit(solution)/shard_map/ppermute | solution.py:259
  34.8 14.0 %copy-start.2 = (bf16[16,256]{1,0:T(8,128)(2,1)S(1)}, bf16[16,256]{1,0:T(8,128)(2,1)}, u32[]{:S(2)}) copy-start(bf16[16,256]{1,0:T(8,128)(2,1)} %tright_ref.3) | copy-start | bytes 24580
  34.9 9.2 %collective-permute-start.3 = (bf16[4,128,128]{2,1,0:T(8,128)(2,1)S(1)}, bf16[4,128,128]{2,1,0:T(8,128)(2,1)S(1)}, u32[]{:S(2)}, u32[]{:S(2)}) collective-permute-start(bf16[4,128,128]{2,1,0:T(8,128)(2,1)S(1)} %slice.8), channel_id=1, source_target_pairs={{0,64},{64,128},{128,192},{192,256},{256,320},{320,384},{384,448},... | collective-permute-start | bytes 393224 | tf_op jit(solution)/shard_map/ppermute | solution.py:259
  40.7 8.1 %collective-permute-start.7 = (bf16[4,128,128]{2,1,0:T(8,128)(2,1)S(1)}, bf16[4,128,128]{2,1,0:T(8,128)(2,1)S(1)}, u32[]{:S(2)}, u32[]{:S(2)}) collective-permute-start(bf16[4,128,128]{2,1,0:T(8,128)(2,1)S(1)} %slice.9), channel_id=1, source_target_pairs={{0,448},{64,0},{128,64},{192,128},{256,192},{320,256},{384,320},{4... | collective-permute-start | bytes 393224 | tf_op jit(solution)/shard_map/ppermute | solution.py:259
  48.8 28.8 %copy-start.3 = (bf16[16,256]{1,0:T(8,128)(2,1)S(1)}, bf16[16,256]{1,0:T(8,128)(2,1)}, u32[]{:S(2)}) copy-start(bf16[16,256]{1,0:T(8,128)(2,1)} %tleft_ref.3) | copy-start | bytes 24580
  50.9 54.4 %copy-start = (bf16[4,1024,256]{2,1,0:T(8,128)(2,1)S(1)}, bf16[4,1024,256]{2,1,0:T(8,128)(2,1)}, u32[]{:S(2)}) copy-start(bf16[4,1024,256]{2,1,0:T(8,128)(2,1)} %left_ref.1) | copy-start | bytes 6291460
  50.9 3.6 %collective-permute-start.8 = (bf16[32,16,256]{2,1,0:T(8,128)(2,1)S(1)}, bf16[32,16,256]{2,1,0:T(8,128)(2,1)S(1)}, u32[]{:S(2)}, u32[]{:S(2)}) collective-permute-start(bf16[32,16,256]{2,1,0:T(8,128)(2,1)S(1)} %get-tuple-element.33), channel_id=1, source_target_pairs={{0,1},{1,0},{2,3},{3,2},{4,5},{5,4},{6,7},{7,6},{8,9},{9,8},{10,11... | collective-permute-start | bytes 786440 | tf_op jit(solution)/shard_map/ppermute | solution.py:259
  101.3 4.0 %collective-permute-start.9 = (bf16[32,16,640]{2,1,0:T(8,128)(2,1)S(1)}, bf16[32,16,640]{2,1,0:T(8,128)(2,1)S(1)}, u32[]{:S(2)}, u32[]{:S(2)}) collective-permute-start(bf16[32,16,640]{2,1,0:T(8,128)(2,1)S(1)} %all_to_all.16.mine_ref), channel_id=1, source_target_pairs={{0,1},{1,0},{2,3},{3,2},{4,5},{5,4},{6,7},{7,6},{8,9},{9,8},{10,11... | collective-permute-start | bytes 1966088 | tf_op jit(solution)/shard_map/ppermute | solution.py:259
  113.1 3.4 %collective-permute-start.10 = (bf16[32,16,256]{2,1,0:T(8,128)(2,1)S(1)}, bf16[32,16,256]{2,1,0:T(8,128)(2,1)S(1)}, u32[]{:S(2)}, u32[]{:S(2)}) collective-permute-start(bf16[32,16,256]{2,1,0:T(8,128)(2,1)S(1)} %get-tuple-element.40), channel_id=1, source_target_pairs={{0,1},{1,0},{2,3},{3,2},{4,5},{5,4},{6,7},{7,6},{8,9},{9,8},{10,11... | collective-permute-start | bytes 786440 | tf_op jit(solution)/shard_map/ppermute | solution.py:259
  117.3 18.3 %all-to-all-start.2 = ((bf16[32,16,256]{2,1,0:T(8,128)(2,1)}), bf16[32,16,256]{2,1,0:T(8,128)(2,1)S(1)}, u32[]{:S(2)}, u32[]{:S(2)}) async-start(bf16[32,16,256]{2,1,0:T(8,128)(2,1)} %add.19), calls=%async_computation.2 | async-start | bytes 524288 | tf_op jit(solution)/shard_map/all_to_all | solution.py:392

commit v6 on v5

--- a/solution.py
+++ b/solution.py
@@ -131,9 +131,10 @@
                 pivot_ref[pl.ds(at, n), cols] = ref[k + slots]
 
     put(own, 0)
+    odd = lax.rem(group, 2) == 1
     for s, (f, b) in enumerate(((f1, b1), (f2, b2), (f3, b3))):
-        put(f, groups - 1 - s)
-        put(b, 1 + s)
+        put(f, jnp.where(odd, groups - 1 - s, 1 + s))
+        put(b, jnp.where(odd, 1 + s, groups - 1 - s))
     put(None, groups // 2)
     for k in range(slots):
         pair_ref[k] = dot(factor[:, 128 * k : 128 * k + 128], right_ref[k], 0, 0)
@@ -259,6 +260,11 @@
     return lax.ppermute(x, axis, [(i, (i + by) % n) for i in range(n)])
 
 
+def paired(x, axis, first):
+    n = lax.axis_size(axis)
+    return lax.ppermute(x, axis, [(i, (i + 1 - 2 * ((i + first) % 2)) % n) for i in range(n)])
+
+
 def near(x):
     return pltpu.with_memory_space_constraint(x, pltpu.VMEM)
 
@@ -313,21 +319,22 @@
         name="join",
         compiler_params=pltpu.CompilerParams(vmem_limit_bytes=24 << 20),
     )(*(pltpu.with_memory_space_constraint(x, pltpu.HBM) for x in (row_right, row_left)))
-    chunks, probes, up, down = [own], [], own, own
+    chunks, probes, here, there = [own], [], own, own
     for step in range(3):
-        up, down = shift(up, "grp", 1), shift(down, "grp", -1)
+        here, there = paired(here, "grp", 0), paired(there, "grp", 1)
         if step == 0:
             own_sketch = lax.dynamic_slice_in_dim(
                 sketch_cols, lax.axis_index(INNER) * block, block, 0
             )
         if step < 2:
             probe = probed(col_left, sketch_cols, step * (slots // 2), slots // 2)
-            up, probe, own_sketch, place = lax.optimization_barrier(
-                (up, probe, own_sketch, place)
+            here, probe, own_sketch, place = lax.optimization_barrier(
+                (here, probe, own_sketch, place)
             )
             probes.append(probe)
-        chunks += [up, down]
-    last_up, last_down = shift(up[:slots], "grp", 1), shift(down[slots:], "grp", -1)
+        chunks += [here, there]
+        here, there = there, here
+    last_right, last_left = paired(here[:slots], "grp", 0), paired(there[slots:], "grp", 1)
     early, pivot = kernel(
         early_body,
         "early",
@@ -344,8 +351,8 @@
         [(piece, FULL), (piece, LOW), ((slots, 128, width), FULL), ((half, block, 128), LOW)],
         [((rows, width), FULL)],
         place,
-        last_up,
-        last_down,
+        last_right,
+        last_left,
         early,
         pivot,
         *probes,
@@ -376,7 +383,7 @@
         mine,
         other,
         own_sum,
-        last_down,
+        last_left,
         pivot,
         pair,
         given=(target_left, target_right, col_left),

time: 139 us -> 139 us (level); the launches traced: 136 us -> 139 us
  starting transfers between devices: 42 us -> 37 us
  waiting for transfers between devices: 26.8 us -> 31.7 us
  blocking collectives: 46.7 us -> 49.5 us
    ppermute x11 -> x3, starting transfers between devices: 37 us -> 6.01 us  [shift(): return lax.ppermute(x, axis, [(i, (i + by) % n) for i in range(n)])]
    ppermute x0 -> x8, starting transfers between devices: none -> 26 us  [paired(): lax.ppermute(x, axis, [(i, (i + 1 - 2 * ((i + first) % 2)) % n) for i in...]
    ppermute x0 -> x8, waiting for transfers between devices: none -> 14.2 us  [paired(): lax.ppermute(x, axis, [(i, (i + 1 - 2 * ((i + first) % 2)) % n) for i in...]
    ppermute x11 -> x3, waiting for transfers between devices: 14.2 us -> 4.94 us  [shift(): return lax.ppermute(x, axis, [(i, (i + by) % n) for i in range(n)])]
    all_to_all x1, blocking collectives: 23.1 us -> 25.9 us  [shards(): lax.all_to_all(merged, far, 0, 0, tiled=True)]
  transfers between devices with their start and end apart: 12 -> 12, of which waited for: 9 -> 10; matrix products, arithmetic and copies ran while one was open for 1% -> 1% of each run, Pallas kernels for 4% -> 4%
where the time goes in v6:
time: 139 us
  blocking collectives  49.5 us (36%)
  starting transfers between devices  37 us (27%)
  waiting for transfers between devices  31.7 us (23%)
  Pallas kernels  17.6 us (13%)
  between operations  1.5 us (1%)
    ppermute x8, starting transfers between devices, paired(): lax.ppermute(x, axis, [(i, (i + 1 - 2 * ((i + first) % 2)) % n) for i in...  26 us
    all_to_all x1, blocking collectives, shards(): lax.all_to_all(merged, far, 0, 0, tiled=True)  25.9 us
    all_to_all x1, blocking collectives, shards(): mine = lax.all_to_all(mine, far, 0, 0, tiled=True)  23.6 us
    ppermute x8, waiting for transfers between devices, paired(): lax.ppermute(x, axis, [(i, (i + 1 - 2 * ((i + first) % 2)) % n) for i in...  14.2 us
    pallas_call x7, Pallas kernels, kernel(): pl.pallas_call(body, in_specs=[SMEM] * len(first) + [VMEM] * (len(arrays)...  12.8 us
    all_to_all x1, waiting for transfers between devices, shards(): lax.all_to_all(merged, far, 0, 0, tiled=True)  12.6 us
    ppermute x3, starting transfers between devices, shift(): return lax.ppermute(x, axis, [(i, (i + by) % n) for i in range(n)])  6.01 us
    all_to_all x1, starting transfers between devices, shards(): lax.all_to_all(merged, far, 0, 0, tiled=True)  5 us
  transfers between devices with their start and end apart: 12, of which 10 were waited for; matrix products, arithmetic and copies ran while one was open for 1% of the time, Pallas kernels for 4%

profile of v6, /device:TPU:56, one launch (start us, length us, event | category | flops | bytes accessed | tf_op | source)
XLA Modules:
  0.0 138.7 jit_solution(3039943848188850232)
XLA Ops:
  1.6 7.0 %collective-permute-start = (bf16[8,128,128]{2,1,0:T(8,128)(2,1)S(1)}, bf16[8,128,128]{2,1,0:T(8,128)(2,1)S(1)}, u32[]{:S(2)}, u32[]{:S(2)}) collective-permute-start(bf16[8,128,128]{2,1,0:T(8,128)(2,1)S(1)} %join.1.own), channel_id=1, source_target_pairs={{0,448},{64,128},{128,64},{192,256},{256,192},{320,384},{384,320},... | collective-permute-start | bytes 786440 | tf_op jit(solution)/shard_map/ppermute | solution.py:265
  8.7 1.9 %collective-permute-start.2 = (bf16[8,128,128]{2,1,0:T(8,128)(2,1)S(1)}, bf16[8,128,128]{2,1,0:T(8,128)(2,1)S(1)}, u32[]{:S(2)}, u32[]{:S(2)}) collective-permute-start(bf16[8,128,128]{2,1,0:T(8,128)(2,1)S(1)} %join.1.own), channel_id=1, source_target_pairs={{0,64},{64,0},{128,192},{192,128},{256,320},{320,256},{384,448},{4... | collective-permute-start | bytes 786440 | tf_op jit(solution)/shard_map/ppermute | solution.py:265
  13.0 2.9 %collective-permute-start.1 = (bf16[8,128,128]{2,1,0:T(8,128)(2,1)S(1)}, bf16[8,128,128]{2,1,0:T(8,128)(2,1)S(1)}, u32[]{:S(2)}, u32[]{:S(2)}) collective-permute-start(bf16[8,128,128]{2,1,0:T(8,128)(2,1)S(1)} %collective-permute-done.b1), channel_id=1, source_target_pairs={{0,64},{64,0},{128,192},{192,128},{256,320},{320,256},{384,448},{4... | collective-permute-start | bytes 786440 | tf_op jit(solution)/shard_map/ppermute | solution.py:265
  15.9 1.9 %probe.3.probe_low = f32[2,2,128,128]{3,2,1,0:T(8,128)S(1)} custom-call(bf16[4,1024,256]{2,1,0:T(8,128)(2,1)} %left_ref.1, bf16[1024,256]{1,0:T(8,128)(2,1)} %sketch_any.3), custom_call_target="tpu_custom_call" | custom-call | tf_op jit(solution)/shard_map/probe/pallas_call | solution.py:288
  19.2 3.0 %collective-permute-start.5 = (bf16[8,128,128]{2,1,0:T(8,128)(2,1)S(1)}, bf16[8,128,128]{2,1,0:T(8,128)(2,1)S(1)}, u32[]{:S(2)}, u32[]{:S(2)}) collective-permute-start(bf16[8,128,128]{2,1,0:T(8,128)(2,1)S(1)} %collective-permute-done.2.f1), channel_id=1, source_target_pairs={{0,448},{64,128},{128,64},{192,256},{256,192},{320,384},{384,320},... | collective-permute-start | bytes 786440 | tf_op jit(solution)/shard_map/ppermute | solution.py:265
  22.2 1.9 %probe.2.probe_high = f32[2,2,128,128]{3,2,1,0:T(8,128)S(1)} custom-call(bf16[4,1024,256]{2,1,0:T(8,128)(2,1)} %left_ref.1, bf16[1024,256]{1,0:T(8,128)(2,1)} %sketch_any.3), custom_call_target="tpu_custom_call" | custom-call | tf_op jit(solution)/shard_map/probe/pallas_call | solution.py:288
  24.1 4.1 %collective-permute-start.3 = (bf16[8,128,128]{2,1,0:T(8,128)(2,1)S(1)}, bf16[8,128,128]{2,1,0:T(8,128)(2,1)S(1)}, u32[]{:S(2)}, u32[]{:S(2)}) collective-permute-start(bf16[8,128,128]{2,1,0:T(8,128)(2,1)S(1)} %collective-permute-done.1.f2), channel_id=1, source_target_pairs={{0,448},{64,128},{128,64},{192,256},{256,192},{320,384},{384,320},... | collective-permute-start | bytes 786440 | tf_op jit(solution)/shard_map/ppermute | solution.py:265
  28.2 3.1 %collective-permute-done.5.b2 = bf16[8,128,128]{2,1,0:T(8,128)(2,1)S(1)} collective-permute-done((bf16[8,128,128]{2,1,0:T(8,128)(2,1)S(1)}, bf16[8,128,128]{2,1,0:T(8,128)(2,1)S(1)}, u32[]{:S(2)}, u32[]{:S(2)}) %collective-permute-start.5) | collective-permute-done | bytes 262176 | tf_op jit(solution)/shard_map/ppermute | solution.py:265
  31.3 1.9 %collective-permute-start.6 = (bf16[8,128,128]{2,1,0:T(8,128)(2,1)S(1)}, bf16[8,128,128]{2,1,0:T(8,128)(2,1)S(1)}, u32[]{:S(2)}, u32[]{:S(2)}) collective-permute-start(bf16[8,128,128]{2,1,0:T(8,128)(2,1)S(1)} %collective-permute-done.5.b2), channel_id=1, source_target_pairs={{0,64},{64,0},{128,192},{192,128},{256,320},{320,256},{384,448},{4... | collective-permute-start | bytes 786440 | tf_op jit(solution)/shard_map/ppermute | solution.py:265
  34.3 2.8 %collective-permute-start.4 = (bf16[4,128,128]{2,1,0:T(8,128)(2,1)S(1)}, bf16[4,128,128]{2,1,0:T(8,128)(2,1)S(1)}, u32[]{:S(2)}, u32[]{:S(2)}) collective-permute-start(bf16[4,128,128]{2,1,0:T(8,128)(2,1)S(1)} %slice.8), channel_id=1, source_target_pairs={{0,64},{64,0},{128,192},{192,128},{256,320},{320,256},{384,448},{4... | collective-permute-start | bytes 393224 | tf_op jit(solution)/shard_map/ppermute | solution.py:265
  37.2 3.3 %collective-permute-done.6.f3 = bf16[8,128,128]{2,1,0:T(8,128)(2,1)S(1)} collective-permute-done((bf16[8,128,128]{2,1,0:T(8,128)(2,1)S(1)}, bf16[8,128,128]{2,1,0:T(8,128)(2,1)S(1)}, u32[]{:S(2)}, u32[]{:S(2)}) %collective-permute-start.6) | collective-permute-done | bytes 262176 | tf_op jit(solution)/shard_map/ppermute | solution.py:265
  40.5 2.4 %collective-permute-start.7 = (bf16[4,128,128]{2,1,0:T(8,128)(2,1)S(1)}, bf16[4,128,128]{2,1,0:T(8,128)(2,1)S(1)}, u32[]{:S(2)}, u32[]{:S(2)}) collective-permute-start(bf16[4,128,128]{2,1,0:T(8,128)(2,1)S(1)} %slice.9), channel_id=1, source_target_pairs={{0,448},{64,128},{128,64},{192,256},{256,192},{320,384},{384,320},... | collective-permute-start | bytes 393224 | tf_op jit(solution)/shard_map/ppermute | solution.py:265
  44.3 4.3 %collective-permute-done.7.b4 = bf16[4,128,128]{2,1,0:T(8,128)(2,1)S(1)} collective-permute-done((bf16[4,128,128]{2,1,0:T(8,128)(2,1)S(1)}, bf16[4,128,128]{2,1,0:T(8,128)(2,1)S(1)}, u32[]{:S(2)}, u32[]{:S(2)}) %collective-permute-start.7) | collective-permute-done | bytes 131104 | tf_op jit(solution)/shard_map/ppermute | solution.py:265
  48.6 2.0 %forward.1 = (f32[32,16,256]{2,1,0:T(8,128)S(1)}, bf16[32,16,256]{2,1,0:T(8,128)(2,1)S(1)}, f32[4,128,256]{2,1,0:T(8,128)S(1)}, bf16[32,16,128]{2,1,0:T(8,128)(2,1)S(1)}) custom-call(s32[4]{0:T(128)S(1)} %pad_add_fusion.place_ref, bf16[4,128,128]{2,1,0:T(8,128)(2,1)S(1)} %collective-permute-done.4.f4, bf16[4,128,128]{2,1,0:T(8,128)(2,1)S(1)} %collective-permute-done.7.b4, ...), custom_call_target="tpu_custom_call" | custom-call | tf_op jit(solution)/shard_map/forward/pallas_call | solution.py:274
  50.7 2.1 %collective-permute-start.8 = (bf16[32,16,256]{2,1,0:T(8,128)(2,1)S(1)}, bf16[32,16,256]{2,1,0:T(8,128)(2,1)S(1)}, u32[]{:S(2)}, u32[]{:S(2)}) collective-permute-start(bf16[32,16,256]{2,1,0:T(8,128)(2,1)S(1)} %get-tuple-element.33), channel_id=1, source_target_pairs={{0,1},{1,0},{2,3},{3,2},{4,5},{5,4},{6,7},{7,6},{8,9},{9,8},{10,11... | collective-permute-start | bytes 786440 | tf_op jit(solution)/shard_map/ppermute | solution.py:260
  52.7 1.5 %collective-permute-done.8.come_ref = bf16[32,16,256]{2,1,0:T(8,128)(2,1)S(1)} collective-permute-done((bf16[32,16,256]{2,1,0:T(8,128)(2,1)S(1)}, bf16[32,16,256]{2,1,0:T(8,128)(2,1)S(1)}, u32[]{:S(2)}, u32[]{:S(2)}) %collective-permute-start.8) | collective-permute-done | bytes 262176 | tf_op jit(solution)/shard_map/ppermute | solution.py:260
  54.3 25.9 %all_to_all.15.pieces_ref = bf16[32,16,384]{2,1,0:T(8,128)(2,1)S(1)} all-to-all(bf16[32,16,384]{2,1,0:T(8,128)(2,1)S(1)} %merge.1), channel_id=1, replica_groups=mesh['grp'=8,'inner_0'=8,'inner_1'=4,'inner_2'=2] {'inner_0','inner_1'}, dimensions={0} | all-to-all | bytes 786432 | tf_op jit(solution)/shard_map/all_to_all | solution.py:372
  80.3 23.6 %all_to_all.16.mine_ref = bf16[32,16,640]{2,1,0:T(8,128)(2,1)S(1)} all-to-all(bf16[32,16,640]{2,1,0:T(8,128)(2,1)S(1)} %get-tuple-element.35), channel_id=1, replica_groups=mesh['grp'=8,'inner_0'=8,'inner_1'=4,'inner_2'=2] {'inner_0','inner_1'}, dimensions={0} | all-to-all | bytes 1310720 | tf_op jit(solution)/shard_map/all_to_all | solution.py:375
  103.8 1.9 %collective-permute-start.9 = (bf16[32,16,640]{2,1,0:T(8,128)(2,1)S(1)}, bf16[32,16,640]{2,1,0:T(8,128)(2,1)S(1)}, u32[]{:S(2)}, u32[]{:S(2)}) collective-permute-start(bf16[32,16,640]{2,1,0:T(8,128)(2,1)S(1)} %all_to_all.16.mine_ref), channel_id=1, source_target_pairs={{0,1},{1,0},{2,3},{3,2},{4,5},{5,4},{6,7},{7,6},{8,9},{9,8},{10,11... | collective-permute-start | bytes 1966088 | tf_op jit(solution)/shard_map/ppermute | solution.py:260
  105.8 2.1 %collective-permute-done.9.other_ref = bf16[32,16,640]{2,1,0:T(8,128)(2,1)S(1)} collective-permute-done((bf16[32,16,640]{2,1,0:T(8,128)(2,1)S(1)}, bf16[32,16,640]{2,1,0:T(8,128)(2,1)S(1)}, u32[]{:S(2)}, u32[]{:S(2)}) %collective-permute-start.9) | collective-permute-done | bytes 655392 | tf_op jit(solution)/shard_map/ppermute | solution.py:260
  107.8 7.8 %backward.1 = (f32[16,256]{1,0:T(8,128)S(1)}, f32[32,16,256]{2,1,0:T(8,128)S(1)}, bf16[32,16,256]{2,1,0:T(8,128)(2,1)S(1)}, f32[16,256]{1,0:T(8,128)S(1)}) custom-call(s32[4]{0:T(128)S(1)} %pad_add_fusion.place_ref, bf16[32,16,640]{2,1,0:T(8,128)(2,1)S(1)} %all_to_all.16.mine_ref, bf16[32,16,640]{2,1,0:T(8,128)(2,1)S(1)} %collective-permute-done.9.other_ref, ...), custom_call_target="tpu_custom_call" | custom-call | tf_op jit(solution)/shard_map/backward/pallas_call | solution.py:274
  115.6 2.0 %collective-permute-start.10 = (bf16[32,16,256]{2,1,0:T(8,128)(2,1)S(1)}, bf16[32,16,256]{2,1,0:T(8,128)(2,1)S(1)}, u32[]{:S(2)}, u32[]{:S(2)}) collective-permute-start(bf16[32,16,256]{2,1,0:T(8,128)(2,1)S(1)} %get-tuple-element.40), channel_id=1, source_target_pairs={{0,1},{1,0},{2,3},{3,2},{4,5},{5,4},{6,7},{7,6},{8,9},{9,8},{10,11... | collective-permute-start | bytes 786440 | tf_op jit(solution)/shard_map/ppermute | solution.py:260
  119.8 5.0 %all-to-all-start.2 = ((bf16[32,16,256]{2,1,0:T(8,128)(2,1)}), bf16[32,16,256]{2,1,0:T(8,128)(2,1)S(1)}, u32[]{:S(2)}, u32[]{:S(2)}) async-start(bf16[32,16,256]{2,1,0:T(8,128)(2,1)} %add.19), calls=%async_computation.2 | async-start | bytes 524288 | tf_op jit(solution)/shard_map/all_to_all | solution.py:399
  125.5 12.6 %all-to-all-done.2.pieces_ref = bf16[32,16,256]{2,1,0:T(8,128)(2,1)S(1)} async-done(((bf16[32,16,256]{2,1,0:T(8,128)(2,1)}), bf16[32,16,256]{2,1,0:T(8,128)(2,1)S(1)}, u32[]{:S(2)}, u32[]{:S(2)}) %all-to-all-start.2) | async-done | bytes 262176 | tf_op jit(solution)/shard_map/all_to_all | solution.py:399
  (25 shorter events, 10.2 us)
Async XLA Ops:
  1.6 11.4 %collective-permute-start = (bf16[8,128,128]{2,1,0:T(8,128)(2,1)S(1)}, bf16[8,128,128]{2,1,0:T(8,128)(2,1)S(1)}, u32[]{:S(2)}, u32[]{:S(2)}) collective-permute-start(bf16[8,128,128]{2,1,0:T(8,128)(2,1)S(1)} %join.1.own), channel_id=1, source_target_pairs={{0,448},{64,128},{128,64},{192,256},{256,192},{320,384},{384,320},... | collective-permute-start | bytes 786440 | tf_op jit(solution)/shard_map/ppermute | solution.py:265
  8.7 10.5 %collective-permute-start.2 = (bf16[8,128,128]{2,1,0:T(8,128)(2,1)S(1)}, bf16[8,128,128]{2,1,0:T(8,128)(2,1)S(1)}, u32[]{:S(2)}, u32[]{:S(2)}) collective-permute-start(bf16[8,128,128]{2,1,0:T(8,128)(2,1)S(1)} %join.1.own), channel_id=1, source_target_pairs={{0,64},{64,0},{128,192},{192,128},{256,320},{320,256},{384,448},{4... | collective-permute-start | bytes 786440 | tf_op jit(solution)/shard_map/ppermute | solution.py:265
  13.0 11.1 %collective-permute-start.1 = (bf16[8,128,128]{2,1,0:T(8,128)(2,1)S(1)}, bf16[8,128,128]{2,1,0:T(8,128)(2,1)S(1)}, u32[]{:S(2)}, u32[]{:S(2)}) collective-permute-start(bf16[8,128,128]{2,1,0:T(8,128)(2,1)S(1)} %collective-permute-done.b1), channel_id=1, source_target_pairs={{0,64},{64,0},{128,192},{192,128},{256,320},{320,256},{384,448},{4... | collective-permute-start | bytes 786440 | tf_op jit(solution)/shard_map/ppermute | solution.py:265
  17.9 25.1 %copy-start.1 = (bf16[4,1024,256]{2,1,0:T(8,128)(2,1)S(1)}, bf16[4,1024,256]{2,1,0:T(8,128)(2,1)}, u32[]{:S(2)}) copy-start(bf16[4,1024,256]{2,1,0:T(8,128)(2,1)} %right_ref.3) | copy-start | bytes 6291460
  19.2 12.1 %collective-permute-start.5 = (bf16[8,128,128]{2,1,0:T(8,128)(2,1)S(1)}, bf16[8,128,128]{2,1,0:T(8,128)(2,1)S(1)}, u32[]{:S(2)}, u32[]{:S(2)}) collective-permute-start(bf16[8,128,128]{2,1,0:T(8,128)(2,1)S(1)} %collective-permute-done.2.f1), channel_id=1, source_target_pairs={{0,448},{64,128},{128,64},{192,256},{256,192},{320,384},{384,320},... | collective-permute-start | bytes 786440 | tf_op jit(solution)/shard_map/ppermute | solution.py:265
  24.1 10.2 %collective-permute-start.3 = (bf16[8,128,128]{2,1,0:T(8,128)(2,1)S(1)}, bf16[8,128,128]{2,1,0:T(8,128)(2,1)S(1)}, u32[]{:S(2)}, u32[]{:S(2)}) collective-permute-start(bf16[8,128,128]{2,1,0:T(8,128)(2,1)S(1)} %collective-permute-done.1.f2), channel_id=1, source_target_pairs={{0,448},{64,128},{128,64},{192,256},{256,192},{320,384},{384,320},... | collective-permute-start | bytes 786440 | tf_op jit(solution)/shard_map/ppermute | solution.py:265
  31.3 9.2 %collective-permute-start.6 = (bf16[8,128,128]{2,1,0:T(8,128)(2,1)S(1)}, bf16[8,128,128]{2,1,0:T(8,128)(2,1)S(1)}, u32[]{:S(2)}, u32[]{:S(2)}) collective-permute-start(bf16[8,128,128]{2,1,0:T(8,128)(2,1)S(1)} %collective-permute-done.5.b2), channel_id=1, source_target_pairs={{0,64},{64,0},{128,192},{192,128},{256,320},{320,256},{384,448},{4... | collective-permute-start | bytes 786440 | tf_op jit(solution)/shard_map/ppermute | solution.py:265
  34.3 14.3 %copy-start.2 = (bf16[16,256]{1,0:T(8,128)(2,1)S(1)}, bf16[16,256]{1,0:T(8,128)(2,1)}, u32[]{:S(2)}) copy-start(bf16[16,256]{1,0:T(8,128)(2,1)} %tright_ref.3) | copy-start | bytes 24580
  34.3 10.0 %collective-permute-start.4 = (bf16[4,128,128]{2,1,0:T(8,128)(2,1)S(1)}, bf16[4,128,128]{2,1,0:T(8,128)(2,1)S(1)}, u32[]{:S(2)}, u32[]{:S(2)}) collective-permute-start(bf16[4,128,128]{2,1,0:T(8,128)(2,1)S(1)} %slice.8), channel_id=1, source_target_pairs={{0,64},{64,0},{128,192},{192,128},{256,320},{320,256},{384,448},{4... | collective-permute-start | bytes 393224 | tf_op jit(solution)/shard_map/ppermute | solution.py:265
  40.5 8.1 %collective-permute-start.7 = (bf16[4,128,128]{2,1,0:T(8,128)(2,1)S(1)}, bf16[4,128,128]{2,1,0:T(8,128)(2,1)S(1)}, u32[]{:S(2)}, u32[]{:S(2)}) collective-permute-start(bf16[4,128,128]{2,1,0:T(8,128)(2,1)S(1)} %slice.9), channel_id=1, source_target_pairs={{0,448},{64,128},{128,64},{192,256},{256,192},{320,384},{384,320},... | collective-permute-start | bytes 393224 | tf_op jit(solution)/shard_map/ppermute | solution.py:265
  48.6 31.6 %copy-start.3 = (bf16[16,256]{1,0:T(8,128)(2,1)S(1)}, bf16[16,256]{1,0:T(8,128)(2,1)}, u32[]{:S(2)}) copy-start(bf16[16,256]{1,0:T(8,128)(2,1)} %tleft_ref.3) | copy-start | bytes 24580
  50.6 57.2 %copy-start = (bf16[4,1024,256]{2,1,0:T(8,128)(2,1)S(1)}, bf16[4,1024,256]{2,1,0:T(8,128)(2,1)}, u32[]{:S(2)}) copy-start(bf16[4,1024,256]{2,1,0:T(8,128)(2,1)} %left_ref.1) | copy-start | bytes 6291460
  50.7 3.6 %collective-permute-start.8 = (bf16[32,16,256]{2,1,0:T(8,128)(2,1)S(1)}, bf16[32,16,256]{2,1,0:T(8,128)(2,1)S(1)}, u32[]{:S(2)}, u32[]{:S(2)}) collective-permute-start(bf16[32,16,256]{2,1,0:T(8,128)(2,1)S(1)} %get-tuple-element.33), channel_id=1, source_target_pairs={{0,1},{1,0},{2,3},{3,2},{4,5},{5,4},{6,7},{7,6},{8,9},{9,8},{10,11... | collective-permute-start | bytes 786440 | tf_op jit(solution)/shard_map/ppermute | solution.py:260
  103.8 4.0 %collective-permute-start.9 = (bf16[32,16,640]{2,1,0:T(8,128)(2,1)S(1)}, bf16[32,16,640]{2,1,0:T(8,128)(2,1)S(1)}, u32[]{:S(2)}, u32[]{:S(2)}) collective-permute-start(bf16[32,16,640]{2,1,0:T(8,128)(2,1)S(1)} %all_to_all.16.mine_ref), channel_id=1, source_target_pairs={{0,1},{1,0},{2,3},{3,2},{4,5},{5,4},{6,7},{7,6},{8,9},{9,8},{10,11... | collective-permute-start | bytes 1966088 | tf_op jit(solution)/shard_map/ppermute | solution.py:260
  115.6 3.4 %collective-permute-start.10 = (bf16[32,16,256]{2,1,0:T(8,128)(2,1)S(1)}, bf16[32,16,256]{2,1,0:T(8,128)(2,1)S(1)}, u32[]{:S(2)}, u32[]{:S(2)}) collective-permute-start(bf16[32,16,256]{2,1,0:T(8,128)(2,1)S(1)} %get-tuple-element.40), channel_id=1, source_target_pairs={{0,1},{1,0},{2,3},{3,2},{4,5},{5,4},{6,7},{7,6},{8,9},{9,8},{10,11... | collective-permute-start | bytes 786440 | tf_op jit(solution)/shard_map/ppermute | solution.py:260
  119.8 18.3 %all-to-all-start.2 = ((bf16[32,16,256]{2,1,0:T(8,128)(2,1)}), bf16[32,16,256]{2,1,0:T(8,128)(2,1)S(1)}, u32[]{:S(2)}, u32[]{:S(2)}) async-start(bf16[32,16,256]{2,1,0:T(8,128)(2,1)} %add.19), calls=%async_computation.2 | async-start | bytes 524288 | tf_op jit(solution)/shard_map/all_to_all | solution.py:399

commit v7 on v5

--- a/solution.py
+++ b/solution.py
@@ -98,7 +98,9 @@
         c.wait()
 
 
-def probe_body(left_any, sketch_any, out_ref, left_ref, sketch_ref, sems, *, first):
+def probe_body(
+    place_ref, left_any, sketch_any, out_ref, own_ref, left_ref, sketch_ref, sems, *, first
+):
     count = out_ref.shape[0]
     copies = [pltpu.make_async_copy(sketch_any, sketch_ref, sems.at[count])]
     for k in range(count):
@@ -108,6 +110,8 @@
     for c in copies:
         c.start()
     copies[0].wait()
+    lines = own_ref.shape[0]
+    own_ref[...] = sketch_ref[pl.ds(pl.multiple_of(place_ref[4] * lines, lines), lines), :]
     for k in range(count):
         copies[1 + k].wait()
         for t in range(2):
@@ -139,9 +143,34 @@
         pair_ref[k] = dot(factor[:, 128 * k : 128 * k + 128], right_ref[k], 0, 0)
 
 
+def upper_lines(shape):
+    return lax.broadcasted_iota(jnp.int32, shape, 1) < 4
+
+
+def packed(x):
+    x = x.reshape(16, 8, 128)
+    high = x.astype(LOW).astype(FULL)
+    low, top = x - high, upper_lines(x.shape)
+    even = jnp.where(top, high, pltpu.roll(low, 4, 1))
+    odd = jnp.where(top, pltpu.roll(high, 4, 1), low)
+    return jnp.concatenate([even[:, None], odd[:, None]], 1).reshape(32, 8, 128)
+
+
+def repacked(x):
+    total = x + pltpu.roll(x, 4, 1)
+    high = total.astype(LOW).astype(FULL)
+    return jnp.where(upper_lines(x.shape), high, total - high)
+
+
+def unpacked(x):
+    total = (x + pltpu.roll(x, 4, 1)).reshape(16, 2, 8, 128)
+    even, odd = total[:, 0], total[:, 1]
+    return jnp.where(upper_lines(even.shape), even, odd).reshape(128, 128)
+
+
 def forward_body(
     place_ref, f4, b4, early_ref, pivot_ref, probe_low, probe_high, sketch_ref, right_ref, tright_ref,
-    keep_ref, send_ref, pair_ref, core_ref, part,
+    keep_ref, send_ref, pair_ref, part,
 ):
     group, live, groups, core = place_ref[0], place_ref[1], place_ref[2], place_ref[3]
     slots, n, half = right_ref.shape[0], f4.shape[1], keep_ref.shape[0]
@@ -165,10 +194,13 @@
         dot(tright_ref[:, 128 * t : 128 * t + 128], sketch_ref[:, 128 * t : 128 * t + 128], 0, 0)
         for t in range(2)
     ]
-    core_ref[...] = jnp.concatenate(halves(jnp.concatenate(cores, 0).reshape(half, 8, 128)), 1)
-    whole = part[...].reshape(half, 2, 16, part.shape[1])
-    keep_ref[...] = jnp.where(core == 0, whole[:, 0], whole[:, 1])
-    send_ref[...] = jnp.where(core == 0, whole[:, 1], whole[:, 0]).astype(LOW)
+    for t in range(2):
+        whole = part[:, 128 * t : 128 * t + 128].reshape(half, 2, 16, 128)
+        lines = slice(16 * t, 16 * t + 16)
+        keep_ref[:, lines] = jnp.where(core == 0, whole[:, 0], whole[:, 1])
+        send_ref[:, lines] = jnp.where(core == 0, whole[:, 1], whole[:, 0]).astype(LOW)
+    keep_ref[:, 32:] = packed(jnp.where(core == 0, cores[0], cores[1]))
+    send_ref[:, 32:] = packed(jnp.where(core == 0, cores[1], cores[0])).astype(LOW)
 
 
 def add_body(keep_ref, come_ref, out_ref):
@@ -179,19 +211,25 @@
     out_ref[...] = (jnp.sum(pieces_ref[...].astype(FULL), 0) + direct_ref[...]) / rows
 
 
-def merge_body(keep_ref, come_ref, core_ref, out_ref):
-    width = keep_ref.shape[2]
-    out_ref[:, :, :width] = (keep_ref[...] + come_ref[...].astype(FULL)).astype(LOW)
-    out_ref[:, :, width:] = core_ref[...]
+def merge_body(keep_ref, come_ref, out_ref):
+    total = keep_ref[...] + come_ref[...].astype(FULL)
+    out_ref[:, :32] = total[:, :32].astype(LOW)
+    out_ref[:, 32:] = repacked(total[:, 32:]).astype(LOW)
 
 
 def own_body(pieces_ref, tleft_ref, sum_ref, out_ref):
-    width = sum_ref.shape[1]
     total = jnp.sum(pieces_ref[...].astype(FULL), 0)
-    sum_ref[...] = total[:, :width]
-    core = jnp.concatenate(halves(total[:8, width:] + total[8:, width:]), 0)
-    row = jnp.concatenate([total[:, :width].astype(LOW), tleft_ref[...], core], 1)
-    out_ref[...] = jnp.broadcast_to(row[None], out_ref.shape)
+    sum_ref[...] = jnp.concatenate([total[:16], total[16:32]], 1)
+    lines = jnp.concatenate(
+        [
+            total[:32].astype(LOW),
+            tleft_ref[:, :128],
+            tleft_ref[:, 128:],
+            repacked(total[None, 32:])[0].astype(LOW),
+        ],
+        0,
+    )
+    out_ref[...] = jnp.broadcast_to(lines[None], out_ref.shape)
 
 
 def backward_body(
@@ -200,23 +238,22 @@
 ):
     group, live, groups, core = place_ref[0], place_ref[1], place_ref[2], place_ref[3]
     slots, rows, n = left_ref.shape[0], tall.shape[0], b4.shape[1]
-    width = own_ref.shape[1]
-
-    def ordered(cols):
-        mine, other = mine_ref[:, :, cols], other_ref[:, :, cols]
+
+    def ordered(first):
+        mine, other = mine_ref[:, first : first + 16], other_ref[:, first : first + 16]
         even, odd = jnp.where(core == 0, mine, other), jnp.where(core == 0, other, mine)
         return jnp.concatenate([even[:, None], odd[:, None]], 1).reshape(rows, -1)
 
-    tall[...] = ordered(slice(width, 2 * width))
-    parts = mine_ref[:, :, 2 * width :].astype(FULL) + other_ref[:, :, 2 * width :].astype(FULL)
-    cores = (parts[:, :8] + parts[:, 8:]).reshape(2 * 128, 128).astype(LOW)
+    blocks = [mine_ref[:, 64:].astype(FULL), other_ref[:, 64:].astype(FULL)]
     at = pl.multiple_of(lax.rem(group + groups // 2, groups) * n, n)
     last = jnp.concatenate([b4[k] for k in range(slots)], 1)
     whole, own, grams, seen, seen_target = [], [], [], [], []
     for t in range(2):
         cols = slice(128 * t, 128 * t + 128)
-        target_core = cores[cols]
-        s = ordered(cols).astype(FULL) + dot(tall[:, cols], target_core, 1, 0)
+        block = jnp.where(core == t, blocks[0], blocks[1])
+        target_core = unpacked(block).astype(LOW)
+        tall[:, cols] = ordered(32 + 16 * t)
+        s = ordered(16 * t).astype(FULL) + dot(tall[:, cols], target_core, 1, 0)
         own.append(own_ref[:, cols] + dot(tleft_ref[:, cols], target_core, 1, 0))
         turned = s.T
         high, low = halves(turned)
@@ -274,24 +311,27 @@
         ],
         scratch_shapes=[pltpu.VMEM(*o) for o in scratch],
         name=name,
-        compiler_params=pltpu.CompilerParams(vmem_limit_bytes=24 << 20),
+        compiler_params=pltpu.CompilerParams(vmem_limit_bytes=16 << 20),
     )(*first, *[near(x) for x in arrays], *given)
 
 
-def probed(col_left, sketch_cols, first, count):
+def probed(place, col_left, sketch_cols, block, first, count):
     return pl.pallas_call(
         functools.partial(probe_body, first=first),
-        in_specs=[pl.BlockSpec(memory_space=pltpu.HBM)] * 2,
-        out_specs=VMEM,
-        out_shape=pltpu.VMEM((count, 2, 128, 128), FULL),
+        in_specs=[SMEM] + [pl.BlockSpec(memory_space=pltpu.HBM)] * 2,
+        out_specs=[VMEM] * 2,
+        out_shape=[
+            pltpu.VMEM((count, 2, 128, 128), FULL),
+            pltpu.VMEM((block, sketch_cols.shape[1]), LOW),
+        ],
         scratch_shapes=[
             pltpu.VMEM((count, *col_left.shape[1:]), LOW),
             pltpu.VMEM(sketch_cols.shape, LOW),
             pltpu.SemaphoreType.DMA((count + 1,)),
         ],
         name="probe",
-        compiler_params=pltpu.CompilerParams(vmem_limit_bytes=24 << 20),
-    )(*(pltpu.with_memory_space_constraint(x, pltpu.HBM) for x in (col_left, sketch_cols)))
+        compiler_params=pltpu.CompilerParams(vmem_limit_bytes=16 << 20),
+    )(place, *(pltpu.with_memory_space_constraint(x, pltpu.HBM) for x in (col_left, sketch_cols)))
 
 
 def shards(
@@ -302,7 +342,13 @@
     n, far, groups = lax.axis_size(INNER), INNER[:2], lax.axis_size("grp")
     half = n // 2
     place = jnp.stack(
-        [lax.axis_index("grp"), live_counts[0], jnp.int32(groups), lax.axis_index(INNER[2])]
+        [
+            lax.axis_index("grp"),
+            live_counts[0],
+            jnp.int32(groups),
+            lax.axis_index(INNER[2]),
+            lax.axis_index(INNER),
+        ]
     ).astype(jnp.int32)
     own = pl.pallas_call(
         join_body,
@@ -311,20 +357,17 @@
         out_shape=pltpu.VMEM((2 * slots, *row_left.shape[1:]), LOW),
         scratch_shapes=[pltpu.SemaphoreType.DMA((2,))],
         name="join",
-        compiler_params=pltpu.CompilerParams(vmem_limit_bytes=24 << 20),
+        compiler_params=pltpu.CompilerParams(vmem_limit_bytes=16 << 20),
     )(*(pltpu.with_memory_space_constraint(x, pltpu.HBM) for x in (row_right, row_left)))
     chunks, probes, up, down = [own], [], own, own
     for step in range(3):
         up, down = shift(up, "grp", 1), shift(down, "grp", -1)
-        if step == 0:
-            own_sketch = lax.dynamic_slice_in_dim(
-                sketch_cols, lax.axis_index(INNER) * block, block, 0
+        if step != 1:
+            half_slots = slots // 2
+            probe, own_sketch = probed(
+                place, col_left, sketch_cols, block, step // 2 * half_slots, half_slots
             )
-        if step < 2:
-            probe = probed(col_left, sketch_cols, step * (slots // 2), slots // 2)
-            up, probe, own_sketch, place = lax.optimization_barrier(
-                (up, probe, own_sketch, place)
-            )
+            up, probe = lax.optimization_barrier((up, probe))
             probes.append(probe)
         chunks += [up, down]
     last_up, last_down = shift(up[:slots], "grp", 1), shift(down[slots:], "grp", -1)
@@ -338,10 +381,10 @@
         given=(col_right,),
     )
     piece = (half, block, width)
-    keep, send, pair, core = kernel(
+    keep, send, pair = kernel(
         forward_body,
         "forward",
-        [(piece, FULL), (piece, LOW), ((slots, 128, width), FULL), ((half, block, 128), LOW)],
+        [((half, 40, 128), FULL), ((half, 40, 128), LOW), ((slots, 128, width), FULL)],
         [((rows, width), FULL)],
         place,
         last_up,
@@ -353,13 +396,12 @@
         given=(col_right, target_right),
     )
     (merged,) = kernel(
-        merge_body, "merge", [((half, block, width + 128), LOW)], [], None,
-        keep, shift(send, INNER[2], 1), core,
+        merge_body, "merge", [((half, 40, 128), LOW)], [], None, keep, shift(send, INNER[2], 1)
     )
     own_sum, mine = kernel(
         own_body,
         "own",
-        [((block, width), FULL), ((half, block, 2 * width + 128), LOW)],
+        [((block, width), FULL), ((half, 72, 128), LOW)],
         [],
         None,
         lax.all_to_all(merged, far, 0, 0, tiled=True),

time: 139 us -> 136 us (0.978)
  blocking collectives: 46.7 us -> 44.2 us
  Pallas kernels: 17.6 us -> 19 us
    all_to_all x1, blocking collectives: 23.6 us -> 22.1 us  [shards(): mine = lax.all_to_all(mine, far, 0, 0, tiled=True)]
  transfers between devices with their start and end apart: 12 -> 12, of which waited for: 9 -> 9; matrix products, arithmetic and copies ran while one was open for 1% -> 1% of each run, Pallas kernels for 4% -> 5%
where the time goes in v7:
time: 136 us; the launch traced here: 134 us
  blocking collectives  44.2 us (32%)
  starting transfers between devices  41.9 us (31%)
  waiting for transfers between devices  26.4 us (19%)
  Pallas kernels  19 us (14%)
  between operations  1.51 us (1%)
    ppermute x11, starting transfers between devices, shift(): return lax.ppermute(x, axis, [(i, (i + by) % n) for i in range(n)])  37.1 us
    all_to_all x1, blocking collectives, shards(): mine = lax.all_to_all(mine, far, 0, 0, tiled=True)  22.1 us
    all_to_all x1, blocking collectives, shards(): lax.all_to_all(merged, far, 0, 0, tiled=True)  22 us
    ppermute x11, waiting for transfers between devices, shift(): return lax.ppermute(x, axis, [(i, (i + by) % n) for i in range(n)])  13.8 us
    pallas_call x7, Pallas kernels, kernel(): pl.pallas_call(body, in_specs=[SMEM] * len(first) + [VMEM] * (len(arrays)...  12.9 us
    all_to_all x1, waiting for transfers between devices, shards(): lax.all_to_all(merged, far, 0, 0, tiled=True)  12.6 us
    pallas_call x2, Pallas kernels, probed(): pl.pallas_call(functools.partial(probe_body, first=first), in_specs=[SMEM...  5.16 us
    all_to_all x1, starting transfers between devices, shards(): lax.all_to_all(merged, far, 0, 0, tiled=True)  4.8 us
  transfers between devices with their start and end apart: 12, of which 9 were waited for; matrix products, arithmetic and copies ran while one was open for 1% of the time, Pallas kernels for 5%

profile of v7, /device:TPU:56, one launch (start us, length us, event | category | flops | bytes accessed | tf_op | source)
XLA Modules:
  0.0 133.8 jit_solution(12451892106878646705)
XLA Ops:
  1.6 7.0 %collective-permute-start = (bf16[8,128,128]{2,1,0:T(8,128)(2,1)S(1)}, bf16[8,128,128]{2,1,0:T(8,128)(2,1)S(1)}, u32[]{:S(2)}, u32[]{:S(2)}) collective-permute-start(bf16[8,128,128]{2,1,0:T(8,128)(2,1)S(1)} %join.1.own), channel_id=1, source_target_pairs={{0,64},{64,128},{128,192},{192,256},{256,320},{320,384},{384,448},... | collective-permute-start | bytes 786440 | tf_op jit(solution)/shard_map/ppermute | solution.py:296
  8.7 1.9 %collective-permute-start.4 = (bf16[8,128,128]{2,1,0:T(8,128)(2,1)S(1)}, bf16[8,128,128]{2,1,0:T(8,128)(2,1)S(1)}, u32[]{:S(2)}, u32[]{:S(2)}) collective-permute-start(bf16[8,128,128]{2,1,0:T(8,128)(2,1)S(1)} %join.1.own), channel_id=1, source_target_pairs={{0,448},{64,0},{128,64},{192,128},{256,192},{320,256},{384,320},{4... | collective-permute-start | bytes 786440 | tf_op jit(solution)/shard_map/ppermute | solution.py:296
  11.3 2.7 %probe.2 = (f32[2,2,128,128]{3,2,1,0:T(8,128)S(1)}, bf16[16,256]{1,0:T(8,128)(2,1)}) custom-call(s32[5]{0:T(128)S(1)} %stack.15.place_ref, bf16[4,1024,256]{2,1,0:T(8,128)(2,1)} %left_ref.1, bf16[1024,256]{1,0:T(8,128)(2,1)} %sketch_any.3), custom_call_target="tpu_custom_call" | custom-call | tf_op jit(solution)/shard_map/probe/pallas_call | solution.py:319
  14.1 5.3 %collective-permute-start.1 = (bf16[8,128,128]{2,1,0:T(8,128)(2,1)S(1)}, bf16[8,128,128]{2,1,0:T(8,128)(2,1)S(1)}, u32[]{:S(2)}, u32[]{:S(2)}) collective-permute-start(bf16[8,128,128]{2,1,0:T(8,128)(2,1)S(1)} %collective-permute-done.f1), channel_id=1, source_target_pairs={{0,64},{64,128},{128,192},{192,256},{256,320},{320,384},{384,448},... | collective-permute-start | bytes 786440 | tf_op jit(solution)/shard_map/ppermute | solution.py:296
  19.3 1.9 %collective-permute-start.5 = (bf16[8,128,128]{2,1,0:T(8,128)(2,1)S(1)}, bf16[8,128,128]{2,1,0:T(8,128)(2,1)S(1)}, u32[]{:S(2)}, u32[]{:S(2)}) collective-permute-start(bf16[8,128,128]{2,1,0:T(8,128)(2,1)S(1)} %collective-permute-done.4.b1), channel_id=1, source_target_pairs={{0,448},{64,0},{128,64},{192,128},{256,192},{320,256},{384,320},{4... | collective-permute-start | bytes 786440 | tf_op jit(solution)/shard_map/ppermute | solution.py:296
  21.3 2.9 %collective-permute-done.1.f2 = bf16[8,128,128]{2,1,0:T(8,128)(2,1)S(1)} collective-permute-done((bf16[8,128,128]{2,1,0:T(8,128)(2,1)S(1)}, bf16[8,128,128]{2,1,0:T(8,128)(2,1)S(1)}, u32[]{:S(2)}, u32[]{:S(2)}) %collective-permute-start.1) | collective-permute-done | bytes 262176 | tf_op jit(solution)/shard_map/ppermute | solution.py:296
  24.2 5.6 %collective-permute-start.2 = (bf16[8,128,128]{2,1,0:T(8,128)(2,1)S(1)}, bf16[8,128,128]{2,1,0:T(8,128)(2,1)S(1)}, u32[]{:S(2)}, u32[]{:S(2)}) collective-permute-start(bf16[8,128,128]{2,1,0:T(8,128)(2,1)S(1)} %collective-permute-done.1.f2), channel_id=1, source_target_pairs={{0,64},{64,128},{128,192},{192,256},{256,320},{320,384},{384,448},... | collective-permute-start | bytes 786440 | tf_op jit(solution)/shard_map/ppermute | solution.py:296
  30.1 1.9 %collective-permute-start.6 = (bf16[8,128,128]{2,1,0:T(8,128)(2,1)S(1)}, bf16[8,128,128]{2,1,0:T(8,128)(2,1)S(1)}, u32[]{:S(2)}, u32[]{:S(2)}) collective-permute-start(bf16[8,128,128]{2,1,0:T(8,128)(2,1)S(1)} %collective-permute-done.5.b2), channel_id=1, source_target_pairs={{0,448},{64,0},{128,64},{192,128},{256,192},{320,256},{384,320},{4... | collective-permute-start | bytes 786440 | tf_op jit(solution)/shard_map/ppermute | solution.py:296
  32.0 2.5 %probe.3 = (f32[2,2,128,128]{3,2,1,0:T(8,128)S(1)}, bf16[16,256]{1,0:T(8,128)(2,1)S(1)}) custom-call(s32[5]{0:T(128)S(1)} %stack.15.place_ref, bf16[4,1024,256]{2,1,0:T(8,128)(2,1)} %left_ref.1, bf16[1024,256]{1,0:T(8,128)(2,1)} %sketch_any.3), custom_call_target="tpu_custom_call" | custom-call | tf_op jit(solution)/shard_map/probe/pallas_call | solution.py:319
  35.1 5.6 %collective-permute-start.3 = (bf16[4,128,128]{2,1,0:T(8,128)(2,1)S(1)}, bf16[4,128,128]{2,1,0:T(8,128)(2,1)S(1)}, u32[]{:S(2)}, u32[]{:S(2)}) collective-permute-start(bf16[4,128,128]{2,1,0:T(8,128)(2,1)S(1)} %slice.6), channel_id=1, source_target_pairs={{0,64},{64,128},{128,192},{192,256},{256,320},{320,384},{384,448},... | collective-permute-start | bytes 393224 | tf_op jit(solution)/shard_map/ppermute | solution.py:296
  41.0 1.9 %collective-permute-start.7 = (bf16[4,128,128]{2,1,0:T(8,128)(2,1)S(1)}, bf16[4,128,128]{2,1,0:T(8,128)(2,1)S(1)}, u32[]{:S(2)}, u32[]{:S(2)}) collective-permute-start(bf16[4,128,128]{2,1,0:T(8,128)(2,1)S(1)} %slice.8), channel_id=1, source_target_pairs={{0,448},{64,0},{128,64},{192,128},{256,192},{320,256},{384,320},{4... | collective-permute-start | bytes 393224 | tf_op jit(solution)/shard_map/ppermute | solution.py:296
  42.9 1.4 %early.1 = (f32[4,128,256]{2,1,0:T(8,128)S(1)}, bf16[1024,512]{1,0:T(8,128)(2,1)S(1)}) custom-call(s32[5]{0:T(128)S(1)} %stack.15.place_ref, bf16[8,128,128]{2,1,0:T(8,128)(2,1)S(1)} %join.1.own, bf16[8,128,128]{2,1,0:T(8,128)(2,1)S(1)} %collective-permute-done.f1, bf16[8,128,128]{2,1,0:T(8,128)(2,1)S(1)} %collective-permute-done.4.b1, ...), custom_call_target="tpu_custom_call" | custom-call | tf_op jit(solution)/shard_map/early/pallas_call | solution.py:305
  44.3 4.7 %collective-permute-done.7.b4 = bf16[4,128,128]{2,1,0:T(8,128)(2,1)S(1)} collective-permute-done((bf16[4,128,128]{2,1,0:T(8,128)(2,1)S(1)}, bf16[4,128,128]{2,1,0:T(8,128)(2,1)S(1)}, u32[]{:S(2)}, u32[]{:S(2)}) %collective-permute-start.7) | collective-permute-done | bytes 131104 | tf_op jit(solution)/shard_map/ppermute | solution.py:296
  49.1 2.0 %forward.1 = (f32[32,40,128]{2,1,0:T(8,128)S(1)}, bf16[32,40,128]{2,1,0:T(8,128)(2,1)S(1)}, f32[4,128,256]{2,1,0:T(8,128)S(1)}) custom-call(s32[5]{0:T(128)S(1)} %stack.15.place_ref, bf16[4,128,128]{2,1,0:T(8,128)(2,1)S(1)} %collective-permute-done.3.f4, bf16[4,128,128]{2,1,0:T(8,128)(2,1)S(1)} %collective-permute-done.7.b4, ...), custom_call_target="tpu_custom_call" | custom-call | tf_op jit(solution)/shard_map/forward/pallas_call | solution.py:305
  51.1 2.1 %collective-permute-start.8 = (bf16[32,40,128]{2,1,0:T(8,128)(2,1)S(1)}, bf16[32,40,128]{2,1,0:T(8,128)(2,1)S(1)}, u32[]{:S(2)}, u32[]{:S(2)}) collective-permute-start(bf16[32,40,128]{2,1,0:T(8,128)(2,1)S(1)} %get-tuple-element.30), channel_id=1, source_target_pairs={{0,1},{1,0},{2,3},{3,2},{4,5},{5,4},{6,7},{7,6},{8,9},{9,8},{10,11... | collective-permute-start | bytes 983048 | tf_op jit(solution)/shard_map/ppermute | solution.py:296
  53.2 1.6 %collective-permute-done.8.come_ref = bf16[32,40,128]{2,1,0:T(8,128)(2,1)S(1)} collective-permute-done((bf16[32,40,128]{2,1,0:T(8,128)(2,1)S(1)}, bf16[32,40,128]{2,1,0:T(8,128)(2,1)S(1)}, u32[]{:S(2)}, u32[]{:S(2)}) %collective-permute-start.8) | collective-permute-done | bytes 327712 | tf_op jit(solution)/shard_map/ppermute | solution.py:296
  54.9 22.0 %all_to_all.15.pieces_ref = bf16[32,40,128]{2,1,0:T(8,128)(2,1)S(1)} all-to-all(bf16[32,40,128]{2,1,0:T(8,128)(2,1)S(1)} %merge.1), channel_id=1, replica_groups=mesh['grp'=8,'inner_0'=8,'inner_1'=4,'inner_2'=2] {'inner_0','inner_1'}, dimensions={0} | all-to-all | bytes 655360 | tf_op jit(solution)/shard_map/all_to_all | solution.py:407
  77.0 22.1 %all_to_all.16.mine_ref = bf16[32,72,128]{2,1,0:T(8,128)(2,1)S(1)} all-to-all(bf16[32,72,128]{2,1,0:T(8,128)(2,1)S(1)} %get-tuple-element.31), channel_id=1, replica_groups=mesh['grp'=8,'inner_0'=8,'inner_1'=4,'inner_2'=2] {'inner_0','inner_1'}, dimensions={0} | all-to-all | bytes 1179648 | tf_op jit(solution)/shard_map/all_to_all | solution.py:410
  99.2 1.9 %collective-permute-start.9 = (bf16[32,72,128]{2,1,0:T(8,128)(2,1)S(1)}, bf16[32,72,128]{2,1,0:T(8,128)(2,1)S(1)}, u32[]{:S(2)}, u32[]{:S(2)}) collective-permute-start(bf16[32,72,128]{2,1,0:T(8,128)(2,1)S(1)} %all_to_all.16.mine_ref), channel_id=1, source_target_pairs={{0,1},{1,0},{2,3},{3,2},{4,5},{5,4},{6,7},{7,6},{8,9},{9,8},{10,11... | collective-permute-start | bytes 1769480 | tf_op jit(solution)/shard_map/ppermute | solution.py:296
  101.1 2.0 %collective-permute-done.9.other_ref = bf16[32,72,128]{2,1,0:T(8,128)(2,1)S(1)} collective-permute-done((bf16[32,72,128]{2,1,0:T(8,128)(2,1)S(1)}, bf16[32,72,128]{2,1,0:T(8,128)(2,1)S(1)}, u32[]{:S(2)}, u32[]{:S(2)}) %collective-permute-start.9) | collective-permute-done | bytes 589856 | tf_op jit(solution)/shard_map/ppermute | solution.py:296
  103.1 7.8 %backward.1 = (f32[16,256]{1,0:T(8,128)S(1)}, f32[32,16,256]{2,1,0:T(8,128)S(1)}, bf16[32,16,256]{2,1,0:T(8,128)(2,1)S(1)}, f32[16,256]{1,0:T(8,128)S(1)}) custom-call(s32[5]{0:T(128)S(1)} %stack.15.place_ref, bf16[32,72,128]{2,1,0:T(8,128)(2,1)S(1)} %all_to_all.16.mine_ref, bf16[32,72,128]{2,1,0:T(8,128)(2,1)S(1)} %collective-permute-done.9.other_ref, ...), custom_call_target="tpu_custom_call" | custom-call | tf_op jit(solution)/shard_map/backward/pallas_call | solution.py:305
  110.9 2.0 %collective-permute-start.10 = (bf16[32,16,256]{2,1,0:T(8,128)(2,1)S(1)}, bf16[32,16,256]{2,1,0:T(8,128)(2,1)S(1)}, u32[]{:S(2)}, u32[]{:S(2)}) collective-permute-start(bf16[32,16,256]{2,1,0:T(8,128)(2,1)S(1)} %get-tuple-element.36), channel_id=1, source_target_pairs={{0,1},{1,0},{2,3},{3,2},{4,5},{5,4},{6,7},{7,6},{8,9},{9,8},{10,11... | collective-permute-start | bytes 786440 | tf_op jit(solution)/shard_map/ppermute | solution.py:296
  115.1 4.8 %all-to-all-start.2 = ((bf16[32,16,256]{2,1,0:T(8,128)(2,1)}), bf16[32,16,256]{2,1,0:T(8,128)(2,1)S(1)}, u32[]{:S(2)}, u32[]{:S(2)}) async-start(bf16[32,16,256]{2,1,0:T(8,128)(2,1)} %add.9), calls=%async_computation.2 | async-start | bytes 524288 | tf_op jit(solution)/shard_map/all_to_all | solution.py:434
  120.5 12.6 %all-to-all-done.2.pieces_ref = bf16[32,16,256]{2,1,0:T(8,128)(2,1)S(1)} async-done(((bf16[32,16,256]{2,1,0:T(8,128)(2,1)}), bf16[32,16,256]{2,1,0:T(8,128)(2,1)S(1)}, u32[]{:S(2)}, u32[]{:S(2)}) %all-to-all-start.2) | async-done | bytes 262176 | tf_op jit(solution)/shard_map/all_to_all | solution.py:434
  (24 shorter events, 5.9 us)
Async XLA Ops:
  1.6 12.4 %collective-permute-start = (bf16[8,128,128]{2,1,0:T(8,128)(2,1)S(1)}, bf16[8,128,128]{2,1,0:T(8,128)(2,1)S(1)}, u32[]{:S(2)}, u32[]{:S(2)}) collective-permute-start(bf16[8,128,128]{2,1,0:T(8,128)(2,1)S(1)} %join.1.own), channel_id=1, source_target_pairs={{0,64},{64,128},{128,192},{192,256},{256,320},{320,384},{384,448},... | collective-permute-start | bytes 786440 | tf_op jit(solution)/shard_map/ppermute | solution.py:296
  8.7 10.7 %collective-permute-start.4 = (bf16[8,128,128]{2,1,0:T(8,128)(2,1)S(1)}, bf16[8,128,128]{2,1,0:T(8,128)(2,1)S(1)}, u32[]{:S(2)}, u32[]{:S(2)}) collective-permute-start(bf16[8,128,128]{2,1,0:T(8,128)(2,1)S(1)} %join.1.own), channel_id=1, source_target_pairs={{0,448},{64,0},{128,64},{192,128},{256,192},{320,256},{384,320},{4... | collective-permute-start | bytes 786440 | tf_op jit(solution)/shard_map/ppermute | solution.py:296
  14.0 28.9 %copy-start.1 = (bf16[4,1024,256]{2,1,0:T(8,128)(2,1)S(1)}, bf16[4,1024,256]{2,1,0:T(8,128)(2,1)}, u32[]{:S(2)}) copy-start(bf16[4,1024,256]{2,1,0:T(8,128)(2,1)} %right_ref.3) | copy-start | bytes 6291460
  14.1 10.2 %collective-permute-start.1 = (bf16[8,128,128]{2,1,0:T(8,128)(2,1)S(1)}, bf16[8,128,128]{2,1,0:T(8,128)(2,1)S(1)}, u32[]{:S(2)}, u32[]{:S(2)}) collective-permute-start(bf16[8,128,128]{2,1,0:T(8,128)(2,1)S(1)} %collective-permute-done.f1), channel_id=1, source_target_pairs={{0,64},{64,128},{128,192},{192,256},{256,320},{320,384},{384,448},... | collective-permute-start | bytes 786440 | tf_op jit(solution)/shard_map/ppermute | solution.py:296
  19.3 10.8 %collective-permute-start.5 = (bf16[8,128,128]{2,1,0:T(8,128)(2,1)S(1)}, bf16[8,128,128]{2,1,0:T(8,128)(2,1)S(1)}, u32[]{:S(2)}, u32[]{:S(2)}) collective-permute-start(bf16[8,128,128]{2,1,0:T(8,128)(2,1)S(1)} %collective-permute-done.4.b1), channel_id=1, source_target_pairs={{0,448},{64,0},{128,64},{192,128},{256,192},{320,256},{384,320},{4... | collective-permute-start | bytes 786440 | tf_op jit(solution)/shard_map/ppermute | solution.py:296
  24.2 10.9 %collective-permute-start.2 = (bf16[8,128,128]{2,1,0:T(8,128)(2,1)S(1)}, bf16[8,128,128]{2,1,0:T(8,128)(2,1)S(1)}, u32[]{:S(2)}, u32[]{:S(2)}) collective-permute-start(bf16[8,128,128]{2,1,0:T(8,128)(2,1)S(1)} %collective-permute-done.1.f2), channel_id=1, source_target_pairs={{0,64},{64,128},{128,192},{192,256},{256,320},{320,384},{384,448},... | collective-permute-start | bytes 786440 | tf_op jit(solution)/shard_map/ppermute | solution.py:296
  30.1 10.9 %collective-permute-start.6 = (bf16[8,128,128]{2,1,0:T(8,128)(2,1)S(1)}, bf16[8,128,128]{2,1,0:T(8,128)(2,1)S(1)}, u32[]{:S(2)}, u32[]{:S(2)}) collective-permute-start(bf16[8,128,128]{2,1,0:T(8,128)(2,1)S(1)} %collective-permute-done.5.b2), channel_id=1, source_target_pairs={{0,448},{64,0},{128,64},{192,128},{256,192},{320,256},{384,320},{4... | collective-permute-start | bytes 786440 | tf_op jit(solution)/shard_map/ppermute | solution.py:296
  35.1 14.0 %copy-start.2 = (bf16[16,256]{1,0:T(8,128)(2,1)S(1)}, bf16[16,256]{1,0:T(8,128)(2,1)}, u32[]{:S(2)}) copy-start(bf16[16,256]{1,0:T(8,128)(2,1)} %tright_ref.3) | copy-start | bytes 24580
  35.1 9.2 %collective-permute-start.3 = (bf16[4,128,128]{2,1,0:T(8,128)(2,1)S(1)}, bf16[4,128,128]{2,1,0:T(8,128)(2,1)S(1)}, u32[]{:S(2)}, u32[]{:S(2)}) collective-permute-start(bf16[4,128,128]{2,1,0:T(8,128)(2,1)S(1)} %slice.6), channel_id=1, source_target_pairs={{0,64},{64,128},{128,192},{192,256},{256,320},{320,384},{384,448},... | collective-permute-start | bytes 393224 | tf_op jit(solution)/shard_map/ppermute | solution.py:296
  41.0 8.1 %collective-permute-start.7 = (bf16[4,128,128]{2,1,0:T(8,128)(2,1)S(1)}, bf16[4,128,128]{2,1,0:T(8,128)(2,1)S(1)}, u32[]{:S(2)}, u32[]{:S(2)}) collective-permute-start(bf16[4,128,128]{2,1,0:T(8,128)(2,1)S(1)} %slice.8), channel_id=1, source_target_pairs={{0,448},{64,0},{128,64},{192,128},{256,192},{320,256},{384,320},{4... | collective-permute-start | bytes 393224 | tf_op jit(solution)/shard_map/ppermute | solution.py:296
  49.1 27.9 %copy-start.3 = (bf16[16,256]{1,0:T(8,128)(2,1)S(1)}, bf16[16,256]{1,0:T(8,128)(2,1)}, u32[]{:S(2)}) copy-start(bf16[16,256]{1,0:T(8,128)(2,1)} %tleft_ref.3) | copy-start | bytes 24580
  51.1 51.9 %copy-start = (bf16[4,1024,256]{2,1,0:T(8,128)(2,1)S(1)}, bf16[4,1024,256]{2,1,0:T(8,128)(2,1)}, u32[]{:S(2)}) copy-start(bf16[4,1024,256]{2,1,0:T(8,128)(2,1)} %left_ref.1) | copy-start | bytes 6291460
  51.1 3.7 %collective-permute-start.8 = (bf16[32,40,128]{2,1,0:T(8,128)(2,1)S(1)}, bf16[32,40,128]{2,1,0:T(8,128)(2,1)S(1)}, u32[]{:S(2)}, u32[]{:S(2)}) collective-permute-start(bf16[32,40,128]{2,1,0:T(8,128)(2,1)S(1)} %get-tuple-element.30), channel_id=1, source_target_pairs={{0,1},{1,0},{2,3},{3,2},{4,5},{5,4},{6,7},{7,6},{8,9},{9,8},{10,11... | collective-permute-start | bytes 983048 | tf_op jit(solution)/shard_map/ppermute | solution.py:296
  99.2 3.9 %collective-permute-start.9 = (bf16[32,72,128]{2,1,0:T(8,128)(2,1)S(1)}, bf16[32,72,128]{2,1,0:T(8,128)(2,1)S(1)}, u32[]{:S(2)}, u32[]{:S(2)}) collective-permute-start(bf16[32,72,128]{2,1,0:T(8,128)(2,1)S(1)} %all_to_all.16.mine_ref), channel_id=1, source_target_pairs={{0,1},{1,0},{2,3},{3,2},{4,5},{5,4},{6,7},{7,6},{8,9},{9,8},{10,11... | collective-permute-start | bytes 1769480 | tf_op jit(solution)/shard_map/ppermute | solution.py:296
  110.9 3.4 %collective-permute-start.10 = (bf16[32,16,256]{2,1,0:T(8,128)(2,1)S(1)}, bf16[32,16,256]{2,1,0:T(8,128)(2,1)S(1)}, u32[]{:S(2)}, u32[]{:S(2)}) collective-permute-start(bf16[32,16,256]{2,1,0:T(8,128)(2,1)S(1)} %get-tuple-element.36), channel_id=1, source_target_pairs={{0,1},{1,0},{2,3},{3,2},{4,5},{5,4},{6,7},{7,6},{8,9},{9,8},{10,11... | collective-permute-start | bytes 786440 | tf_op jit(solution)/shard_map/ppermute | solution.py:296
  115.1 18.1 %all-to-all-start.2 = ((bf16[32,16,256]{2,1,0:T(8,128)(2,1)}), bf16[32,16,256]{2,1,0:T(8,128)(2,1)S(1)}, u32[]{:S(2)}, u32[]{:S(2)}) async-start(bf16[32,16,256]{2,1,0:T(8,128)(2,1)} %add.9), calls=%async_computation.2 | async-start | bytes 524288 | tf_op jit(solution)/shard_map/all_to_all | solution.py:434

commit v8 on v7

--- a/solution.py
+++ b/solution.py
@@ -120,7 +120,7 @@
 
 
 def early_body(place_ref, own, f1, b1, f2, b2, f3, b3, right_ref, pair_ref, pivot_ref, factor):
-    group, groups = place_ref[0], place_ref[2]
+    group, groups, core = place_ref[0], place_ref[2], place_ref[3]
     slots, n = right_ref.shape[0], own.shape[1]
 
     def put(ref, distance):
@@ -136,8 +136,8 @@
 
     put(own, 0)
     for s, (f, b) in enumerate(((f1, b1), (f2, b2), (f3, b3))):
-        put(f, groups - 1 - s)
-        put(b, 1 + s)
+        put(f, jnp.where(core == 0, groups - 1 - s, 1 + s))
+        put(b, jnp.where(core == 0, 1 + s, groups - 1 - s))
     put(None, groups // 2)
     for k in range(slots):
         pair_ref[k] = dot(factor[:, 128 * k : 128 * k + 128], right_ref[k], 0, 0)
@@ -296,6 +296,16 @@
     return lax.ppermute(x, axis, [(i, (i + by) % n) for i in range(n)])
 
 
+def around(x, by):
+    n = lax.axis_size("grp")
+    pairs = [
+        (2 * i + core, 2 * ((i + (by if core == 0 else -by)) % n) + core)
+        for i in range(n)
+        for core in range(2)
+    ]
+    return lax.ppermute(x, ("grp", INNER[2]), pairs)
+
+
 def near(x):
     return pltpu.with_memory_space_constraint(x, pltpu.VMEM)
 
@@ -307,7 +317,7 @@
         in_specs=[SMEM] * len(first) + [VMEM] * (len(arrays) + len(given)),
         out_specs=[VMEM] * len(outs),
         out_shape=[
-            (jax.ShapeDtypeStruct if o[0] == leave else pltpu.VMEM)(*o) for o in outs
+            (jax.ShapeDtypeStruct if i == leave else pltpu.VMEM)(*o) for i, o in enumerate(outs)
         ],
         scratch_shapes=[pltpu.VMEM(*o) for o in scratch],
         name=name,
@@ -361,16 +371,16 @@
     )(*(pltpu.with_memory_space_constraint(x, pltpu.HBM) for x in (row_right, row_left)))
     chunks, probes, up, down = [own], [], own, own
     for step in range(3):
-        up, down = shift(up, "grp", 1), shift(down, "grp", -1)
-        if step != 1:
+        up, down = around(up, 1), around(down, -1)
+        if step:
             half_slots = slots // 2
             probe, own_sketch = probed(
-                place, col_left, sketch_cols, block, step // 2 * half_slots, half_slots
+                place, col_left, sketch_cols, block, (step - 1) * half_slots, half_slots
             )
             up, probe = lax.optimization_barrier((up, probe))
             probes.append(probe)
         chunks += [up, down]
-    last_up, last_down = shift(up[:slots], "grp", 1), shift(down[slots:], "grp", -1)
+    last_up, last_down = around(up[:slots], 1), around(down[slots:], -1)
     early, pivot = kernel(
         early_body,
         "early",
@@ -422,6 +432,7 @@
         pivot,
         pair,
         given=(target_left, target_right, col_left),
+        leave=0,
     )
     (merged,) = kernel(add_body, "add", [(piece, LOW)], [], None, keep, shift(send, INNER[2], 1))
     merged = near(merged)
@@ -433,7 +444,7 @@
         None,
         lax.all_to_all(merged, far, 0, 0, tiled=True),
         direct,
-        leave=(block, width),
+        leave=0,
     )
     return basis, coeffs
 

time: 136 us -> 139 us (1.022)
  the two profiles are of different devices: /device:TPU:56 before, /device:TPU:24 now
where the time goes in v8:
time: 139 us
  blocking collectives  67.4 us (48%)
  starting transfers between devices  35.1 us (25%)
  Pallas kernels  18.6 us (13%)
  waiting for transfers between devices  15.8 us (11%)
  between operations  1.51 us (1%)
    all_to_all x2, blocking collectives, shards(): lax.all_to_all(merged, far, 0, 0, tiled=True)  45.3 us
    ppermute x8, starting transfers between devices, around(): return lax.ppermute(x, ('grp', INNER[2]), pairs)  29.2 us
    all_to_all x1, blocking collectives, shards(): mine = lax.all_to_all(mine, far, 0, 0, tiled=True)  22.1 us
    pallas_call x7, Pallas kernels, kernel(): pl.pallas_call(body, in_specs=[SMEM] * len(first) + [VMEM] * (len(arrays)...  12.5 us
    ppermute x8, waiting for transfers between devices, around(): return lax.ppermute(x, ('grp', INNER[2]), pairs)  10.8 us
    ppermute x3, starting transfers between devices, shift(): return lax.ppermute(x, axis, [(i, (i + by) % n) for i in range(n)])  5.98 us
    pallas_call x2, Pallas kernels, probed(): pl.pallas_call(functools.partial(probe_body, first=first), in_specs=[SMEM...  5.15 us
    ppermute x3, waiting for transfers between devices, shift(): return lax.ppermute(x, axis, [(i, (i + by) % n) for i in range(n)])  4.95 us
  transfers between devices with their start and end apart: 11, of which 7 were waited for; matrix products, arithmetic and copies ran while one was open for 0% of the time, Pallas kernels for 5%

profile of v8, /device:TPU:24, one launch (start us, length us, event | category | flops | bytes accessed | tf_op | source)
XLA Modules:
  0.0 138.6 jit_solution(11820240383900931533)
XLA Ops:
  1.6 4.7 %collective-permute-start = (bf16[8,128,128]{2,1,0:T(8,128)(2,1)S(1)}, bf16[8,128,128]{2,1,0:T(8,128)(2,1)S(1)}, u32[]{:S(2)}, u32[]{:S(2)}) collective-permute-start(bf16[8,128,128]{2,1,0:T(8,128)(2,1)S(1)} %join.1.own), channel_id=1, source_target_pairs={{0,64},{1,449},{64,128},{65,1},{128,192},{129,65},{192,256},{193,1... | collective-permute-start | bytes 786440 | tf_op jit(solution)/shard_map/ppermute | solution.py:306
  6.3 1.9 %collective-permute-start.4 = (bf16[8,128,128]{2,1,0:T(8,128)(2,1)S(1)}, bf16[8,128,128]{2,1,0:T(8,128)(2,1)S(1)}, u32[]{:S(2)}, u32[]{:S(2)}) collective-permute-start(bf16[8,128,128]{2,1,0:T(8,128)(2,1)S(1)} %join.1.own), channel_id=1, source_target_pairs={{0,448},{1,65},{64,0},{65,129},{128,64},{129,193},{192,128},{193,2... | collective-permute-start | bytes 786440 | tf_op jit(solution)/shard_map/ppermute | solution.py:306
  8.3 3.8 %collective-permute-done.f1 = bf16[8,128,128]{2,1,0:T(8,128)(2,1)S(1)} collective-permute-done((bf16[8,128,128]{2,1,0:T(8,128)(2,1)S(1)}, bf16[8,128,128]{2,1,0:T(8,128)(2,1)S(1)}, u32[]{:S(2)}, u32[]{:S(2)}) %collective-permute-start) | collective-permute-done | bytes 262176 | tf_op jit(solution)/shard_map/ppermute | solution.py:306
  12.0 5.6 %collective-permute-start.1 = (bf16[8,128,128]{2,1,0:T(8,128)(2,1)S(1)}, bf16[8,128,128]{2,1,0:T(8,128)(2,1)S(1)}, u32[]{:S(2)}, u32[]{:S(2)}) collective-permute-start(bf16[8,128,128]{2,1,0:T(8,128)(2,1)S(1)} %collective-permute-done.f1), channel_id=1, source_target_pairs={{0,64},{1,449},{64,128},{65,1},{128,192},{129,65},{192,256},{193,1... | collective-permute-start | bytes 786440 | tf_op jit(solution)/shard_map/ppermute | solution.py:306
  17.7 1.9 %collective-permute-start.5 = (bf16[8,128,128]{2,1,0:T(8,128)(2,1)S(1)}, bf16[8,128,128]{2,1,0:T(8,128)(2,1)S(1)}, u32[]{:S(2)}, u32[]{:S(2)}) collective-permute-start(bf16[8,128,128]{2,1,0:T(8,128)(2,1)S(1)} %collective-permute-done.4.b1), channel_id=1, source_target_pairs={{0,448},{1,65},{64,0},{65,129},{128,64},{129,193},{192,128},{193,2... | collective-permute-start | bytes 786440 | tf_op jit(solution)/shard_map/ppermute | solution.py:306
  20.3 2.7 %probe.2 = (f32[2,2,128,128]{3,2,1,0:T(8,128)S(1)}, bf16[16,256]{1,0:T(8,128)(2,1)}) custom-call(s32[5]{0:T(128)S(1)} %stack.15.place_ref, bf16[4,1024,256]{2,1,0:T(8,128)(2,1)} %left_ref.1, bf16[1024,256]{1,0:T(8,128)(2,1)} %sketch_any.3), custom_call_target="tpu_custom_call" | custom-call | tf_op jit(solution)/shard_map/probe/pallas_call | solution.py:329
  24.1 5.6 %collective-permute-start.2 = (bf16[8,128,128]{2,1,0:T(8,128)(2,1)S(1)}, bf16[8,128,128]{2,1,0:T(8,128)(2,1)S(1)}, u32[]{:S(2)}, u32[]{:S(2)}) collective-permute-start(bf16[8,128,128]{2,1,0:T(8,128)(2,1)S(1)} %collective-permute-done.1.f2), channel_id=1, source_target_pairs={{0,64},{1,449},{64,128},{65,1},{128,192},{129,65},{192,256},{193,1... | collective-permute-start | bytes 786440 | tf_op jit(solution)/shard_map/ppermute | solution.py:306
  29.7 1.9 %collective-permute-start.6 = (bf16[8,128,128]{2,1,0:T(8,128)(2,1)S(1)}, bf16[8,128,128]{2,1,0:T(8,128)(2,1)S(1)}, u32[]{:S(2)}, u32[]{:S(2)}) collective-permute-start(bf16[8,128,128]{2,1,0:T(8,128)(2,1)S(1)} %collective-permute-done.5.b2), channel_id=1, source_target_pairs={{0,448},{1,65},{64,0},{65,129},{128,64},{129,193},{192,128},{193,2... | collective-permute-start | bytes 786440 | tf_op jit(solution)/shard_map/ppermute | solution.py:306
  31.7 2.4 %probe.3 = (f32[2,2,128,128]{3,2,1,0:T(8,128)S(1)}, bf16[16,256]{1,0:T(8,128)(2,1)S(1)}) custom-call(s32[5]{0:T(128)S(1)} %stack.15.place_ref, bf16[4,1024,256]{2,1,0:T(8,128)(2,1)} %left_ref.1, bf16[1024,256]{1,0:T(8,128)(2,1)} %sketch_any.3), custom_call_target="tpu_custom_call" | custom-call | tf_op jit(solution)/shard_map/probe/pallas_call | solution.py:329
  35.4 5.6 %collective-permute-start.3 = (bf16[4,128,128]{2,1,0:T(8,128)(2,1)S(1)}, bf16[4,128,128]{2,1,0:T(8,128)(2,1)S(1)}, u32[]{:S(2)}, u32[]{:S(2)}) collective-permute-start(bf16[4,128,128]{2,1,0:T(8,128)(2,1)S(1)} %slice.6), channel_id=1, source_target_pairs={{0,64},{1,449},{64,128},{65,1},{128,192},{129,65},{192,256},{193,1... | collective-permute-start | bytes 393224 | tf_op jit(solution)/shard_map/ppermute | solution.py:306
  41.0 1.9 %collective-permute-start.7 = (bf16[4,128,128]{2,1,0:T(8,128)(2,1)S(1)}, bf16[4,128,128]{2,1,0:T(8,128)(2,1)S(1)}, u32[]{:S(2)}, u32[]{:S(2)}) collective-permute-start(bf16[4,128,128]{2,1,0:T(8,128)(2,1)S(1)} %slice.8), channel_id=1, source_target_pairs={{0,448},{1,65},{64,0},{65,129},{128,64},{129,193},{192,128},{193,2... | collective-permute-start | bytes 393224 | tf_op jit(solution)/shard_map/ppermute | solution.py:306
  43.0 1.4 early.1
  44.4 4.7 %collective-permute-done.7.b4 = bf16[4,128,128]{2,1,0:T(8,128)(2,1)S(1)} collective-permute-done((bf16[4,128,128]{2,1,0:T(8,128)(2,1)S(1)}, bf16[4,128,128]{2,1,0:T(8,128)(2,1)S(1)}, u32[]{:S(2)}, u32[]{:S(2)}) %collective-permute-start.7) | collective-permute-done | bytes 131104 | tf_op jit(solution)/shard_map/ppermute | solution.py:306
  49.1 2.0 %forward.1 = (f32[32,40,128]{2,1,0:T(8,128)S(1)}, bf16[32,40,128]{2,1,0:T(8,128)(2,1)S(1)}, f32[4,128,256]{2,1,0:T(8,128)S(1)}) custom-call(s32[5]{0:T(128)S(1)} %stack.15.place_ref, bf16[4,128,128]{2,1,0:T(8,128)(2,1)S(1)} %collective-permute-done.3.f4, bf16[4,128,128]{2,1,0:T(8,128)(2,1)S(1)} %collective-permute-done.7.b4, ...), custom_call_target="tpu_custom_call" | custom-call | tf_op jit(solution)/shard_map/forward/pallas_call | solution.py:315
  51.2 2.1 %collective-permute-start.8 = (bf16[32,40,128]{2,1,0:T(8,128)(2,1)S(1)}, bf16[32,40,128]{2,1,0:T(8,128)(2,1)S(1)}, u32[]{:S(2)}, u32[]{:S(2)}) collective-permute-start(bf16[32,40,128]{2,1,0:T(8,128)(2,1)S(1)} %get-tuple-element.30), channel_id=1, source_target_pairs={{0,1},{1,0},{2,3},{3,2},{4,5},{5,4},{6,7},{7,6},{8,9},{9,8},{10,11... | collective-permute-start | bytes 983048 | tf_op jit(solution)/shard_map/ppermute | solution.py:296
  53.2 1.6 %collective-permute-done.8.come_ref = bf16[32,40,128]{2,1,0:T(8,128)(2,1)S(1)} collective-permute-done((bf16[32,40,128]{2,1,0:T(8,128)(2,1)S(1)}, bf16[32,40,128]{2,1,0:T(8,128)(2,1)S(1)}, u32[]{:S(2)}, u32[]{:S(2)}) %collective-permute-start.8) | collective-permute-done | bytes 327712 | tf_op jit(solution)/shard_map/ppermute | solution.py:296
  54.9 27.5 %all_to_all.15.pieces_ref = bf16[32,40,128]{2,1,0:T(8,128)(2,1)S(1)} all-to-all(bf16[32,40,128]{2,1,0:T(8,128)(2,1)S(1)} %merge.1), channel_id=1, replica_groups=mesh['grp'=8,'inner_0'=8,'inner_1'=4,'inner_2'=2] {'inner_0','inner_1'}, dimensions={0} | all-to-all | bytes 655360 | tf_op jit(solution)/shard_map/all_to_all | solution.py:417
  82.5 22.1 %all_to_all.16.mine_ref = bf16[32,72,128]{2,1,0:T(8,128)(2,1)S(1)} all-to-all(bf16[32,72,128]{2,1,0:T(8,128)(2,1)S(1)} %get-tuple-element.31), channel_id=1, replica_groups=mesh['grp'=8,'inner_0'=8,'inner_1'=4,'inner_2'=2] {'inner_0','inner_1'}, dimensions={0} | all-to-all | bytes 1179648 | tf_op jit(solution)/shard_map/all_to_all | solution.py:420
  104.6 1.9 %collective-permute-start.9 = (bf16[32,72,128]{2,1,0:T(8,128)(2,1)S(1)}, bf16[32,72,128]{2,1,0:T(8,128)(2,1)S(1)}, u32[]{:S(2)}, u32[]{:S(2)}) collective-permute-start(bf16[32,72,128]{2,1,0:T(8,128)(2,1)S(1)} %all_to_all.16.mine_ref), channel_id=1, source_target_pairs={{0,1},{1,0},{2,3},{3,2},{4,5},{5,4},{6,7},{7,6},{8,9},{9,8},{10,11... | collective-permute-start | bytes 1769480 | tf_op jit(solution)/shard_map/ppermute | solution.py:296
  106.5 2.0 %collective-permute-done.9.other_ref = bf16[32,72,128]{2,1,0:T(8,128)(2,1)S(1)} collective-permute-done((bf16[32,72,128]{2,1,0:T(8,128)(2,1)S(1)}, bf16[32,72,128]{2,1,0:T(8,128)(2,1)S(1)}, u32[]{:S(2)}, u32[]{:S(2)}) %collective-permute-start.9) | collective-permute-done | bytes 589856 | tf_op jit(solution)/shard_map/ppermute | solution.py:296
  108.5 8.1 %backward.1 = (f32[16,256]{1,0:T(8,128)}, f32[32,16,256]{2,1,0:T(8,128)S(1)}, bf16[32,16,256]{2,1,0:T(8,128)(2,1)S(1)}, f32[16,256]{1,0:T(8,128)S(1)}) custom-call(s32[5]{0:T(128)S(1)} %stack.15.place_ref, bf16[32,72,128]{2,1,0:T(8,128)(2,1)S(1)} %all_to_all.16.mine_ref, bf16[32,72,128]{2,1,0:T(8,128)(2,1)S(1)} %collective-permute-done.9.other_ref, ...), custom_call_target="tpu_custom_call" | custom-call | tf_op jit(solution)/shard_map/backward/pallas_call | solution.py:315
  116.6 2.0 %collective-permute-start.10 = (bf16[32,16,256]{2,1,0:T(8,128)(2,1)S(1)}, bf16[32,16,256]{2,1,0:T(8,128)(2,1)S(1)}, u32[]{:S(2)}, u32[]{:S(2)}) collective-permute-start(bf16[32,16,256]{2,1,0:T(8,128)(2,1)S(1)} %get-tuple-element.36), channel_id=1, source_target_pairs={{0,1},{1,0},{2,3},{3,2},{4,5},{5,4},{6,7},{7,6},{8,9},{9,8},{10,11... | collective-permute-start | bytes 786440 | tf_op jit(solution)/shard_map/ppermute | solution.py:296
  118.7 1.4 %collective-permute-done.10.come_ref = bf16[32,16,256]{2,1,0:T(8,128)(2,1)S(1)} collective-permute-done((bf16[32,16,256]{2,1,0:T(8,128)(2,1)S(1)}, bf16[32,16,256]{2,1,0:T(8,128)(2,1)S(1)}, u32[]{:S(2)}, u32[]{:S(2)}) %collective-permute-start.10) | collective-permute-done | bytes 262176 | tf_op jit(solution)/shard_map/ppermute | solution.py:296
  120.1 17.9 %all_to_all.17.pieces_ref = bf16[32,16,256]{2,1,0:T(8,128)(2,1)S(1)} all-to-all(bf16[32,16,256]{2,1,0:T(8,128)(2,1)S(1)} %add.9), channel_id=1, replica_groups=mesh['grp'=8,'inner_0'=8,'inner_1'=4,'inner_2'=2] {'inner_0','inner_1'}, dimensions={0} | all-to-all | bytes 524288 | tf_op jit(solution)/shard_map/all_to_all | solution.py:445
  (22 shorter events, 4.4 us)
Async XLA Ops:
  1.6 10.4 %collective-permute-start = (bf16[8,128,128]{2,1,0:T(8,128)(2,1)S(1)}, bf16[8,128,128]{2,1,0:T(8,128)(2,1)S(1)}, u32[]{:S(2)}, u32[]{:S(2)}) collective-permute-start(bf16[8,128,128]{2,1,0:T(8,128)(2,1)S(1)} %join.1.own), channel_id=1, source_target_pairs={{0,64},{1,449},{64,128},{65,1},{128,192},{129,65},{192,256},{193,1... | collective-permute-start | bytes 786440 | tf_op jit(solution)/shard_map/ppermute | solution.py:306
  6.3 11.3 %collective-permute-start.4 = (bf16[8,128,128]{2,1,0:T(8,128)(2,1)S(1)}, bf16[8,128,128]{2,1,0:T(8,128)(2,1)S(1)}, u32[]{:S(2)}, u32[]{:S(2)}) collective-permute-start(bf16[8,128,128]{2,1,0:T(8,128)(2,1)S(1)} %join.1.own), channel_id=1, source_target_pairs={{0,448},{1,65},{64,0},{65,129},{128,64},{129,193},{192,128},{193,2... | collective-permute-start | bytes 786440 | tf_op jit(solution)/shard_map/ppermute | solution.py:306
  12.0 12.1 %collective-permute-start.1 = (bf16[8,128,128]{2,1,0:T(8,128)(2,1)S(1)}, bf16[8,128,128]{2,1,0:T(8,128)(2,1)S(1)}, u32[]{:S(2)}, u32[]{:S(2)}) collective-permute-start(bf16[8,128,128]{2,1,0:T(8,128)(2,1)S(1)} %collective-permute-done.f1), channel_id=1, source_target_pairs={{0,64},{1,449},{64,128},{65,1},{128,192},{129,65},{192,256},{193,1... | collective-permute-start | bytes 786440 | tf_op jit(solution)/shard_map/ppermute | solution.py:306
  17.7 12.1 %collective-permute-start.5 = (bf16[8,128,128]{2,1,0:T(8,128)(2,1)S(1)}, bf16[8,128,128]{2,1,0:T(8,128)(2,1)S(1)}, u32[]{:S(2)}, u32[]{:S(2)}) collective-permute-start(bf16[8,128,128]{2,1,0:T(8,128)(2,1)S(1)} %collective-permute-done.4.b1), channel_id=1, source_target_pairs={{0,448},{1,65},{64,0},{65,129},{128,64},{129,193},{192,128},{193,2... | collective-permute-start | bytes 786440 | tf_op jit(solution)/shard_map/ppermute | solution.py:306
  23.0 19.9 %copy-start.1 = (bf16[4,1024,256]{2,1,0:T(8,128)(2,1)S(1)}, bf16[4,1024,256]{2,1,0:T(8,128)(2,1)}, u32[]{:S(2)}) copy-start(bf16[4,1024,256]{2,1,0:T(8,128)(2,1)} %right_ref.3) | copy-start | bytes 6291460
  24.1 11.2 %collective-permute-start.2 = (bf16[8,128,128]{2,1,0:T(8,128)(2,1)S(1)}, bf16[8,128,128]{2,1,0:T(8,128)(2,1)S(1)}, u32[]{:S(2)}, u32[]{:S(2)}) collective-permute-start(bf16[8,128,128]{2,1,0:T(8,128)(2,1)S(1)} %collective-permute-done.1.f2), channel_id=1, source_target_pairs={{0,64},{1,449},{64,128},{65,1},{128,192},{129,65},{192,256},{193,1... | collective-permute-start | bytes 786440 | tf_op jit(solution)/shard_map/ppermute | solution.py:306
  29.7 11.3 %collective-permute-start.6 = (bf16[8,128,128]{2,1,0:T(8,128)(2,1)S(1)}, bf16[8,128,128]{2,1,0:T(8,128)(2,1)S(1)}, u32[]{:S(2)}, u32[]{:S(2)}) collective-permute-start(bf16[8,128,128]{2,1,0:T(8,128)(2,1)S(1)} %collective-permute-done.5.b2), channel_id=1, source_target_pairs={{0,448},{1,65},{64,0},{65,129},{128,64},{129,193},{192,128},{193,2... | collective-permute-start | bytes 786440 | tf_op jit(solution)/shard_map/ppermute | solution.py:306
  35.4 13.7 %copy-start.2 = (bf16[16,256]{1,0:T(8,128)(2,1)S(1)}, bf16[16,256]{1,0:T(8,128)(2,1)}, u32[]{:S(2)}) copy-start(bf16[16,256]{1,0:T(8,128)(2,1)} %tright_ref.3) | copy-start | bytes 24580
  35.4 9.0 %collective-permute-start.3 = (bf16[4,128,128]{2,1,0:T(8,128)(2,1)S(1)}, bf16[4,128,128]{2,1,0:T(8,128)(2,1)S(1)}, u32[]{:S(2)}, u32[]{:S(2)}) collective-permute-start(bf16[4,128,128]{2,1,0:T(8,128)(2,1)S(1)} %slice.6), channel_id=1, source_target_pairs={{0,64},{1,449},{64,128},{65,1},{128,192},{129,65},{192,256},{193,1... | collective-permute-start | bytes 393224 | tf_op jit(solution)/shard_map/ppermute | solution.py:306
  41.0 8.1 %collective-permute-start.7 = (bf16[4,128,128]{2,1,0:T(8,128)(2,1)S(1)}, bf16[4,128,128]{2,1,0:T(8,128)(2,1)S(1)}, u32[]{:S(2)}, u32[]{:S(2)}) collective-permute-start(bf16[4,128,128]{2,1,0:T(8,128)(2,1)S(1)} %slice.8), channel_id=1, source_target_pairs={{0,448},{1,65},{64,0},{65,129},{128,64},{129,193},{192,128},{193,2... | collective-permute-start | bytes 393224 | tf_op jit(solution)/shard_map/ppermute | solution.py:306
  49.1 33.3 %copy-start.3 = (bf16[16,256]{1,0:T(8,128)(2,1)S(1)}, bf16[16,256]{1,0:T(8,128)(2,1)}, u32[]{:S(2)}) copy-start(bf16[16,256]{1,0:T(8,128)(2,1)} %tleft_ref.3) | copy-start | bytes 24580
  51.1 57.4 %copy-start = (bf16[4,1024,256]{2,1,0:T(8,128)(2,1)S(1)}, bf16[4,1024,256]{2,1,0:T(8,128)(2,1)}, u32[]{:S(2)}) copy-start(bf16[4,1024,256]{2,1,0:T(8,128)(2,1)} %left_ref.1) | copy-start | bytes 6291460
  51.2 3.7 %collective-permute-start.8 = (bf16[32,40,128]{2,1,0:T(8,128)(2,1)S(1)}, bf16[32,40,128]{2,1,0:T(8,128)(2,1)S(1)}, u32[]{:S(2)}, u32[]{:S(2)}) collective-permute-start(bf16[32,40,128]{2,1,0:T(8,128)(2,1)S(1)} %get-tuple-element.30), channel_id=1, source_target_pairs={{0,1},{1,0},{2,3},{3,2},{4,5},{5,4},{6,7},{7,6},{8,9},{9,8},{10,11... | collective-permute-start | bytes 983048 | tf_op jit(solution)/shard_map/ppermute | solution.py:296
  104.6 3.9 %collective-permute-start.9 = (bf16[32,72,128]{2,1,0:T(8,128)(2,1)S(1)}, bf16[32,72,128]{2,1,0:T(8,128)(2,1)S(1)}, u32[]{:S(2)}, u32[]{:S(2)}) collective-permute-start(bf16[32,72,128]{2,1,0:T(8,128)(2,1)S(1)} %all_to_all.16.mine_ref), channel_id=1, source_target_pairs={{0,1},{1,0},{2,3},{3,2},{4,5},{5,4},{6,7},{7,6},{8,9},{9,8},{10,11... | collective-permute-start | bytes 1769480 | tf_op jit(solution)/shard_map/ppermute | solution.py:296
  116.6 3.4 %collective-permute-start.10 = (bf16[32,16,256]{2,1,0:T(8,128)(2,1)S(1)}, bf16[32,16,256]{2,1,0:T(8,128)(2,1)S(1)}, u32[]{:S(2)}, u32[]{:S(2)}) collective-permute-start(bf16[32,16,256]{2,1,0:T(8,128)(2,1)S(1)} %get-tuple-element.36), channel_id=1, source_target_pairs={{0,1},{1,0},{2,3},{3,2},{4,5},{5,4},{6,7},{7,6},{8,9},{9,8},{10,11... | collective-permute-start | bytes 786440 | tf_op jit(solution)/shard_map/ppermute | solution.py:296

commit v9 on v7

--- a/solution.py
+++ b/solution.py
@@ -119,7 +119,10 @@
             out_ref[k, t] = dot(left_ref[k, :, cols], sketch_ref[:, cols], 0, 0)
 
 
-def early_body(place_ref, own, f1, b1, f2, b2, f3, b3, right_ref, pair_ref, pivot_ref, factor):
+def early_body(
+    place_ref, own, f1, b1, f2, b2, f3, b3, sketch_ref, right_ref, tright_ref,
+    pair_ref, pivot_ref, core_keep, core_send, factor,
+):
     group, groups = place_ref[0], place_ref[2]
     slots, n = right_ref.shape[0], own.shape[1]
 
@@ -141,6 +144,13 @@
     put(None, groups // 2)
     for k in range(slots):
         pair_ref[k] = dot(factor[:, 128 * k : 128 * k + 128], right_ref[k], 0, 0)
+    core = place_ref[3]
+    cores = [
+        dot(tright_ref[:, 128 * t : 128 * t + 128], sketch_ref[:, 128 * t : 128 * t + 128], 0, 0)
+        for t in range(2)
+    ]
+    core_keep[...] = packed(jnp.where(core == 0, cores[0], cores[1]))
+    core_send[...] = packed(jnp.where(core == 0, cores[1], cores[0]))
 
 
 def upper_lines(shape):
@@ -169,7 +179,7 @@
 
 
 def forward_body(
-    place_ref, f4, b4, early_ref, pivot_ref, probe_low, probe_high, sketch_ref, right_ref, tright_ref,
+    place_ref, f4, b4, early_ref, pivot_ref, probe_low, probe_high, core_keep, core_send, right_ref,
     keep_ref, send_ref, pair_ref, part,
 ):
     group, live, groups, core = place_ref[0], place_ref[1], place_ref[2], place_ref[3]
@@ -190,17 +200,13 @@
     part[...] = dot(pivot_ref[...], mixed, 1, 0)
     last = jnp.concatenate([b4[k] for k in range(slots)], 1)
     part[pl.ds(at, n), :] = dot(last, mixed, 1, 0)
-    cores = [
-        dot(tright_ref[:, 128 * t : 128 * t + 128], sketch_ref[:, 128 * t : 128 * t + 128], 0, 0)
-        for t in range(2)
-    ]
     for t in range(2):
         whole = part[:, 128 * t : 128 * t + 128].reshape(half, 2, 16, 128)
         lines = slice(16 * t, 16 * t + 16)
         keep_ref[:, lines] = jnp.where(core == 0, whole[:, 0], whole[:, 1])
         send_ref[:, lines] = jnp.where(core == 0, whole[:, 1], whole[:, 0]).astype(LOW)
-    keep_ref[:, 32:] = packed(jnp.where(core == 0, cores[0], cores[1]))
-    send_ref[:, 32:] = packed(jnp.where(core == 0, cores[1], cores[0])).astype(LOW)
+    keep_ref[:, 32:] = core_keep[...]
+    send_ref[:, 32:] = core_send[...].astype(LOW)
 
 
 def add_body(keep_ref, come_ref, out_ref):
@@ -307,7 +313,7 @@
         in_specs=[SMEM] * len(first) + [VMEM] * (len(arrays) + len(given)),
         out_specs=[VMEM] * len(outs),
         out_shape=[
-            (jax.ShapeDtypeStruct if o[0] == leave else pltpu.VMEM)(*o) for o in outs
+            (jax.ShapeDtypeStruct if i == leave else pltpu.VMEM)(*o) for i, o in enumerate(outs)
         ],
         scratch_shapes=[pltpu.VMEM(*o) for o in scratch],
         name=name,
@@ -362,23 +368,24 @@
     chunks, probes, up, down = [own], [], own, own
     for step in range(3):
         up, down = shift(up, "grp", 1), shift(down, "grp", -1)
-        if step != 1:
+        if step:
             half_slots = slots // 2
             probe, own_sketch = probed(
-                place, col_left, sketch_cols, block, step // 2 * half_slots, half_slots
+                place, col_left, sketch_cols, block, (step - 1) * half_slots, half_slots
             )
             up, probe = lax.optimization_barrier((up, probe))
             probes.append(probe)
         chunks += [up, down]
     last_up, last_down = shift(up[:slots], "grp", 1), shift(down[slots:], "grp", -1)
-    early, pivot = kernel(
+    early, pivot, core_keep, core_send = kernel(
         early_body,
         "early",
-        [((slots, 128, width), FULL), ((rows, factors), LOW)],
+        [((slots, 128, width), FULL), ((rows, factors), LOW)] + [((half, 8, 128), FULL)] * 2,
         [((rows, factors), LOW)],
         place,
         *chunks,
-        given=(col_right,),
+        own_sketch,
+        given=(col_right, target_right),
     )
     piece = (half, block, width)
     keep, send, pair = kernel(
@@ -392,8 +399,9 @@
         early,
         pivot,
         *probes,
-        own_sketch,
-        given=(col_right, target_right),
+        core_keep,
+        core_send,
+        given=(col_right,),
     )
     (merged,) = kernel(
         merge_body, "merge", [((half, 40, 128), LOW)], [], None, keep, shift(send, INNER[2], 1)
@@ -422,6 +430,7 @@
         pivot,
         pair,
         given=(target_left, target_right, col_left),
+        leave=0,
     )
     (merged,) = kernel(add_body, "add", [(piece, LOW)], [], None, keep, shift(send, INNER[2], 1))
     merged = near(merged)
@@ -433,7 +442,7 @@
         None,
         lax.all_to_all(merged, far, 0, 0, tiled=True),
         direct,
-        leave=(block, width),
+        leave=0,
     )
     return basis, coeffs
 

time: 136 us -> 136 us (level)
  the two profiles are of different devices: /device:TPU:56 before, /device:TPU:24 now
where the time goes in v9:
time: 136 us
  blocking collectives  67.4 us (50%)
  starting transfers between devices  34.5 us (25%)
  Pallas kernels  18.6 us (14%)
  waiting for transfers between devices  13.2 us (10%)
  between operations  1.53 us (1%)
    all_to_all x2, blocking collectives, shards(): lax.all_to_all(merged, far, 0, 0, tiled=True)  45.3 us
    ppermute x11, starting transfers between devices, shift(): return lax.ppermute(x, axis, [(i, (i + by) % n) for i in range(n)])  34.5 us
    all_to_all x1, blocking collectives, shards(): mine = lax.all_to_all(mine, far, 0, 0, tiled=True)  22.1 us
    ppermute x11, waiting for transfers between devices, shift(): return lax.ppermute(x, axis, [(i, (i + by) % n) for i in range(n)])  13.2 us
    pallas_call x7, Pallas kernels, kernel(): pl.pallas_call(body, in_specs=[SMEM] * len(first) + [VMEM] * (len(arrays)...  12.5 us
    pallas_call x2, Pallas kernels, probed(): pl.pallas_call(functools.partial(probe_body, first=first), in_specs=[SMEM...  5.15 us
  transfers between devices with their start and end apart: 11, of which 5 were waited for; matrix products, arithmetic and copies ran while one was open for 0% of the time, Pallas kernels for 5%

profile of v9, /device:TPU:24, one launch (start us, length us, event | category | flops | bytes accessed | tf_op | source)
XLA Modules:
  0.0 135.5 jit_solution(15031720825899802996)
XLA Ops:
  1.6 4.7 %collective-permute-start = (bf16[8,128,128]{2,1,0:T(8,128)(2,1)S(1)}, bf16[8,128,128]{2,1,0:T(8,128)(2,1)S(1)}, u32[]{:S(2)}, u32[]{:S(2)}) collective-permute-start(bf16[8,128,128]{2,1,0:T(8,128)(2,1)S(1)} %join.1.own), channel_id=1, source_target_pairs={{0,64},{64,128},{128,192},{192,256},{256,320},{320,384},{384,448},... | collective-permute-start | bytes 786440 | tf_op jit(solution)/shard_map/ppermute | solution.py:302
  6.3 1.9 %collective-permute-start.4 = (bf16[8,128,128]{2,1,0:T(8,128)(2,1)S(1)}, bf16[8,128,128]{2,1,0:T(8,128)(2,1)S(1)}, u32[]{:S(2)}, u32[]{:S(2)}) collective-permute-start(bf16[8,128,128]{2,1,0:T(8,128)(2,1)S(1)} %join.1.own), channel_id=1, source_target_pairs={{0,448},{64,0},{128,64},{192,128},{256,192},{320,256},{384,320},{4... | collective-permute-start | bytes 786440 | tf_op jit(solution)/shard_map/ppermute | solution.py:302
  8.3 3.6 %collective-permute-done.f1 = bf16[8,128,128]{2,1,0:T(8,128)(2,1)S(1)} collective-permute-done((bf16[8,128,128]{2,1,0:T(8,128)(2,1)S(1)}, bf16[8,128,128]{2,1,0:T(8,128)(2,1)S(1)}, u32[]{:S(2)}, u32[]{:S(2)}) %collective-permute-start) | collective-permute-done | bytes 262176 | tf_op jit(solution)/shard_map/ppermute | solution.py:302
  11.9 5.6 %collective-permute-start.1 = (bf16[8,128,128]{2,1,0:T(8,128)(2,1)S(1)}, bf16[8,128,128]{2,1,0:T(8,128)(2,1)S(1)}, u32[]{:S(2)}, u32[]{:S(2)}) collective-permute-start(bf16[8,128,128]{2,1,0:T(8,128)(2,1)S(1)} %collective-permute-done.f1), channel_id=1, source_target_pairs={{0,64},{64,128},{128,192},{192,256},{256,320},{320,384},{384,448},... | collective-permute-start | bytes 786440 | tf_op jit(solution)/shard_map/ppermute | solution.py:302
  17.5 1.9 %collective-permute-start.5 = (bf16[8,128,128]{2,1,0:T(8,128)(2,1)S(1)}, bf16[8,128,128]{2,1,0:T(8,128)(2,1)S(1)}, u32[]{:S(2)}, u32[]{:S(2)}) collective-permute-start(bf16[8,128,128]{2,1,0:T(8,128)(2,1)S(1)} %collective-permute-done.4.b1), channel_id=1, source_target_pairs={{0,448},{64,0},{128,64},{192,128},{256,192},{320,256},{384,320},{4... | collective-permute-start | bytes 786440 | tf_op jit(solution)/shard_map/ppermute | solution.py:302
  20.1 2.7 %probe.2 = (f32[2,2,128,128]{3,2,1,0:T(8,128)S(1)}, bf16[16,256]{1,0:T(8,128)(2,1)}) custom-call(s32[5]{0:T(128)S(1)} %stack.15.place_ref, bf16[4,1024,256]{2,1,0:T(8,128)(2,1)} %left_ref.1, bf16[1024,256]{1,0:T(8,128)(2,1)} %sketch_any.3), custom_call_target="tpu_custom_call" | custom-call | tf_op jit(solution)/shard_map/probe/pallas_call | solution.py:325
  22.9 5.3 %collective-permute-start.2 = (bf16[8,128,128]{2,1,0:T(8,128)(2,1)S(1)}, bf16[8,128,128]{2,1,0:T(8,128)(2,1)S(1)}, u32[]{:S(2)}, u32[]{:S(2)}) collective-permute-start(bf16[8,128,128]{2,1,0:T(8,128)(2,1)S(1)} %collective-permute-done.1.f2), channel_id=1, source_target_pairs={{0,64},{64,128},{128,192},{192,256},{256,320},{320,384},{384,448},... | collective-permute-start | bytes 786440 | tf_op jit(solution)/shard_map/ppermute | solution.py:302
  28.2 1.9 %collective-permute-start.6 = (bf16[8,128,128]{2,1,0:T(8,128)(2,1)S(1)}, bf16[8,128,128]{2,1,0:T(8,128)(2,1)S(1)}, u32[]{:S(2)}, u32[]{:S(2)}) collective-permute-start(bf16[8,128,128]{2,1,0:T(8,128)(2,1)S(1)} %collective-permute-done.5.b2), channel_id=1, source_target_pairs={{0,448},{64,0},{128,64},{192,128},{256,192},{320,256},{384,320},{4... | collective-permute-start | bytes 786440 | tf_op jit(solution)/shard_map/ppermute | solution.py:302
  30.1 2.4 %probe.3 = (f32[2,2,128,128]{3,2,1,0:T(8,128)S(1)}, bf16[16,256]{1,0:T(8,128)(2,1)S(1)}) custom-call(s32[5]{0:T(128)S(1)} %stack.15.place_ref, bf16[4,1024,256]{2,1,0:T(8,128)(2,1)} %left_ref.1, bf16[1024,256]{1,0:T(8,128)(2,1)} %sketch_any.3), custom_call_target="tpu_custom_call" | custom-call | tf_op jit(solution)/shard_map/probe/pallas_call | solution.py:325
  32.6 5.3 %collective-permute-start.3 = (bf16[4,128,128]{2,1,0:T(8,128)(2,1)S(1)}, bf16[4,128,128]{2,1,0:T(8,128)(2,1)S(1)}, u32[]{:S(2)}, u32[]{:S(2)}) collective-permute-start(bf16[4,128,128]{2,1,0:T(8,128)(2,1)S(1)} %slice.6), channel_id=1, source_target_pairs={{0,64},{64,128},{128,192},{192,256},{256,320},{320,384},{384,448},... | collective-permute-start | bytes 393224 | tf_op jit(solution)/shard_map/ppermute | solution.py:302
  37.9 1.9 %collective-permute-start.7 = (bf16[4,128,128]{2,1,0:T(8,128)(2,1)S(1)}, bf16[4,128,128]{2,1,0:T(8,128)(2,1)S(1)}, u32[]{:S(2)}, u32[]{:S(2)}) collective-permute-start(bf16[4,128,128]{2,1,0:T(8,128)(2,1)S(1)} %slice.8), channel_id=1, source_target_pairs={{0,448},{64,0},{128,64},{192,128},{256,192},{320,256},{384,320},{4... | collective-permute-start | bytes 393224 | tf_op jit(solution)/shard_map/ppermute | solution.py:302
  39.9 1.4 %early.1 = (f32[4,128,256]{2,1,0:T(8,128)S(1)}, bf16[1024,512]{1,0:T(8,128)(2,1)S(1)}, f32[32,8,128]{2,1,0:T(8,128)S(1)}, f32[32,8,128]{2,1,0:T(8,128)S(1)}) custom-call(s32[5]{0:T(128)S(1)} %stack.15.place_ref, bf16[8,128,128]{2,1,0:T(8,128)(2,1)S(1)} %join.1.own, bf16[8,128,128]{2,1,0:T(8,128)(2,1)S(1)} %collective-permute-done.f1, ...), custom_call_target="tpu_custom_call" | custom-call | tf_op jit(solution)/shard_map/early/pallas_call | solution.py:311
  41.3 4.7 %collective-permute-done.7.b4 = bf16[4,128,128]{2,1,0:T(8,128)(2,1)S(1)} collective-permute-done((bf16[4,128,128]{2,1,0:T(8,128)(2,1)S(1)}, bf16[4,128,128]{2,1,0:T(8,128)(2,1)S(1)}, u32[]{:S(2)}, u32[]{:S(2)}) %collective-permute-start.7) | collective-permute-done | bytes 131104 | tf_op jit(solution)/shard_map/ppermute | solution.py:302
  46.0 2.0 %forward.1 = (f32[32,40,128]{2,1,0:T(8,128)S(1)}, bf16[32,40,128]{2,1,0:T(8,128)(2,1)S(1)}, f32[4,128,256]{2,1,0:T(8,128)S(1)}) custom-call(s32[5]{0:T(128)S(1)} %stack.15.place_ref, bf16[4,128,128]{2,1,0:T(8,128)(2,1)S(1)} %collective-permute-done.3.f4, bf16[4,128,128]{2,1,0:T(8,128)(2,1)S(1)} %collective-permute-done.7.b4, ...), custom_call_target="tpu_custom_call" | custom-call | tf_op jit(solution)/shard_map/forward/pallas_call | solution.py:311
  48.1 2.1 %collective-permute-start.8 = (bf16[32,40,128]{2,1,0:T(8,128)(2,1)S(1)}, bf16[32,40,128]{2,1,0:T(8,128)(2,1)S(1)}, u32[]{:S(2)}, u32[]{:S(2)}) collective-permute-start(bf16[32,40,128]{2,1,0:T(8,128)(2,1)S(1)} %get-tuple-element.34), channel_id=1, source_target_pairs={{0,1},{1,0},{2,3},{3,2},{4,5},{5,4},{6,7},{7,6},{8,9},{9,8},{10,11... | collective-permute-start | bytes 983048 | tf_op jit(solution)/shard_map/ppermute | solution.py:302
  50.1 1.6 %collective-permute-done.8.come_ref = bf16[32,40,128]{2,1,0:T(8,128)(2,1)S(1)} collective-permute-done((bf16[32,40,128]{2,1,0:T(8,128)(2,1)S(1)}, bf16[32,40,128]{2,1,0:T(8,128)(2,1)S(1)}, u32[]{:S(2)}, u32[]{:S(2)}) %collective-permute-start.8) | collective-permute-done | bytes 327712 | tf_op jit(solution)/shard_map/ppermute | solution.py:302
  51.8 27.5 %all_to_all.15.pieces_ref = bf16[32,40,128]{2,1,0:T(8,128)(2,1)S(1)} all-to-all(bf16[32,40,128]{2,1,0:T(8,128)(2,1)S(1)} %merge.1), channel_id=1, replica_groups=mesh['grp'=8,'inner_0'=8,'inner_1'=4,'inner_2'=2] {'inner_0','inner_1'}, dimensions={0} | all-to-all | bytes 655360 | tf_op jit(solution)/shard_map/all_to_all | solution.py:415
  79.4 22.1 %all_to_all.16.mine_ref = bf16[32,72,128]{2,1,0:T(8,128)(2,1)S(1)} all-to-all(bf16[32,72,128]{2,1,0:T(8,128)(2,1)S(1)} %get-tuple-element.35), channel_id=1, replica_groups=mesh['grp'=8,'inner_0'=8,'inner_1'=4,'inner_2'=2] {'inner_0','inner_1'}, dimensions={0} | all-to-all | bytes 1179648 | tf_op jit(solution)/shard_map/all_to_all | solution.py:418
  101.5 1.9 %collective-permute-start.9 = (bf16[32,72,128]{2,1,0:T(8,128)(2,1)S(1)}, bf16[32,72,128]{2,1,0:T(8,128)(2,1)S(1)}, u32[]{:S(2)}, u32[]{:S(2)}) collective-permute-start(bf16[32,72,128]{2,1,0:T(8,128)(2,1)S(1)} %all_to_all.16.mine_ref), channel_id=1, source_target_pairs={{0,1},{1,0},{2,3},{3,2},{4,5},{5,4},{6,7},{7,6},{8,9},{9,8},{10,11... | collective-permute-start | bytes 1769480 | tf_op jit(solution)/shard_map/ppermute | solution.py:302
  103.4 2.0 %collective-permute-done.9.other_ref = bf16[32,72,128]{2,1,0:T(8,128)(2,1)S(1)} collective-permute-done((bf16[32,72,128]{2,1,0:T(8,128)(2,1)S(1)}, bf16[32,72,128]{2,1,0:T(8,128)(2,1)S(1)}, u32[]{:S(2)}, u32[]{:S(2)}) %collective-permute-start.9) | collective-permute-done | bytes 589856 | tf_op jit(solution)/shard_map/ppermute | solution.py:302
  105.4 8.1 %backward.1 = (f32[16,256]{1,0:T(8,128)}, f32[32,16,256]{2,1,0:T(8,128)S(1)}, bf16[32,16,256]{2,1,0:T(8,128)(2,1)S(1)}, f32[16,256]{1,0:T(8,128)S(1)}) custom-call(s32[5]{0:T(128)S(1)} %stack.15.place_ref, bf16[32,72,128]{2,1,0:T(8,128)(2,1)S(1)} %all_to_all.16.mine_ref, bf16[32,72,128]{2,1,0:T(8,128)(2,1)S(1)} %collective-permute-done.9.other_ref, ...), custom_call_target="tpu_custom_call" | custom-call | tf_op jit(solution)/shard_map/backward/pallas_call | solution.py:311
  113.5 2.0 %collective-permute-start.10 = (bf16[32,16,256]{2,1,0:T(8,128)(2,1)S(1)}, bf16[32,16,256]{2,1,0:T(8,128)(2,1)S(1)}, u32[]{:S(2)}, u32[]{:S(2)}) collective-permute-start(bf16[32,16,256]{2,1,0:T(8,128)(2,1)S(1)} %get-tuple-element.40), channel_id=1, source_target_pairs={{0,1},{1,0},{2,3},{3,2},{4,5},{5,4},{6,7},{7,6},{8,9},{9,8},{10,11... | collective-permute-start | bytes 786440 | tf_op jit(solution)/shard_map/ppermute | solution.py:302
  115.6 1.4 %collective-permute-done.10.come_ref = bf16[32,16,256]{2,1,0:T(8,128)(2,1)S(1)} collective-permute-done((bf16[32,16,256]{2,1,0:T(8,128)(2,1)S(1)}, bf16[32,16,256]{2,1,0:T(8,128)(2,1)S(1)}, u32[]{:S(2)}, u32[]{:S(2)}) %collective-permute-start.10) | collective-permute-done | bytes 262176 | tf_op jit(solution)/shard_map/ppermute | solution.py:302
  117.0 17.9 %all_to_all.17.pieces_ref = bf16[32,16,256]{2,1,0:T(8,128)(2,1)S(1)} all-to-all(bf16[32,16,256]{2,1,0:T(8,128)(2,1)S(1)} %add.9), channel_id=1, replica_groups=mesh['grp'=8,'inner_0'=8,'inner_1'=4,'inner_2'=2] {'inner_0','inner_1'}, dimensions={0} | all-to-all | bytes 524288 | tf_op jit(solution)/shard_map/all_to_all | solution.py:443
  (22 shorter events, 2.0 us)
Async XLA Ops:
  1.6 10.2 %collective-permute-start = (bf16[8,128,128]{2,1,0:T(8,128)(2,1)S(1)}, bf16[8,128,128]{2,1,0:T(8,128)(2,1)S(1)}, u32[]{:S(2)}, u32[]{:S(2)}) collective-permute-start(bf16[8,128,128]{2,1,0:T(8,128)(2,1)S(1)} %join.1.own), channel_id=1, source_target_pairs={{0,64},{64,128},{128,192},{192,256},{256,320},{320,384},{384,448},... | collective-permute-start | bytes 786440 | tf_op jit(solution)/shard_map/ppermute | solution.py:302
  6.3 11.1 %collective-permute-start.4 = (bf16[8,128,128]{2,1,0:T(8,128)(2,1)S(1)}, bf16[8,128,128]{2,1,0:T(8,128)(2,1)S(1)}, u32[]{:S(2)}, u32[]{:S(2)}) collective-permute-start(bf16[8,128,128]{2,1,0:T(8,128)(2,1)S(1)} %join.1.own), channel_id=1, source_target_pairs={{0,448},{64,0},{128,64},{192,128},{256,192},{320,256},{384,320},{4... | collective-permute-start | bytes 786440 | tf_op jit(solution)/shard_map/ppermute | solution.py:302
  11.9 11.0 %collective-permute-start.1 = (bf16[8,128,128]{2,1,0:T(8,128)(2,1)S(1)}, bf16[8,128,128]{2,1,0:T(8,128)(2,1)S(1)}, u32[]{:S(2)}, u32[]{:S(2)}) collective-permute-start(bf16[8,128,128]{2,1,0:T(8,128)(2,1)S(1)} %collective-permute-done.f1), channel_id=1, source_target_pairs={{0,64},{64,128},{128,192},{192,256},{256,320},{320,384},{384,448},... | collective-permute-start | bytes 786440 | tf_op jit(solution)/shard_map/ppermute | solution.py:302
  17.5 10.7 %collective-permute-start.5 = (bf16[8,128,128]{2,1,0:T(8,128)(2,1)S(1)}, bf16[8,128,128]{2,1,0:T(8,128)(2,1)S(1)}, u32[]{:S(2)}, u32[]{:S(2)}) collective-permute-start(bf16[8,128,128]{2,1,0:T(8,128)(2,1)S(1)} %collective-permute-done.4.b1), channel_id=1, source_target_pairs={{0,448},{64,0},{128,64},{192,128},{256,192},{320,256},{384,320},{4... | collective-permute-start | bytes 786440 | tf_op jit(solution)/shard_map/ppermute | solution.py:302
  22.9 17.0 %copy-start.1 = (bf16[4,1024,256]{2,1,0:T(8,128)(2,1)S(1)}, bf16[4,1024,256]{2,1,0:T(8,128)(2,1)}, u32[]{:S(2)}) copy-start(bf16[4,1024,256]{2,1,0:T(8,128)(2,1)} %right_ref.3) | copy-start | bytes 6291460
  22.9 17.0 %copy-start.2 = (bf16[16,256]{1,0:T(8,128)(2,1)S(1)}, bf16[16,256]{1,0:T(8,128)(2,1)}, u32[]{:S(2)}) copy-start(bf16[16,256]{1,0:T(8,128)(2,1)} %tright_ref.3) | copy-start | bytes 24580
  22.9 9.7 %collective-permute-start.2 = (bf16[8,128,128]{2,1,0:T(8,128)(2,1)S(1)}, bf16[8,128,128]{2,1,0:T(8,128)(2,1)S(1)}, u32[]{:S(2)}, u32[]{:S(2)}) collective-permute-start(bf16[8,128,128]{2,1,0:T(8,128)(2,1)S(1)} %collective-permute-done.1.f2), channel_id=1, source_target_pairs={{0,64},{64,128},{128,192},{192,256},{256,320},{320,384},{384,448},... | collective-permute-start | bytes 786440 | tf_op jit(solution)/shard_map/ppermute | solution.py:302
  28.2 9.7 %collective-permute-start.6 = (bf16[8,128,128]{2,1,0:T(8,128)(2,1)S(1)}, bf16[8,128,128]{2,1,0:T(8,128)(2,1)S(1)}, u32[]{:S(2)}, u32[]{:S(2)}) collective-permute-start(bf16[8,128,128]{2,1,0:T(8,128)(2,1)S(1)} %collective-permute-done.5.b2), channel_id=1, source_target_pairs={{0,448},{64,0},{128,64},{192,128},{256,192},{320,256},{384,320},{4... | collective-permute-start | bytes 786440 | tf_op jit(solution)/shard_map/ppermute | solution.py:302
  32.6 8.7 %collective-permute-start.3 = (bf16[4,128,128]{2,1,0:T(8,128)(2,1)S(1)}, bf16[4,128,128]{2,1,0:T(8,128)(2,1)S(1)}, u32[]{:S(2)}, u32[]{:S(2)}) collective-permute-start(bf16[4,128,128]{2,1,0:T(8,128)(2,1)S(1)} %slice.6), channel_id=1, source_target_pairs={{0,64},{64,128},{128,192},{192,256},{256,320},{320,384},{384,448},... | collective-permute-start | bytes 393224 | tf_op jit(solution)/shard_map/ppermute | solution.py:302
  37.9 8.1 %collective-permute-start.7 = (bf16[4,128,128]{2,1,0:T(8,128)(2,1)S(1)}, bf16[4,128,128]{2,1,0:T(8,128)(2,1)S(1)}, u32[]{:S(2)}, u32[]{:S(2)}) collective-permute-start(bf16[4,128,128]{2,1,0:T(8,128)(2,1)S(1)} %slice.8), channel_id=1, source_target_pairs={{0,448},{64,0},{128,64},{192,128},{256,192},{320,256},{384,320},{4... | collective-permute-start | bytes 393224 | tf_op jit(solution)/shard_map/ppermute | solution.py:302
  46.0 33.3 %copy-start.3 = (bf16[16,256]{1,0:T(8,128)(2,1)S(1)}, bf16[16,256]{1,0:T(8,128)(2,1)}, u32[]{:S(2)}) copy-start(bf16[16,256]{1,0:T(8,128)(2,1)} %tleft_ref.3) | copy-start | bytes 24580
  48.1 57.3 %copy-start = (bf16[4,1024,256]{2,1,0:T(8,128)(2,1)S(1)}, bf16[4,1024,256]{2,1,0:T(8,128)(2,1)}, u32[]{:S(2)}) copy-start(bf16[4,1024,256]{2,1,0:T(8,128)(2,1)} %left_ref.1) | copy-start | bytes 6291460
  48.1 3.7 %collective-permute-start.8 = (bf16[32,40,128]{2,1,0:T(8,128)(2,1)S(1)}, bf16[32,40,128]{2,1,0:T(8,128)(2,1)S(1)}, u32[]{:S(2)}, u32[]{:S(2)}) collective-permute-start(bf16[32,40,128]{2,1,0:T(8,128)(2,1)S(1)} %get-tuple-element.34), channel_id=1, source_target_pairs={{0,1},{1,0},{2,3},{3,2},{4,5},{5,4},{6,7},{7,6},{8,9},{9,8},{10,11... | collective-permute-start | bytes 983048 | tf_op jit(solution)/shard_map/ppermute | solution.py:302
  101.5 3.9 %collective-permute-start.9 = (bf16[32,72,128]{2,1,0:T(8,128)(2,1)S(1)}, bf16[32,72,128]{2,1,0:T(8,128)(2,1)S(1)}, u32[]{:S(2)}, u32[]{:S(2)}) collective-permute-start(bf16[32,72,128]{2,1,0:T(8,128)(2,1)S(1)} %all_to_all.16.mine_ref), channel_id=1, source_target_pairs={{0,1},{1,0},{2,3},{3,2},{4,5},{5,4},{6,7},{7,6},{8,9},{9,8},{10,11... | collective-permute-start | bytes 1769480 | tf_op jit(solution)/shard_map/ppermute | solution.py:302
  113.5 3.4 %collective-permute-start.10 = (bf16[32,16,256]{2,1,0:T(8,128)(2,1)S(1)}, bf16[32,16,256]{2,1,0:T(8,128)(2,1)S(1)}, u32[]{:S(2)}, u32[]{:S(2)}) collective-permute-start(bf16[32,16,256]{2,1,0:T(8,128)(2,1)S(1)} %get-tuple-element.40), channel_id=1, source_target_pairs={{0,1},{1,0},{2,3},{3,2},{4,5},{5,4},{6,7},{7,6},{8,9},{9,8},{10,11... | collective-permute-start | bytes 786440 | tf_op jit(solution)/shard_map/ppermute | solution.py:302
